TPU v7x, 512 devices: a whole 4x8x8 slice. The times are simulated.
512 devices in a mesh: box: 128 (over z, y, core), col: 4 (over x).
Axes of the slice: x: 4, y: 8, z: 8, core: 2. Of those that a mesh axis runs over, the one named last changes fastest.
Arguments:
- basis: float32 [4, 2, 64, 65536], P(None, None, 'col', 'box'), may hold values from -1000 to 1000
- offsets: float32 [3, 65536], P(None, 'box'), may hold values from -0.5 to 0.5
- weights: float32 [65536], P('box'), may hold values from 0.03 to 0.3
- interp: float32 [512, 32, 128], P('box'), may hold values from 0 to 1
- skeleton: int32 [512, 32], P('box'), may hold values from 0 to 127, as said below
- near_boxes: int32 [512, 27], P('box'), may hold values from 0 to 511, as said below
- near_count: int32 [512], P('box'), may hold values from 3 to 27, as said below
Outputs:
- new_block: float32 [2, 64, 65536], P(None, 'col', 'box')
- coupling: float32 [4, 64, 64], replicated
- factor: float32 [64, 64], replicated
Inputs may be any that keep to these rules, and one draw needn't show every extreme that they name: `skeleton`: each row holds 32 different points of the box. `near_boxes`: entry 0 of box b's row is b itself, entry 1 is b + 4 and entry 2 is b - 4, both clipped to the boxes; every entry lies within 4 boxes of b. Box b's near field is the first near_count[b] entries of its row of near_boxes.
All inputs are finite; a program needn't handle non-finite values.
Results may differ from a plain program's by a relative error of at most 0.0003.
Values sent between devices are 32-bit elements; how exact they have to be, the bound alone decides.
No kernel may reach another device: no remote copies, remote signals or barrier semaphores. Data moves between devices by JAX's collectives and lax.ppermute only.
A program may use at most 64 MiB of HBM per device.

v0:
```python
import math

import jax
import jax.numpy as jnp
from jax import lax
from jax.sharding import PartitionSpec as P

BOX_DEV = 4


WAVENUMBER = 6.0
SMOOTHING = 0.1
SHIFT_SCALE = 0.02
EPSILON = 1e-06
HIGHEST = lax.Precision.HIGHEST
SOURCE_BLOCK = 2048


def extended_2(cells, sides, width):
    for axis, dim in sides:
        count = lax.axis_size(axis)
        ends = count - 1
        head = lax.slice_in_dim(cells, 0, width, axis=dim)
        tail = lax.slice_in_dim(cells, cells.shape[dim] - width, cells.shape[dim], axis=dim)
        cells = jnp.concatenate(
            [
                lax.ppermute(tail, axis, [(i, (i + 1) % count) for i in range(ends)]),
                cells,
                lax.ppermute(head, axis, [((i + 1) % count, i) for i in range(ends)]),
            ],
            axis=dim,
        )
    return cells


def box_centers(box_index):
    along_band = (box_index // BOX_DEV).astype(jnp.float32)
    across = (box_index % BOX_DEV).astype(jnp.float32)
    return jnp.stack([along_band, across, jnp.zeros_like(along_band)])


def helmholtz_pair(targets, sources):
    spread = SMOOTHING * SMOOTHING
    for axis_index in range(3):
        spread = (
            spread + (targets[axis_index][..., :, None] - sources[axis_index][..., None, :]) ** 2
        )
    distance = jnp.sqrt(spread)
    factor = 1.0 / (4.0 * math.pi * distance)
    return (jnp.cos(WAVENUMBER * distance) * factor, jnp.sin(WAVENUMBER * distance) * factor)


def far_block(skel_count, target_pos, target_weight, running, shard_piece, first_row):
    value_rows = shard_piece.shape[0] - 3
    source_count = shard_piece.shape[1]
    source_boxes = source_count // skel_count
    target_count = target_pos.shape[1]
    box_weight = lax.dynamic_slice_in_dim(target_weight, first_row // skel_count, source_boxes, 1)
    kernel_re, kernel_im = helmholtz_pair(target_pos, shard_piece[value_rows:])
    kernel_re = (
        kernel_re.reshape(target_count, source_boxes, skel_count) * box_weight[:, :, None]
    ).reshape(target_count, source_count)
    kernel_im = (
        kernel_im.reshape(target_count, source_boxes, skel_count) * box_weight[:, :, None]
    ).reshape(target_count, source_count)
    stacked = jnp.stack([kernel_re, kernel_im])
    charge_rows = shard_piece[:value_rows].reshape(2, value_rows // 2, source_count)
    product = jnp.einsum("gts,pcs->gpct", stacked, charge_rows, precision=HIGHEST)
    return running + jnp.stack([product[0, 0] - product[1, 1], product[1, 0] + product[0, 1]])


def far_fold(skel_count, target_pos, target_weight, running, shard_piece):
    source_count = shard_piece.shape[1]

    def one_block(block_index, carry):
        offset = block_index * SOURCE_BLOCK
        block_piece = lax.dynamic_slice_in_dim(shard_piece, offset, SOURCE_BLOCK, 1)
        return far_block(skel_count, target_pos, target_weight, carry, block_piece, offset)

    return lax.fori_loop(0, source_count // SOURCE_BLOCK, one_block, running)


def shards(basis, offsets, weights, interp, skeleton, near_boxes, near_count):
    box_count = near_count.shape[0]
    points = interp.shape[2]
    skel_count = interp.shape[1]
    slot_count = near_boxes.shape[1]
    prior_blocks = basis.shape[0]
    columns = basis.shape[2]
    total_boxes = box_count * lax.axis_size("box")
    first_box = lax.axis_index("box") * box_count
    own_boxes = first_box + jnp.arange(box_count, dtype=jnp.int32)
    positions = offsets.reshape(3, box_count, points) + box_centers(own_boxes)[:, :, None]
    current = basis[prior_blocks - 1]
    sources = (current * weights).reshape(2, columns, box_count, points)
    payload = jnp.concatenate([sources.reshape(2 * columns, box_count, points), positions], axis=0)
    extended = extended_2(payload, (("box", 1),), box_count)

    def near_slot(slot_index, running):
        listed = lax.dynamic_index_in_dim(near_boxes, slot_index, 1, keepdims=False)
        live_slot = (slot_index < near_count).astype(jnp.float32)
        picked = jnp.take(extended, listed - first_box + box_count, axis=1)
        source_pos = picked[2 * columns :]
        source_val = (picked[: 2 * columns] * live_slot[None, :, None]).reshape(
            2, columns, box_count, points
        )
        kernel_re, kernel_im = helmholtz_pair(positions, source_pos)
        stacked = jnp.stack([kernel_re, kernel_im])
        product = jnp.einsum("gbtq,pcbq->gpcbt", stacked, source_val, precision=HIGHEST)
        return running + jnp.stack([product[0, 0] - product[1, 1], product[1, 0] + product[0, 1]])

    near_init = jnp.zeros((2, columns, box_count, points), jnp.float32)
    near_field = lax.fori_loop(0, slot_count, near_slot, near_init)
    charges = jnp.einsum("bkq,pcbq->pcbk", interp, sources, precision=HIGHEST).reshape(
        2, columns, box_count * skel_count
    )
    skel_pos = jnp.take_along_axis(
        positions, jnp.broadcast_to(skeleton[None], (3, box_count, skel_count)), axis=2
    ).reshape(3, box_count * skel_count)
    slot_live = jnp.arange(slot_count, dtype=jnp.int32)[None, :] < near_count[:, None]
    every_box = jnp.arange(total_boxes, dtype=jnp.int32)
    box_listed = jnp.any(
        (near_boxes[:, :, None] == every_box[None, None, :]) & slot_live[:, :, None], axis=1
    )
    target_weight = jnp.repeat(1.0 - box_listed.astype(jnp.float32), skel_count, axis=0)
    payload_far = jnp.concatenate(
        [charges.reshape(2 * columns, box_count * skel_count), skel_pos], axis=0
    )
    zero_phi = jnp.zeros((2, columns, box_count * skel_count), jnp.float32)
    potentials = far_fold(
        skel_count,
        skel_pos,
        target_weight,
        zero_phi,
        lax.all_gather(payload_far, "box", axis=1, tiled=True),
    )
    potentials = potentials.reshape(2, columns, box_count, skel_count)
    far_field = jnp.einsum("bkq,pcbk->pcbq", interp, potentials, precision=HIGHEST)
    applied = 0.5 * current + (near_field + far_field).reshape(2, columns, box_count * points)
    rows_basis, rows_applied = (
        lax.all_to_all(basis, "col", split_axis=3, concat_axis=2, tiled=True),
        lax.all_to_all(applied[None], "col", split_axis=3, concat_axis=2, tiled=True),
    )
    rows_applied = rows_applied[0]
    all_columns = rows_applied.shape[1]
    row_total = rows_applied.shape[2] * lax.axis_size("box") * lax.axis_size("col")
    part_coupling = (
        jnp.einsum("kpiq,pjq->kij", rows_basis, rows_applied, precision=HIGHEST) / row_total
    )
    coupling = lax.psum(part_coupling, ("box", "col"))
    residual = rows_applied - jnp.einsum("kpiq,kij->pjq", rows_basis, coupling, precision=HIGHEST)
    part_gram = jnp.einsum("piq,pjq->ij", residual, residual, precision=HIGHEST) / row_total
    gram_matrix = lax.psum(part_gram, ("box", "col"))
    identity = jnp.eye(all_columns, dtype=jnp.float32)
    shift_term = SHIFT_SCALE * jnp.trace(gram_matrix) / all_columns + EPSILON
    lower_factor = jnp.linalg.cholesky(gram_matrix + shift_term * identity)
    inverse = jax.scipy.linalg.solve_triangular(lower_factor, identity, lower=True)
    normalized = jnp.einsum("ij,pjq->piq", inverse, residual, precision=HIGHEST)
    new_block = lax.all_to_all(normalized, "col", split_axis=1, concat_axis=2, tiled=True)
    return (new_block, coupling, lower_factor.T)


def solution(mesh):
    return jax.shard_map(
        shards,
        mesh=mesh,
        in_specs=(
            P(None, None, "col", "box"),
            P(None, "box"),
            P("box"),
            P("box", None, None),
            P("box", None),
            P("box", None),
            P("box"),
        ),
        out_specs=(P(None, "col", "box"), P(), P()),
        check_vma=False,
    )
```

profile of v0, /device:TPU:1, one launch (start us, length us, event | category | flops | bytes accessed | tf_op | source)
XLA Modules:
  0.0 589.7 jit_solution(7123391067058255241)
XLA Ops:
  9.8 4.6 collective-permute-start
  14.4 5.5 collective-permute-start.1
  22.9 3.8 gather_fusion.1
  28.9 2.3 reshape.851
  31.2 3.4 all-to-all-start.1
  35.1 71.1 %while.32 = (s32[]{:T(128)}, f32[2,16,4,128]{3,1,2,0:T(8,128)S(1)}, s32[4,27]{0,1:T(8,128)S(1)}, s32[]{:T(128)}, f32[35,12,128]{2,0,1:T(8,128)S(1)}, /*index=5*/...) while((s32[]{:T(128)}, f32[2,16,4,128]{3,1,2,0:T(8,128)S(1)}, ...), condition=%wide.region_1.2_spmd.clone, body=%wide.region_0.1_spmd.clone.sunk | while | flops 51481128 | bytes 2097387 | solution.py:113
  43.7 1.2 cosine_multiply_fusion.2
  49.0 1.2 cosine_multiply_fusion.2
  51.6 1.2 cosine_multiply_fusion.2
  54.3 1.2 cosine_multiply_fusion.2
  62.2 1.2 cosine_multiply_fusion.2
  83.2 1.2 cosine_multiply_fusion.2
  85.9 1.2 cosine_multiply_fusion.2
  88.5 1.2 cosine_multiply_fusion.2
  93.8 1.2 cosine_multiply_fusion.2
  99.0 1.2 cosine_multiply_fusion.2
  101.7 1.2 cosine_multiply_fusion.2
  104.3 1.2 cosine_multiply_fusion.2
  106.2 6.0 %all-gather.2.cloned.1.call-done = f32[35,16384]{1,0:T(8,128)} async-done(((f32[35,128]{1,0:T(8,128)}), f32[35,16384]{1,0:T(8,128)}) %all-gather.2.cloned.1.call-update) | async-done | bytes 2293776 | tf_op jit(solution)/shard_map/all_gather | solution.py:135
  112.3 73.7 %while.33 = (s32[]{:T(128)}, f32[2,16,128]{2,1,0:T(8,128)S(1)}, f32[35,16384]{1,0:T(8,128)}, f32[3,128]{1,0:T(4,128)S(1)}, f32[128,512]{0,1:T(8,128)S(1)}, /*ind...) while((s32[]{:T(128)}, f32[2,16,128]{2,1,0:T(8,128)S(1)}, ...), condition=%wide.region_4.5_spmd.clone, body=%wide.region_3.4_spmd.clone.sunk | while | flops 206061600 | bytes 9483192 | solution.py:80
  113.8 4.7 multiply_multiply_fusion.3
  119.5 1.9 fusion.58
  123.0 4.7 multiply_multiply_fusion.3
  128.7 1.9 fusion.58
  132.2 4.7 multiply_multiply_fusion.3
  137.9 1.9 fusion.58
  141.5 4.7 multiply_multiply_fusion.3
  147.1 1.9 fusion.58
  150.7 4.7 multiply_multiply_fusion.3
  156.4 1.9 fusion.58
  159.9 4.7 multiply_multiply_fusion.3
  165.6 1.9 fusion.58
  169.1 4.7 multiply_multiply_fusion.3
  174.8 1.9 fusion.58
  178.3 4.7 multiply_multiply_fusion.3
  184.0 1.9 fusion.58
  186.7 1.4 reshape.849
  188.0 3.9 all-to-all-start
  192.5 1.4 reduce.7
  193.8 1.5 reshape.852
  200.3 263.3 %all-reduce.2.cloned.1.call-done = f32[4,64,64]{1,2,0:T(8,128)} async-done(((f32[4,64,64]{1,2,0:T(8,128)}), f32[4,64,64]{1,2,0:T(8,128)}) %all-reduce.2.cloned.1.call-update) | async-done | bytes 65552 | tf_op jit(solution)/shard_map/psum | solution.py:150
  463.7 1.2 fusion.17
  465.1 94.8 %psum.15 = f32[64,64]{1,0:T(8,128)S(1)} all-reduce(f32[64,64]{1,0:T(8,128)S(1)} %fusion.18), channel_id=1, replica_groups=mesh['box'=128,'col'=4] {'box','col'}, use_global_device_ids=true, to_apply=%region_6.7 | all-reduce | flops 4096 | bytes 32768 | tf_op jit(solution)/shard_map/psum | solution.py:153
  561.2 5.8 cholesky.18
  568.4 4.9 custom-call.7
  574.4 3.3 all-to-all-start.2
  578.4 1.7 copy.143
  580.1 2.1 all-to-all-done.2
  (489 shorter events, 93.2 us)
Async XLA Ops:
  7.2 19.6 %copy-start = (f32[4,32,128]{2,1,0:T(8,128)S(1)}, f32[4,32,128]{2,1,0:T(8,128)}, u32[]{:S(2)}) copy-start(f32[4,32,128]{2,1,0:T(8,128)} %param.14) | copy-start | bytes 196612
  7.2 105.1 %all-gather.2.cloned.1.call-start = ((), (), s32[]{:S(2)}) async-start(), calls=%async_computation.3 | async-start | bytes 2641920 | tf_op jit(solution)/shard_map/all_gather | solution.py:135
  9.8 25.3 %collective-permute-start = (f32[35,4,128]{2,0,1:T(8,128)S(1)}, f32[35,4,128]{2,0,1:T(8,128)S(1)}, u32[]{:S(2)}, u32[]{:S(2)}) collective-permute-start(f32[35,4,128]{2,0,1:T(8,128)S(1)} %pad_maximum_fusion.1), channel_id=1, source_target_pairs={{0,4},{4,8},{8,12},{12,16},{16,20},{20,24},{24,28},{28,32},{32,36}... | collective-permute-start | bytes 215048 | tf_op jit(solution)/shard_map/ppermute | solution.py:27
  14.4 20.7 %collective-permute-start.1 = (f32[35,4,128]{2,0,1:T(8,128)S(1)}, f32[35,4,128]{2,0,1:T(8,128)S(1)}, u32[]{:S(2)}, u32[]{:S(2)}) collective-permute-start(f32[35,4,128]{2,0,1:T(8,128)S(1)} %pad_maximum_fusion.1), channel_id=1, source_target_pairs={{4,0},{8,4},{12,8},{16,12},{20,16},{24,20},{28,24},{32,28},{36,32}... | collective-permute-start | bytes 215048 | tf_op jit(solution)/shard_map/ppermute | solution.py:29
  22.9 3.9 copy-start.2
  22.9 4.9 copy-start.1
  27.8 6.8 %copy-start.3 = (s32[4,27]{1,0:T(4,128)S(1)}, s32[4,27]{1,0:T(4,128)}, u32[]{:S(2)}) copy-start(s32[4,27]{1,0:T(4,128)} %param.16) | copy-start | bytes 1300
  27.8 6.9 %copy-start.4 = (s32[4]{0:T(128)S(1)}, s32[4]{0:T(128)}, u32[]{:S(2)}) copy-start(s32[4]{0:T(128)} %param.17) | copy-start | bytes 52
  31.2 156.8 %all-to-all-start.1 = ((f32[4,1,16384]{2,1,0:T(1,128)}), f32[4,1,16384]{2,1,0:T(1,128)S(1)}, u32[]{:S(2)}, u32[]{:S(2)}) async-start(f32[4,1,16384]{2,1,0:T(1,128)} %reshape.851), calls=%async_computation.1 | async-start | bytes 524288 | tf_op jit(solution)/shard_map/all_to_all | solution.py:141
  188.0 8.4 %all-to-all-start = ((f32[4,1,4096]{2,1,0:T(1,128)}), f32[4,1,4096]{2,1,0:T(1,128)S(1)}, u32[]{:S(2)}, u32[]{:S(2)}) async-start(f32[4,1,4096]{2,1,0:T(1,128)} %reshape.849), calls=%async_computation | async-start | bytes 131072 | tf_op jit(solution)/shard_map/all_to_all | solution.py:142
  192.0 271.7 %all-reduce.2.cloned.1.call-start = ((), (), s32[]{:S(2)}) async-start(), calls=%async_computation.4 | async-start | bytes 262144 | tf_op jit(solution)/shard_map/psum | solution.py:150
  574.4 7.7 %all-to-all-start.2 = ((f32[2,64,128]{2,0,1:T(2,128)}), f32[2,64,128]{2,0,1:T(2,128)S(1)}, u32[]{:S(2)}, u32[]{:S(2)}) async-start(f32[2,64,128]{2,0,1:T(2,128)} %copy.141), calls=%async_computation.2 | async-start | bytes 131072 | tf_op jit(solution)/shard_map/all_to_all | solution.py:159
Sparse Core Ops, SparseCore 0:
  27.9 84.2 all-gather.1
  199.5 264.1 all-reduce.1
where the time goes:
time: 591 us; the launch traced here: 590 us
  waiting for transfers between devices  272 us (46%)
  blocking collectives  94.8 us (16%)
  other arithmetic  93.7 us (16%)
  local copies, waits for them, and re-layouts  55.6 us (9%)
  matrix products  34.8 us (6%)
  starting transfers between devices  20.7 us (4%)
  between operations  15.1 us (3%)
    psum x1, waiting for transfers between devices, shards(): coupling = lax.psum(part_coupling, ('box', 'col'))  263 us
    psum x1, blocking collectives, shards(): gram_matrix = lax.psum(part_gram, ('box', 'col'))  94.8 us
    mul x8, other arithmetic, far_block(): kernel_re.reshape(target_count, source_boxes, skel_count)  37.5 us
    mul x27, other arithmetic, helmholtz_pair(): jnp.cos(WAVENUMBER * distance) * factor  31.7 us
    dot_general x27, matrix products, near_slot(): jnp.einsum('gbtq,pcbq->gpcbt', stacked, source_val, precision=HIGHEST)  15.9 us
    dot_general x8, matrix products, far_block(): jnp.einsum('gts,pcs->gpct', stacked, charge_rows, precision=HIGHEST)  15.4 us
    gather x27, local copies, waits for them, and re-layouts, near_slot(): picked = jnp.take(extended, listed - first_box + box_count, axis=1)  15 us
  transfers between devices with their start and end apart: 7, of which 4 were waited for; matrix products, arithmetic and copies ran while one was open for 28% of the time, Pallas kernels for 0%

commit v1 on v0

v1 whole, which is shorter than its diff:
```python
import functools
import math

import jax
import jax.numpy as jnp
from jax import lax
from jax.experimental import pallas as pl
from jax.experimental.pallas import tpu as pltpu
from jax.sharding import Mesh
from jax.sharding import PartitionSpec as P

BOX_DEV = 4
PTS = 128
SKEL = 32
SLOTS = 27
REACH = 4
WAVENUMBER = 6.0
SMOOTHING = 0.1
SHIFT_SCALE = 0.02
EPSILON = 1e-06
HIGHEST = lax.Precision.HIGHEST
F32 = jnp.float32
BF16 = jnp.bfloat16
INTERPRET = False

GRID = (8, 8, 2)
BOX = ("z", "y", "k")
YK = ("y", "k")
ZX = ("z", "x")

TURNS = WAVENUMBER / (2.0 * math.pi)
SIN_C = (3.1415926401307073, -5.167710083507923, 2.5500775232148563, -0.5982912856211671, 0.07765766030589402)
COS_C = (
    0.9999999997799043,
    -4.934802137078822,
    4.0587091595560825,
    -1.335212003047854,
    0.2349373138047365,
    -0.02439632433202294,
)


def poly(coefs, u):
    r = coefs[-1] * u + coefs[-2]
    for c in coefs[-3::-1]:
        r = r * u + c
    return r


def helmholtz(tx, ty, tz, sx, sy, sz, weight):
    dx = tx - sx
    dy = ty - sy
    dz = tz - sz
    s = SMOOTHING * SMOOTHING + dx * dx + dy * dy + dz * dz
    r = lax.rsqrt(s)
    r = r * (1.5 - (0.5 * s) * (r * r))
    t = (s * r) * TURNS
    f = t - lax.round(t, lax.RoundingMethod.TO_NEAREST_EVEN)
    u = f * f
    sn = f * poly(SIN_C, u)
    cs = poly(COS_C, u)
    two = sn + sn
    w = r * weight
    return (1.0 - two * sn) * w, (two * cs) * w


def split(x):
    hi = x.astype(BF16)
    return hi, (x - hi.astype(F32)).astype(BF16)


def dot(a, b, ca, cb, precision=None):
    return lax.dot_general(
        a, b, (((ca,), (cb,)), ((), ())), precision=precision, preferred_element_type=F32
    )


def rotate(rows):
    parts = []
    for g in range(rows.shape[0] // 32):
        parts.append(-rows[32 * g + 16 : 32 * g + 32])
        parts.append(rows[32 * g : 32 * g + 16])
    return jnp.concatenate(parts, axis=0)


def group_index(dims):
    return (lax.axis_index("z") * dims[1] + lax.axis_index("y")) * dims[2] + lax.axis_index("k")


def call(kernel, out_shape, in_specs, scratch=(), flops=0, name=None):
    vmem = pl.BlockSpec(memory_space=pltpu.VMEM)
    single = not isinstance(out_shape, (tuple, list))
    return pl.pallas_call(
        kernel,
        out_shape=out_shape,
        in_specs=in_specs,
        out_specs=vmem if single else [vmem] * len(out_shape),
        scratch_shapes=list(scratch),
        cost_estimate=pl.CostEstimate(flops=flops, bytes_accessed=1 << 19, transcendentals=0),
        interpret=INTERPRET,
        name=name,
    )


VMEM = pl.BlockSpec(memory_space=pltpu.VMEM)
SMEM = pl.BlockSpec(memory_space=pltpu.SMEM)


def prep_kernel(idx, near, count, cur, weights, offsets, interp, skel, halo, far, info):
    i = idx[0].astype(F32)
    x = idx[1]
    src = cur[...] * weights[...]
    halo[0:32, :] = src
    centre = lax.broadcasted_iota(jnp.int32, (8, 1), 0)
    charges = []
    spots = []
    for b in range(BOX_DEV):
        cols = slice(PTS * b, PTS * b + PTS)
        shift = jnp.where(centre == 0, i, jnp.where(centre == 1, float(b), 0.0))
        pos = jnp.concatenate([offsets[:, cols], jnp.zeros((5, PTS), F32)], axis=0) + shift
        halo[32:40, cols] = pos
        charges.append(dot(src[:, cols], interp[b], 1, 1, HIGHEST))
        q = lax.broadcasted_iota(jnp.int32, (PTS, SKEL), 0)
        pick = (q == skel[b : b + 1, :]).astype(F32)
        spots.append(dot(pos, pick, 1, 0, HIGHEST))
    far[0:32, :] = jnp.concatenate(charges, axis=1)
    far[32:40, :] = jnp.concatenate(spots, axis=1)
    row = lax.broadcasted_iota(jnp.int32, (8, PTS), 0)
    lane = lax.broadcasted_iota(jnp.int32, (8, PTS), 1)
    box_of = BOX_DEV * (idx[0] + row - 1) + lane // SKEL
    listed = jnp.zeros((8, PTS), F32)
    for s in range(SLOTS):
        box = jnp.where(s < count[x], near[x, s], -1000)
        listed = jnp.where(box_of == box, 1.0, listed)
    spot = spots[0]
    for b in range(1, BOX_DEV):
        spot = jnp.where(x == b, spots[b], spot)
    info[...] = jnp.concatenate(
        [
            jnp.concatenate([spot[0:3], jnp.zeros((3, PTS - SKEL), F32)], axis=1),
            1.0 - listed[0:3],
            jnp.zeros((2, PTS), F32),
        ],
        axis=0,
    )


def near_kernel(idx, near, count, prev, own, nxt, cur, out, ext, mult, tpos, acc):
    for e in range(BOX_DEV):
        cols = slice(PTS * e, PTS * e + PTS)
        ext[e] = prev[:, cols]
        ext[BOX_DEV + e] = own[:, cols]
        ext[2 * BOX_DEV + e] = nxt[:, cols]
    stack = jnp.concatenate(
        [own[32:40, PTS * t : PTS * t + PTS] for t in range(BOX_DEV)]
        + [jnp.zeros((PTS - 8 * BOX_DEV, PTS), F32)],
        axis=0,
    )
    turned = stack.T
    base = BOX_DEV * (idx[0] - 1)
    erow = lax.broadcasted_iota(jnp.int32, (16, PTS), 0)
    for t in range(BOX_DEV):
        for c in range(3):
            tpos[t, c] = jnp.broadcast_to(turned[:, 8 * t + c : 8 * t + c + 1], (PTS, PTS))
        m = jnp.zeros((16, PTS), F32)
        for s in range(SLOTS):
            box = jnp.where(s < count[t], near[t, s] - base, -1000)
            m = m + jnp.where(erow == box, 1.0, 0.0)
        mult[t] = m
    acc[...] = jnp.zeros_like(acc)

    def step(d, carry):
        for t in range(BOX_DEV):
            e = t + d
            rows = ext[e, 0:32, :]
            re, im = helmholtz(
                tpos[t, 0],
                tpos[t, 1],
                tpos[t, 2],
                ext[e, 32:33, :],
                ext[e, 33:34, :],
                ext[e, 34:35, :],
                0.25 / math.pi,
            )
            khi, klo = split(jnp.concatenate([re, im], axis=1))
            rhi, rlo = split(jnp.concatenate([rows, rotate(rows)], axis=1))
            both = dot(jnp.concatenate([rhi, rlo], axis=0), khi, 1, 1)
            part = both[0:32] + (both[32:64] + dot(rhi, klo, 1, 1))
            acc[t] += part * mult[t, pl.ds(e, 1), :]
        return carry

    lax.fori_loop(0, 2 * REACH + 1, step, 0)
    for t in range(BOX_DEV):
        out[t] = 0.5 * cur[:, PTS * t : PTS * t + PTS] + acc[t]


def far_kernel(dims, idx, info, gathered, out, tpos, rhi, rlo, weight, acc):
    nz, ny, nk, nx = dims
    targets = ny * nk
    stack = jnp.concatenate([info[d] for d in range(targets)], axis=0)
    if targets * 8 < PTS:
        stack = jnp.concatenate([stack, jnp.zeros((PTS - targets * 8, PTS), F32)], axis=0)
    turned = stack.T
    for d in range(targets):
        for c in range(3):
            tpos[c, SKEL * d : SKEL * d + SKEL, :] = jnp.broadcast_to(
                turned[0:SKEL, 8 * d + c : 8 * d + c + 1], (SKEL, PTS)
            )
    for g in range(nz):
        rows = jnp.concatenate([gathered[nx * g + c, 0:32, :] for c in range(nx)], axis=0)
        hi, lo = split(jnp.concatenate([rows, rotate(rows)], axis=1))
        rhi[g] = hi
        rlo[g] = lo
    acc[...] = jnp.zeros_like(acc)
    per = min(4, targets)

    def step(g, carry):
        sx = gathered[nx * g, 32:33, :]
        sy = gathered[nx * g, 33:34, :]
        sz = gathered[nx * g, 34:35, :]
        source_group = g * targets + idx[1]
        for d in range(targets):
            delta = source_group - (idx[0] + d)
            w = jnp.where(delta == -1, info[d, 3:4, :], 1.0)
            w = jnp.where(delta == 0, info[d, 4:5, :], w)
            w = jnp.where(delta == 1, info[d, 5:6, :], w)
            weight[SKEL * d : SKEL * d + SKEL, :] = jnp.broadcast_to(
                w * (0.25 / math.pi), (SKEL, PTS)
            )
        for n in range(targets // per):
            span = slice(SKEL * per * n, SKEL * per * (n + 1))
            re, im = helmholtz(
                tpos[0, span, :],
                tpos[1, span, :],
                tpos[2, span, :],
                sx,
                sy,
                sz,
                weight[span, :],
            )
            khi, klo = split(jnp.concatenate([re, im], axis=1))
            acc[span, :] += dot(khi, rhi[g], 1, 1) + (
                dot(khi, rlo[g], 1, 1) + dot(klo, rhi[g], 1, 1)
            )
        return carry

    lax.fori_loop(0, nz, step, 0)
    for d in range(targets):
        out[d] = acc[SKEL * d : SKEL * d + SKEL, :]


def halves(rows, nx):
    re = jnp.concatenate([rows[32 * c : 32 * c + 16] for c in range(nx)], axis=0)
    im = jnp.concatenate([rows[32 * c + 16 : 32 * c + 32] for c in range(nx)], axis=0)
    return jnp.concatenate([re, im], axis=1)


def couple_kernel(dims, scale, idx, phi, nearf, interp, basis, applied, stacked, part):
    nx = dims[3]
    total = phi[0]
    for d in range(1, phi.shape[0]):
        total = total + phi[d]
    rows = dot(total, interp[idx[2]], 0, 0, HIGHEST)
    rows = rows + jnp.concatenate([nearf[c] for c in range(nx)], axis=0)
    a2 = halves(rows, nx)
    applied[...] = a2
    blocks = []
    for k in range(4):
        b2 = halves(jnp.concatenate([basis[c, 32 * k : 32 * k + 32, :] for c in range(nx)], axis=0), nx)
        stacked[64 * k : 64 * k + 64, :] = b2
        blocks.append(dot(b2, a2, 1, 1, HIGHEST) * scale)
    left = jnp.concatenate(blocks[0:2], axis=0)
    right = jnp.concatenate(blocks[2:4], axis=0)
    packed = jnp.concatenate([left, right], axis=1)
    n = part.shape[0]
    for d in range(n):
        part[d] = packed[8 * d : 8 * d + 8, :]


def residual_kernel(scale, coup, applied, stacked, residual, part, coupling):
    n = coup.shape[0]
    packed = jnp.concatenate([coup[d] for d in range(n)], axis=0)
    c = jnp.concatenate([packed[:, 0:64], packed[:, 64:128]], axis=0)
    for k in range(4):
        coupling[k] = c[64 * k : 64 * k + 64]
    res = applied[...] - dot(c, stacked[...], 0, 0, HIGHEST)
    residual[...] = res
    gram = dot(res, res, 1, 1, HIGHEST) * scale
    both = jnp.concatenate([gram[0:32], gram[32:64]], axis=1)
    per = 32 // n
    for d in range(n):
        part[d] = jnp.concatenate(
            [both[per * d : per * d + per], jnp.zeros((8 - per, PTS), F32)], axis=0
        )


def finish_kernel(dims, idx, gram, residual, out, factor, inv):
    nx = dims[3]
    n = gram.shape[0]
    per = 32 // n
    both = jnp.concatenate([gram[d, 0:per, :] for d in range(n)], axis=0)
    g = jnp.concatenate([both[:, 0:64], both[:, 64:128]], axis=0)
    row = lax.broadcasted_iota(jnp.int32, (64, 64), 0)
    col = lax.broadcasted_iota(jnp.int32, (64, 64), 1)
    eye = row == col
    diag = jnp.where(eye, g, 0.0)
    trace = jnp.sum(jnp.sum(diag, axis=1, keepdims=True), axis=0, keepdims=True)
    g = g + jnp.where(eye, SHIFT_SCALE * trace / 64.0 + EPSILON, 0.0)
    m = jnp.concatenate([g, eye.astype(F32)], axis=1)
    sub = lax.broadcasted_iota(jnp.int32, (64, 1), 0)
    for j in range(63):
        line = m[j : j + 1, :]
        f = jnp.where(sub > j, m[:, j : j + 1] / line[:, j : j + 1], 0.0)
        m = m - f * line
    pivots = jnp.sum(jnp.where(eye, m[:, 0:64], 0.0), axis=1, keepdims=True)
    root = 1.0 / jnp.sqrt(pivots)
    m = m * root
    factor[...] = jnp.where(row <= col, m[:, 0:64], 0.0)
    inv[...] = m[:, 64:128]
    mine = inv[pl.ds(pl.multiple_of(16 * idx[2], 16), 16), :]
    for b in range(nx):
        rows = dot(mine, residual[b], 1, 0, HIGHEST)
        out[0, :, PTS * b : PTS * b + PTS] = rows[:, 0:PTS]
        out[1, :, PTS * b : PTS * b + PTS] = rows[:, PTS : 2 * PTS]


def share(value, axes, count):
    return lax.all_to_all(
        jnp.broadcast_to(value[None], (count,) + value.shape),
        axes,
        split_axis=0,
        concat_axis=0,
        tiled=True,
    )


def trade(value, axes):
    return lax.all_to_all(value, axes, split_axis=0, concat_axis=0, tiled=True)


def all_sum(part, dims):
    nz, ny, nk, nx = dims
    mine = jnp.sum(trade(part, YK), axis=0)
    mine = jnp.sum(share(mine, ZX, nz * nx), axis=0)
    return share(mine, YK, ny * nk)


def shards(dims, basis, offsets, weights, interp, skeleton, near_boxes, near_count):
    nz, ny, nk, nx = dims
    box_dims = dims[:3]
    groups = nz * ny * nk
    targets = ny * nk
    row_total = groups * BOX_DEV * PTS
    group = group_index(box_dims)
    col = lax.axis_index("x")
    idx_prep = jnp.stack([group, col]).astype(jnp.int32)
    idx_far = jnp.stack(
        [
            lax.axis_index("z") * targets,
            lax.axis_index("y") * nk + lax.axis_index("k"),
            col,
        ]
    ).astype(jnp.int32)
    cur = basis[3].reshape(32, BOX_DEV * PTS)
    shape = lambda *s: jax.ShapeDtypeStruct(s, F32)

    with jax.named_scope("prep"):
        halo, far, info = call(
            prep_kernel,
            (shape(40, BOX_DEV * PTS), shape(40, PTS), shape(8, PTS)),
            [SMEM, SMEM, SMEM] + [VMEM] * 5,
            name="prep",
        )(idx_prep, near_boxes, near_count, cur, weights[None], offsets, interp, skeleton)

    with jax.named_scope("info"):
        info_all = share(info, YK, targets)
    with jax.named_scope("gather"):
        far_all = share(far, ZX, nz * nx)
    with jax.named_scope("halo"):
        prev = lax.ppermute(halo, BOX, [(g, g + 1) for g in range(groups - 1)])
        nxt = lax.ppermute(halo, BOX, [(g + 1, g) for g in range(groups - 1)])
    with jax.named_scope("basis"):
        mixed = basis.reshape(4 * 32, BOX_DEV, PTS).transpose(1, 0, 2)
        basis_rows = trade(mixed, "x")

    with jax.named_scope("near"):
        near_part = call(
            near_kernel,
            shape(BOX_DEV, 32, PTS),
            [SMEM, SMEM, SMEM] + [VMEM] * 4,
            [
                pltpu.VMEM((3 * BOX_DEV, 40, PTS), F32),
                pltpu.VMEM((BOX_DEV, 16, PTS), F32),
                pltpu.VMEM((BOX_DEV, 3, PTS, PTS), F32),
                pltpu.VMEM((BOX_DEV, 32, PTS), F32),
            ],
            flops=36 * 2 * 64 * 256 * 128 * 2,
            name="near",
        )(idx_prep, near_boxes, near_count, prev, halo, nxt, cur)
        near_rows = trade(near_part, "x")

    with jax.named_scope("far"):
        far_part = call(
            functools.partial(far_kernel, dims),
            shape(targets, SKEL, 32 * nx),
            [SMEM, VMEM, VMEM],
            [
                pltpu.VMEM((3, SKEL * targets, PTS), F32),
                pltpu.VMEM((nz, 32 * nx, 2 * PTS), BF16),
                pltpu.VMEM((nz, 32 * nx, 2 * PTS), BF16),
                pltpu.VMEM((SKEL * targets, PTS), F32),
                pltpu.VMEM((SKEL * targets, 32 * nx), F32),
            ],
            flops=3 * 2 * 512 * 2048 * 128,
            name="far",
        )(idx_far, info_all, far_all)
        phi = trade(far_part, YK)

    with jax.named_scope("couple"):
        applied, stacked, part = call(
            functools.partial(couple_kernel, dims, 1.0 / row_total),
            (shape(64, 2 * PTS), shape(256, 2 * PTS), shape(16, 8, PTS)),
            [SMEM] + [VMEM] * 4,
            name="couple",
        )(idx_far, phi, near_rows, interp, basis_rows)
        if targets != 16:
            part = part.reshape(targets, 128 // targets, PTS)
        coup = all_sum(part, dims).reshape(16, 8, PTS)

    with jax.named_scope("residual"):
        residual, part, coupling = call(
            functools.partial(residual_kernel, 1.0 / row_total),
            (shape(64, 2 * PTS), shape(16, 8, PTS), shape(4, 64, 64)),
            [VMEM] * 3,
            name="residual",
        )(coup, applied, stacked)
        if targets != 16:
            part = part.reshape(targets, 128 // targets, PTS)
        residual_all = share(residual, "x", nx)
        gram = all_sum(part, dims).reshape(16, 8, PTS)

    with jax.named_scope("finish"):
        new_block, factor = call(
            functools.partial(finish_kernel, dims),
            (shape(2, 16, BOX_DEV * PTS), shape(64, 64)),
            [SMEM, VMEM, VMEM],
            [pltpu.VMEM((64, 64), F32)],
            name="finish",
        )(idx_far, gram, residual_all)
    return new_block, coupling, factor


def solution(mesh):
    boxes, cols = mesh.devices.shape
    nk = GRID[2]
    ny = GRID[1] if boxes == math.prod(GRID) else 2
    nz = boxes // (ny * nk)
    dims = (nz, ny, nk, cols)
    fine = Mesh(mesh.devices.reshape(dims), ("z", "y", "k", "x"))
    return jax.shard_map(
        functools.partial(shards, dims),
        mesh=fine,
        in_specs=(
            P(None, None, "x", BOX),
            P(None, BOX),
            P(BOX),
            P(BOX, None, None),
            P(BOX, None),
            P(BOX, None),
            P(BOX),
        ),
        out_specs=(P(None, "x", BOX), P(), P()),
        check_vma=False,
    )
```

time: 591 us -> 204 us (0.35)
  waiting for transfers between devices: 272 us -> 24.4 us
  other arithmetic: 93.7 us -> 1.38 us
  local copies, waits for them, and re-layouts: 55.6 us -> 5.91 us
  matrix products: 34.8 us -> 0 us
  Pallas kernels: 0 us -> 29.6 us
  between operations: 15.1 us -> 0.75 us
  starting transfers between devices: 20.7 us -> 33.5 us
  blocking collectives: 94.8 us -> 107 us
    psum x1 -> x0, waiting for transfers between devices: 263 us -> none  [shards(): coupling = lax.psum(part_coupling, ('box', 'col'))]
    all_to_all x0 -> x8, blocking collectives: none -> 107 us  [the longest x4 54.7 us: share(): lax.all_to_all(jnp.broadcast_to(value[None], (count,) + value.shape), axe...]
    psum x1 -> x0, blocking collectives: 94.8 us -> none  [shards(): gram_matrix = lax.psum(part_gram, ('box', 'col'))]
    mul x63 -> x0, other arithmetic: 71.9 us -> none  [the longest x8 37.5 us: far_block(): kernel_re.reshape(target_count, source_boxes, skel_count)]
    dot_general x41 -> x0, matrix products: 34.5 us -> none  [the longest x27 15.9 us: near_slot(): jnp.einsum('gbtq,pcbq->gpcbt', stacked, source_val, precision=HIGHEST)]
    pallas_call x0 -> x6, Pallas kernels: none -> 29.6 us  [the longest x1 7.72 us: shards(): call(near_kernel, shape(BOX_DEV, 32, PTS), [SMEM, SMEM, SMEM] + [VMEM] *...]
    gather x29 -> x0, local copies, waits for them, and re-layouts: 18.9 us -> none  [the longest x27 15 us: near_slot(): picked = jnp.take(extended, listed - first_box + box_count, axis=1)]
    all_to_all x3 -> x4, waiting for transfers between devices: 2.19 us -> 20.6 us  [the longest x3 20.6 us: share(): lax.all_to_all(jnp.broadcast_to(value[None], (count,) + value.shape), axe...]
  transfers between devices with their start and end apart: 7 -> 6, of which waited for: 4 -> 3; matrix products, arithmetic and copies ran while one was open for 28% -> 1% of each run, Pallas kernels for 0% -> 8%
where the time goes in v1:
time: 204 us; the launch traced here: 203 us
  blocking collectives  107 us (52%)
  starting transfers between devices  33.5 us (16%)
  Pallas kernels  29.6 us (15%)
  waiting for transfers between devices  24.4 us (12%)
  local copies, waits for them, and re-layouts  5.91 us (3%)
    all_to_all x4, blocking collectives, share(): lax.all_to_all(jnp.broadcast_to(value[None], (count,) + value.shape), axe...  54.7 us
    all_to_all x4, blocking collectives, trade(): return lax.all_to_all(value, axes, split_axis=0, concat_axis=0, tiled=True)  52.5 us
    all_to_all x3, starting transfers between devices, share(): lax.all_to_all(jnp.broadcast_to(value[None], (count,) + value.shape), axe...  23.6 us
    all_to_all x3, waiting for transfers between devices, share(): lax.all_to_all(jnp.broadcast_to(value[None], (count,) + value.shape), axe...  20.6 us
    pallas_call x1, Pallas kernels, shards(): call(near_kernel, shape(BOX_DEV, 32, PTS), [SMEM, SMEM, SMEM] + [VMEM] *...  7.72 us
    pallas_call x1, Pallas kernels, shards(): call(functools.partial(far_kernel, dims), shape(targets, SKEL, 32 * nx),...  7.62 us
    pallas_call x1, Pallas kernels, shards(): call(functools.partial(finish_kernel, dims), (shape(2, 16, BOX_DEV * PTS)...  7.41 us
    all_to_all x1, starting transfers between devices, trade(): return lax.all_to_all(value, axes, split_axis=0, concat_axis=0, tiled=True)  4.43 us
  transfers between devices with their start and end apart: 6, of which 3 were waited for; matrix products, arithmetic and copies ran while one was open for 1% of the time, Pallas kernels for 8%

profile of v1, /device:TPU:1, one launch (start us, length us, event | category | flops | bytes accessed | tf_op | source)
XLA Modules:
  0.0 202.7 jit_solution(9941653877803134431)
XLA Ops:
  0.6 1.5 slice.3
  2.1 0.6 pad_add_fusion.1.idx
  2.7 2.0 prep.1
  4.7 1.3 broadcast_in_dim.17
  6.0 0.0 copy-start.7
  6.0 10.2 %all-to-all-start = ((f32[16,8,128]{2,1,0:T(8,128)}), f32[16,8,128]{2,1,0:T(8,128)S(1)}, u32[]{:S(2)}, u32[]{:S(2)}) async-start(f32[16,8,128]{2,1,0:T(8,128)} %broadcast_in_dim.17), calls=%async_computation | async-start | bytes 131072 | tf_op jit(solution)/shard_map/info/all_to_all | solution.py:328
  16.3 0.0 copy-done.7
  16.3 3.5 %collective-permute-start = (f32[40,512]{1,0:T(8,128)S(1)}, f32[40,512]{1,0:T(8,128)S(1)}, u32[]{:S(2)}, u32[]{:S(2)}) collective-permute-start(f32[40,512]{1,0:T(8,128)S(1)} %copy-done.7), channel_id=1, source_target_pairs={{0,4},{4,8},{8,12},{12,16},{16,20},{20,24},{24,28},{28,32},{32,36}... | collective-permute-start | bytes 245768 | tf_op jit(solution)/shard_map/halo/ppermute | solution.py:380
  19.9 1.9 collective-permute-start.1
  21.8 0.0 collective-permute-done.prev
  21.8 0.0 copy-start.8
  21.8 3.8 %collective-permute-done.1.nxt = f32[40,512]{1,0:T(8,128)S(1)} collective-permute-done((f32[40,512]{1,0:T(8,128)S(1)}, f32[40,512]{1,0:T(8,128)S(1)}, u32[]{:S(2)}, u32[]{:S(2)}) %collective-permute-start.1) | collective-permute-done | bytes 81952 | tf_op jit(solution)/shard_map/halo/ppermute | solution.py:381
  25.6 0.0 copy-done.8
  25.6 0.6 copy-done.9
  26.2 7.7 %near.4 = f32[4,32,128]{2,1,0:T(8,128)} custom-call(s32[2]{0:T(128)} %pad_add_fusion.1.idx, s32[4,27]{1,0:T(4,128)} %near.5, s32[4]{0:T(128)} %count.3, f32[40,512]{1,0:T(8,128)} %copy-done.8, f32[40,512]{1,0:T(8,128)} %get-tuple-element.16.own, f32[40,512]{1,0:T(8,128)} %copy-done.9, f32[32,512]{1,0:T(8,128)} %bitcast.12), custom_call_target="tpu_custom_call" | custom-call | flops 301989888 | bytes 524288 | tf_op jit(solution)/shard_map/near/near/pallas_call | solution.py:387
  34.0 0.0 copy-start.6
  34.0 0.0 all-to-all-done.info
  34.0 8.4 %all_to_all.60.nearf = f32[4,32,128]{2,1,0:T(8,128)} all-to-all(f32[4,32,128]{2,1,0:T(8,128)} %near.4), channel_id=1, replica_groups=mesh['z'=8,'y'=8,'k'=2,'x'=4] {'x'}, dimensions={0} | all-to-all | bytes 131072 | tf_op jit(solution)/shard_map/near/all_to_all | solution.py:338
  42.4 0.0 copy-done.5
  42.4 0.0 copy-done.6
  42.4 0.9 broadcast_in_dim.18
  43.3 9.9 %all-to-all-start.1 = ((f32[32,40,128]{2,1,0:T(8,128)}), f32[32,40,128]{2,1,0:T(8,128)S(1)}, u32[]{:S(2)}, u32[]{:S(2)}) async-start(f32[32,40,128]{2,1,0:T(8,128)} %broadcast_in_dim.18), calls=%async_computation.1 | async-start | bytes 1310720 | tf_op jit(solution)/shard_map/gather/all_to_all | solution.py:328
  53.3 0.0 copy-done.3
  53.3 0.1 reshape.16
  53.4 0.7 copy.13
  54.1 15.1 %all-to-all-done.1.gathered = f32[32,40,128]{2,1,0:T(8,128)S(1)} async-done(((f32[32,40,128]{2,1,0:T(8,128)}), f32[32,40,128]{2,1,0:T(8,128)S(1)}, u32[]{:S(2)}, u32[]{:S(2)}) %all-to-all-start.1) | async-done | bytes 655392 | tf_op jit(solution)/shard_map/gather/all_to_all | solution.py:328
  69.2 4.4 %all-to-all-start.4 = ((f32[4,128,128]{2,1,0:T(8,128)}), f32[4,128,128]{2,1,0:T(8,128)S(1)}, u32[]{:S(2)}, u32[]{:S(2)}) async-start(f32[4,128,128]{2,1,0:T(8,128)} %bitcast.10), calls=%async_computation.4 | async-start | bytes 524288 | tf_op jit(solution)/shard_map/basis/all_to_all | solution.py:338
  73.6 0.7 pad_add_fusion.idx
  74.3 0.0 copy-done.2
  74.3 7.6 %far.1 = f32[16,32,128]{2,1,0:T(8,128)} custom-call(s32[3]{0:T(128)} %pad_add_fusion.idx, f32[16,8,128]{2,1,0:T(8,128)} %copy-done.5, f32[32,40,128]{2,1,0:T(8,128)} %copy-done.2), custom_call_target="tpu_custom_call" | custom-call | flops 805306368 | bytes 524288 | tf_op jit(solution)/shard_map/far/far/pallas_call | solution.py:403
  81.9 0.0 all-to-all-done.4.basis
  81.9 22.1 %all_to_all.61.phi = f32[16,32,128]{2,1,0:T(8,128)} all-to-all(f32[16,32,128]{2,1,0:T(8,128)} %far.1), channel_id=1, replica_groups=mesh['z'=8,'y'=8,'k'=2,'x'=4] {'y','k'}, dimensions={0} | all-to-all | bytes 524288 | tf_op jit(solution)/shard_map/far/all_to_all | solution.py:338
  104.0 0.0 copy-done.1
  104.0 2.5 %couple.1 = (f32[64,256]{1,0:T(8,128)}, f32[256,256]{1,0:T(8,128)}, f32[16,8,128]{2,1,0:T(8,128)}) custom-call(s32[3]{0:T(128)} %pad_add_fusion.idx, f32[16,32,128]{2,1,0:T(8,128)} %all_to_all.61.phi, f32[4,32,128]{2,1,0:T(8,128)} %all_to_all.60.nearf, f32[4,32,128]{2,1,0:T(8,128)} %interp.3, f32[4,128,128]{2,1,0:T(8,128)} %copy-done.1), custom_call_target="tpu_custom_call" | custom-call | bytes 524288 | tf_op jit(solution)/shard_map/couple/couple/pallas_call | solution.py:420
  106.5 10.7 %all_to_all.62 = f32[16,8,128]{2,1,0:T(8,128)S(1)} all-to-all(f32[16,8,128]{2,1,0:T(8,128)} %get-tuple-element.17), channel_id=1, replica_groups=mesh['z'=8,'y'=8,'k'=2,'x'=4] {'y','k'}, dimensions={0} | all-to-all | bytes 131072 | tf_op jit(solution)/shard_map/couple/all_to_all | solution.py:338
  117.2 15.3 %all_to_all.63 = f32[32,8,128]{2,1,0:T(8,128)S(1)} all-to-all(f32[32,8,128]{2,1,0:T(8,128)S(1)} %broadcast_in_dim.19), channel_id=1, replica_groups=mesh['z'=8,'y'=8,'k'=2,'x'=4] {'z','x'}, dimensions={0} | all-to-all | bytes 262144 | tf_op jit(solution)/shard_map/couple/all_to_all | solution.py:328
  132.5 12.8 %all_to_all.64.coup = f32[16,8,128]{2,1,0:T(8,128)} all-to-all(f32[16,8,128]{2,1,0:T(8,128)S(1)} %broadcast_in_dim.20), channel_id=1, replica_groups=mesh['z'=8,'y'=8,'k'=2,'x'=4] {'y','k'}, dimensions={0} | all-to-all | bytes 131072 | tf_op jit(solution)/shard_map/couple/all_to_all | solution.py:328
  145.3 2.4 %residual.1 = (f32[64,256]{1,0:T(8,128)}, f32[16,8,128]{2,1,0:T(8,128)}, f32[4,64,64]{2,1,0:T(8,128)}) custom-call(f32[16,8,128]{2,1,0:T(8,128)} %all_to_all.64.coup, f32[64,256]{1,0:T(8,128)} %get-tuple-element.18.applied, f32[256,256]{1,0:T(8,128)} %get-tuple-element.19.stacked), custom_call_target="tpu_custom_call" | custom-call | bytes 524288 | tf_op jit(solution)/shard_map/residual/residual/pallas_call | solution.py:431
  147.7 11.2 %all_to_all.65 = f32[16,8,128]{2,1,0:T(8,128)S(1)} all-to-all(f32[16,8,128]{2,1,0:T(8,128)} %get-tuple-element.20), channel_id=1, replica_groups=mesh['z'=8,'y'=8,'k'=2,'x'=4] {'y','k'}, dimensions={0} | all-to-all | bytes 131072 | tf_op jit(solution)/shard_map/residual/all_to_all | solution.py:338
  159.0 0.0 copy-start.4
  159.0 12.9 %all_to_all.66 = f32[32,8,128]{2,1,0:T(8,128)S(1)} all-to-all(f32[32,8,128]{2,1,0:T(8,128)S(1)} %broadcast_in_dim.21), channel_id=1, replica_groups=mesh['z'=8,'y'=8,'k'=2,'x'=4] {'z','x'}, dimensions={0} | all-to-all | bytes 262144 | tf_op jit(solution)/shard_map/residual/all_to_all | solution.py:328
  172.0 0.0 copy-done.4
  172.0 0.7 broadcast_in_dim.23
  172.7 3.4 %all-to-all-start.11 = ((f32[4,64,256]{2,1,0:T(8,128)}), f32[4,64,256]{2,1,0:T(8,128)S(1)}, u32[]{:S(2)}, u32[]{:S(2)}) async-start(f32[4,64,256]{2,1,0:T(8,128)} %broadcast_in_dim.23), calls=%async_computation.11 | async-start | bytes 524288 | tf_op jit(solution)/shard_map/residual/all_to_all | solution.py:328
  176.1 5.5 %all-to-all-done.11.residual = f32[4,64,256]{2,1,0:T(8,128)S(1)} async-done(((f32[4,64,256]{2,1,0:T(8,128)}), f32[4,64,256]{2,1,0:T(8,128)S(1)}, u32[]{:S(2)}, u32[]{:S(2)}) %all-to-all-start.11) | async-done | bytes 262176 | tf_op jit(solution)/shard_map/residual/all_to_all | solution.py:328
  181.6 13.7 %all_to_all.67.gram = f32[16,8,128]{2,1,0:T(8,128)} all-to-all(f32[16,8,128]{2,1,0:T(8,128)S(1)} %broadcast_in_dim.22), channel_id=1, replica_groups=mesh['z'=8,'y'=8,'k'=2,'x'=4] {'y','k'}, dimensions={0} | all-to-all | bytes 131072 | tf_op jit(solution)/shard_map/residual/all_to_all | solution.py:328
  195.3 0.0 copy-done
  195.3 7.4 %finish.1 = (f32[2,16,512]{2,1,0:T(8,128)}, f32[64,64]{1,0:T(8,128)}) custom-call(s32[3]{0:T(128)} %pad_add_fusion.idx, f32[16,8,128]{2,1,0:T(8,128)} %all_to_all.67.gram, f32[4,64,256]{2,1,0:T(8,128)} %copy-done), custom_call_target="tpu_custom_call" | custom-call | bytes 524288 | tf_op jit(solution)/shard_map/finish/finish/pallas_call | solution.py:443
  (14 shorter events, 0.2 us)
Async XLA Ops:
  6.0 10.3 %copy-start.7 = (f32[40,512]{1,0:T(8,128)S(1)}, f32[40,512]{1,0:T(8,128)}, u32[]{:S(2)}) copy-start(f32[40,512]{1,0:T(8,128)} %get-tuple-element.16.own) | copy-start | bytes 245764
  6.0 27.9 %all-to-all-start = ((f32[16,8,128]{2,1,0:T(8,128)}), f32[16,8,128]{2,1,0:T(8,128)S(1)}, u32[]{:S(2)}, u32[]{:S(2)}) async-start(f32[16,8,128]{2,1,0:T(8,128)} %broadcast_in_dim.17), calls=%async_computation | async-start | bytes 131072 | tf_op jit(solution)/shard_map/info/all_to_all | solution.py:328
  16.3 5.5 %collective-permute-start = (f32[40,512]{1,0:T(8,128)S(1)}, f32[40,512]{1,0:T(8,128)S(1)}, u32[]{:S(2)}, u32[]{:S(2)}) collective-permute-start(f32[40,512]{1,0:T(8,128)S(1)} %copy-done.7), channel_id=1, source_target_pairs={{0,4},{4,8},{8,12},{12,16},{16,20},{20,24},{24,28},{28,32},{32,36}... | collective-permute-start | bytes 245768 | tf_op jit(solution)/shard_map/halo/ppermute | solution.py:380
  19.9 5.8 %collective-permute-start.1 = (f32[40,512]{1,0:T(8,128)S(1)}, f32[40,512]{1,0:T(8,128)S(1)}, u32[]{:S(2)}, u32[]{:S(2)}) collective-permute-start(f32[40,512]{1,0:T(8,128)S(1)} %copy-done.7), channel_id=1, source_target_pairs={{4,0},{8,4},{12,8},{16,12},{20,16},{24,20},{28,24},{32,28},{36,32}... | collective-permute-start | bytes 245768 | tf_op jit(solution)/shard_map/halo/ppermute | solution.py:381
  21.8 3.8 %copy-start.8 = (f32[40,512]{1,0:T(8,128)}, f32[40,512]{1,0:T(8,128)S(1)}, u32[]{:S(2)}) copy-start(f32[40,512]{1,0:T(8,128)S(1)} %collective-permute-done.prev) | copy-start | bytes 245764
  25.6 0.6 copy-start.9
  34.0 8.5 %copy-start.6 = (f32[40,128]{1,0:T(8,128)S(1)}, f32[40,128]{1,0:T(8,128)}, u32[]{:S(2)}) copy-start(f32[40,128]{1,0:T(8,128)} %get-tuple-element.15) | copy-start | bytes 61444
  34.0 8.4 %copy-start.5 = (f32[16,8,128]{2,1,0:T(8,128)}, f32[16,8,128]{2,1,0:T(8,128)S(1)}, u32[]{:S(2)}) copy-start(f32[16,8,128]{2,1,0:T(8,128)S(1)} %all-to-all-done.info) | copy-start | bytes 196612
  43.3 9.9 %copy-start.3 = (f32[4,2,16,512]{3,2,1,0:T(8,128)S(1)}, f32[4,2,16,512]{3,2,1,0:T(8,128)}, u32[]{:S(2)}) copy-start(f32[4,2,16,512]{3,2,1,0:T(8,128)} %param.7) | copy-start | bytes 786436
  43.3 25.9 %all-to-all-start.1 = ((f32[32,40,128]{2,1,0:T(8,128)}), f32[32,40,128]{2,1,0:T(8,128)S(1)}, u32[]{:S(2)}, u32[]{:S(2)}) async-start(f32[32,40,128]{2,1,0:T(8,128)} %broadcast_in_dim.18), calls=%async_computation.1 | async-start | bytes 1310720 | tf_op jit(solution)/shard_map/gather/all_to_all | solution.py:328
  69.2 5.1 %copy-start.2 = (f32[32,40,128]{2,1,0:T(8,128)}, f32[32,40,128]{2,1,0:T(8,128)S(1)}, u32[]{:S(2)}) copy-start(f32[32,40,128]{2,1,0:T(8,128)S(1)} %all-to-all-done.1.gathered) | copy-start | bytes 1966084
  69.2 12.7 %all-to-all-start.4 = ((f32[4,128,128]{2,1,0:T(8,128)}), f32[4,128,128]{2,1,0:T(8,128)S(1)}, u32[]{:S(2)}, u32[]{:S(2)}) async-start(f32[4,128,128]{2,1,0:T(8,128)} %bitcast.10), calls=%async_computation.4 | async-start | bytes 524288 | tf_op jit(solution)/shard_map/basis/all_to_all | solution.py:338
  81.9 22.1 %copy-start.1 = (f32[4,128,128]{2,1,0:T(8,128)}, f32[4,128,128]{2,1,0:T(8,128)S(1)}, u32[]{:S(2)}) copy-start(f32[4,128,128]{2,1,0:T(8,128)S(1)} %all-to-all-done.4.basis) | copy-start | bytes 786436
  159.0 12.9 %copy-start.4 = (f32[64,256]{1,0:T(8,128)S(1)}, f32[64,256]{1,0:T(8,128)}, u32[]{:S(2)}) copy-start(f32[64,256]{1,0:T(8,128)} %get-tuple-element.21) | copy-start | bytes 196612
  172.7 8.9 %all-to-all-start.11 = ((f32[4,64,256]{2,1,0:T(8,128)}), f32[4,64,256]{2,1,0:T(8,128)S(1)}, u32[]{:S(2)}, u32[]{:S(2)}) async-start(f32[4,64,256]{2,1,0:T(8,128)} %broadcast_in_dim.23), calls=%async_computation.11 | async-start | bytes 524288 | tf_op jit(solution)/shard_map/residual/all_to_all | solution.py:328
  181.6 13.7 %copy-start = (f32[4,64,256]{2,1,0:T(8,128)}, f32[4,64,256]{2,1,0:T(8,128)S(1)}, u32[]{:S(2)}) copy-start(f32[4,64,256]{2,1,0:T(8,128)S(1)} %all-to-all-done.11.residual) | copy-start | bytes 786436

commit v2 on v1

v2 whole, which is shorter than its diff:
```python
import functools
import math

import jax
import jax.numpy as jnp
from jax import lax
from jax.experimental import pallas as pl
from jax.experimental.pallas import tpu as pltpu
from jax.sharding import Mesh
from jax.sharding import PartitionSpec as P

BOX_DEV = 4
PTS = 128
SKEL = 32
SLOTS = 27
REACH = 4
WAVENUMBER = 6.0
SMOOTHING = 0.1
SHIFT_SCALE = 0.02
EPSILON = 1e-06
HIGHEST = lax.Precision.HIGHEST
F32 = jnp.float32
BF16 = jnp.bfloat16
INTERPRET = False

GRID = (8, 8, 2)
BOX = ("z", "y", "k")
YK = ("y", "k")
ZX = ("z", "x")

TURNS = WAVENUMBER / (2.0 * math.pi)
SIN_C = (3.1415926401307073, -5.167710083507923, 2.5500775232148563, -0.5982912856211671, 0.07765766030589402)
COS_C = (
    0.9999999997799043,
    -4.934802137078822,
    4.0587091595560825,
    -1.335212003047854,
    0.2349373138047365,
    -0.02439632433202294,
)


def poly(coefs, u):
    r = coefs[-1] * u + coefs[-2]
    for c in coefs[-3::-1]:
        r = r * u + c
    return r


def helmholtz(tx, ty, tz, sx, sy, sz, weight):
    dx = tx - sx
    dy = ty - sy
    dz = tz - sz
    s = SMOOTHING * SMOOTHING + dx * dx + dy * dy + dz * dz
    r = lax.rsqrt(s)
    r = r * (1.5 - (0.5 * s) * (r * r))
    t = (s * r) * TURNS
    f = t - lax.round(t, lax.RoundingMethod.TO_NEAREST_EVEN)
    u = f * f
    sn = f * poly(SIN_C, u)
    cs = poly(COS_C, u)
    two = sn + sn
    w = r * weight
    return (1.0 - two * sn) * w, (two * cs) * w


def split(x):
    hi = x.astype(BF16)
    return hi, (x - hi.astype(F32)).astype(BF16)


def dot(a, b, ca, cb, precision=None):
    return lax.dot_general(
        a, b, (((ca,), (cb,)), ((), ())), precision=precision, preferred_element_type=F32
    )


def rotate(rows):
    parts = []
    for g in range(rows.shape[0] // 32):
        parts.append(-rows[32 * g + 16 : 32 * g + 32])
        parts.append(rows[32 * g : 32 * g + 16])
    return jnp.concatenate(parts, axis=0)


def group_index(dims):
    return (lax.axis_index("z") * dims[1] + lax.axis_index("y")) * dims[2] + lax.axis_index("k")


def call(kernel, out_shape, in_specs, scratch=(), flops=0):
    vmem = pl.BlockSpec(memory_space=pltpu.VMEM)
    single = not isinstance(out_shape, (tuple, list))
    return pl.pallas_call(
        kernel,
        out_shape=out_shape,
        in_specs=in_specs,
        out_specs=vmem if single else [vmem] * len(out_shape),
        scratch_shapes=list(scratch),
        cost_estimate=pl.CostEstimate(flops=flops, bytes_accessed=1 << 19, transcendentals=0),
        interpret=INTERPRET,
    )


VMEM = pl.BlockSpec(memory_space=pltpu.VMEM)
SMEM = pl.BlockSpec(memory_space=pltpu.SMEM)


def centred(offsets, b, group):
    axis = lax.broadcasted_iota(jnp.int32, (8, 1), 0)
    shift = jnp.where(axis == 0, group.astype(F32), jnp.where(axis == 1, float(b), 0.0))
    cols = slice(PTS * b, PTS * b + PTS)
    return jnp.concatenate([offsets[:, cols], jnp.zeros((5, PTS), F32)], axis=0) + shift


def place_kernel(dims, near, count, offsets, skel, info, skelpos):
    group = group_index(dims)
    x = lax.axis_index("x")
    spots = []
    for b in range(BOX_DEV):
        q = lax.broadcasted_iota(jnp.int32, (PTS, SKEL), 0)
        pick = (q == skel[b : b + 1, :]).astype(F32)
        spots.append(dot(centred(offsets, b, group), pick, 1, 0, HIGHEST))
    skelpos[...] = jnp.concatenate(spots, axis=1)
    row = lax.broadcasted_iota(jnp.int32, (8, PTS), 0)
    lane = lax.broadcasted_iota(jnp.int32, (8, PTS), 1)
    box_of = BOX_DEV * (group + row - 1) + lane // SKEL
    listed = jnp.zeros((8, PTS), F32)
    for s in range(SLOTS):
        box = jnp.where(s < count[x], near[x, s], -1000)
        listed = jnp.where(box_of == box, 1.0, listed)
    spot = spots[0]
    for b in range(1, BOX_DEV):
        spot = jnp.where(x == b, spots[b], spot)
    about = jnp.concatenate(
        [
            jnp.concatenate([spot[0:3], jnp.zeros((3, PTS - SKEL), F32)], axis=1),
            1.0 - listed[0:3],
            jnp.zeros((2, PTS), F32),
        ],
        axis=0,
    )
    info[...] = jnp.broadcast_to(about[None], info.shape)


def prep_kernel(dims, cur, weights, offsets, interp, halo, charge):
    group = group_index(dims)
    src = jnp.concatenate([cur[3, 0], cur[3, 1]], axis=0) * weights[...]
    halo[0:32, :] = src
    charges = []
    for b in range(BOX_DEV):
        cols = slice(PTS * b, PTS * b + PTS)
        halo[32:40, cols] = centred(offsets, b, group)
        charges.append(dot(src[:, cols], interp[b], 1, 1, HIGHEST))
    charge[...] = jnp.concatenate(charges, axis=1)


def from_x(r):
    n = lax.axis_size("x")
    return lax.rem(lax.axis_index("x") + n - r, n)


def pack_kernel(skelpos, *refs):
    charges, far = refs[:-1], refs[-1]
    n = 32 * len(charges)
    for r, ref in enumerate(charges):
        at = pl.multiple_of(32 * from_x(r), 32)
        far[0, pl.ds(at, 32), :] = ref[...]
    far[0, n : n + 8, :] = skelpos[...]
    far[1:] = jnp.broadcast_to(far[0][None], (far.shape[0] - 1,) + far.shape[1:])


def near_kernel(dims, near, count, prev, own, nxt, cur, *refs):
    outs, (ext, mult, tpos, acc) = refs[:-4], refs[-4:]
    for e in range(BOX_DEV):
        cols = slice(PTS * e, PTS * e + PTS)
        ext[e] = prev[:, cols]
        ext[BOX_DEV + e] = own[:, cols]
        ext[2 * BOX_DEV + e] = nxt[:, cols]
    stack = jnp.concatenate(
        [own[32:40, PTS * t : PTS * t + PTS] for t in range(BOX_DEV)]
        + [jnp.zeros((PTS - 8 * BOX_DEV, PTS), F32)],
        axis=0,
    )
    turned = stack.T
    base = BOX_DEV * (group_index(dims) - 1)
    erow = lax.broadcasted_iota(jnp.int32, (16, PTS), 0)
    for t in range(BOX_DEV):
        for c in range(3):
            tpos[t, c] = jnp.broadcast_to(turned[:, 8 * t + c : 8 * t + c + 1], (PTS, PTS))
        m = jnp.zeros((16, PTS), F32)
        for s in range(SLOTS):
            box = jnp.where(s < count[t], near[t, s] - base, -1000)
            m = m + jnp.where(erow == box, 1.0, 0.0)
        mult[t] = m
    acc[...] = jnp.zeros_like(acc)

    def step(d, carry):
        for t in range(BOX_DEV):
            e = t + d
            rows = ext[e, 0:32, :]
            re, im = helmholtz(
                tpos[t, 0],
                tpos[t, 1],
                tpos[t, 2],
                ext[e, 32:33, :],
                ext[e, 33:34, :],
                ext[e, 34:35, :],
                0.25 / math.pi,
            )
            khi, klo = split(jnp.concatenate([re, im], axis=1))
            rhi, rlo = split(jnp.concatenate([rows, rotate(rows)], axis=1))
            both = dot(jnp.concatenate([rhi, rlo], axis=0), khi, 1, 1)
            part = both[0:32] + (both[32:64] + dot(rhi, klo, 1, 1))
            acc[t] += part * mult[t, pl.ds(e, 1), :]
        return carry

    lax.fori_loop(0, 2 * REACH + 1, step, 0)
    for t in range(BOX_DEV):
        cols = slice(PTS * t, PTS * t + PTS)
        acc[t] += 0.5 * jnp.concatenate([cur[3, 0, :, cols], cur[3, 1, :, cols]], axis=0)
    n = len(outs)
    for r, out in enumerate(outs):
        out[...] = acc[lax.rem(lax.axis_index("x") + r, n)]


def far_kernel(dims, info, gathered, out, tpos, rhi, rlo, weight, acc):
    nz, ny, nk, nx = dims
    targets = ny * nk
    mine = lax.axis_index("y") * nk + lax.axis_index("k")
    first = lax.axis_index("z") * targets
    stack = jnp.concatenate([info[d] for d in range(targets)], axis=0)
    if targets * 8 < PTS:
        stack = jnp.concatenate([stack, jnp.zeros((PTS - targets * 8, PTS), F32)], axis=0)
    turned = stack.T
    for d in range(targets):
        for c in range(3):
            tpos[c, SKEL * d : SKEL * d + SKEL, :] = jnp.broadcast_to(
                turned[0:SKEL, 8 * d + c : 8 * d + c + 1], (SKEL, PTS)
            )
    for g in range(nz):
        rows = gathered[g, 0 : 32 * nx, :]
        hi, lo = split(jnp.concatenate([rows, rotate(rows)], axis=1))
        rhi[g] = hi
        rlo[g] = lo
    acc[...] = jnp.zeros_like(acc)
    per = min(4, targets)

    def step(g, carry):
        sx = gathered[g, 32 * nx + 0 : 32 * nx + 1, :]
        sy = gathered[g, 32 * nx + 1 : 32 * nx + 2, :]
        sz = gathered[g, 32 * nx + 2 : 32 * nx + 3, :]
        source_group = g * targets + mine
        for d in range(targets):
            delta = source_group - (first + d)
            w = jnp.where(delta == -1, info[d, 3:4, :], 1.0)
            w = jnp.where(delta == 0, info[d, 4:5, :], w)
            w = jnp.where(delta == 1, info[d, 5:6, :], w)
            weight[SKEL * d : SKEL * d + SKEL, :] = jnp.broadcast_to(
                w * (0.25 / math.pi), (SKEL, PTS)
            )
        for n in range(targets // per):
            span = slice(SKEL * per * n, SKEL * per * (n + 1))
            re, im = helmholtz(
                tpos[0, span, :],
                tpos[1, span, :],
                tpos[2, span, :],
                sx,
                sy,
                sz,
                weight[span, :],
            )
            khi, klo = split(jnp.concatenate([re, im], axis=1))
            acc[span, :] += dot(khi, rhi[g], 1, 1) + (
                dot(khi, rlo[g], 1, 1) + dot(klo, rhi[g], 1, 1)
            )
        return carry

    lax.fori_loop(0, nz, step, 0)
    for d in range(targets):
        out[d] = acc[SKEL * d : SKEL * d + SKEL, :]


def halves(rows, nx):
    re = jnp.concatenate([rows[32 * c : 32 * c + 16] for c in range(nx)], axis=0)
    im = jnp.concatenate([rows[32 * c + 16 : 32 * c + 32] for c in range(nx)], axis=0)
    return jnp.concatenate([re, im], axis=1)


def basis_kernel(scale, *refs):
    parts, (ordered, pieces) = refs[:-2], refs[-2:]
    nx = len(parts)
    for r, ref in enumerate(parts):
        c = from_x(r)
        for k in range(4):
            at = pl.ds(pl.multiple_of(16 * (nx * k + c), 16), 16)
            for p in range(2):
                ordered[p, at, :] = ref[32 * k + 16 * p : 32 * k + 16 * p + 16, :]
    cols = pl.ds(pl.multiple_of(PTS * lax.axis_index("x"), PTS), PTS)
    b2 = jnp.concatenate([ordered[0, :, cols], ordered[1, :, cols]], axis=1)
    gram = dot(b2, b2, 1, 1, HIGHEST) * scale
    n = pieces.shape[0]
    per = 256 // n
    for e in range(per):
        pieces[:, e, :] = gram[n * e : n * e + n, 0:PTS]
        pieces[:, per + e, :] = gram[n * e : n * e + n, PTS : 2 * PTS]


def couple_kernel(scale, phi, interp, ordered, gsum, *refs):
    nears, (applied, part, held) = refs[:-3], refs[-3:]
    nx = len(nears)
    for r, ref in enumerate(nears):
        held[from_x(r)] = ref[...]
    total = phi[0]
    for d in range(1, phi.shape[0]):
        total = total + phi[d]
    rows = dot(total, interp[lax.axis_index("x")], 0, 0, HIGHEST)
    rows = rows + jnp.concatenate([held[c] for c in range(nx)], axis=0)
    a2 = halves(rows, nx)
    applied[...] = a2
    cols = pl.ds(pl.multiple_of(PTS * lax.axis_index("x"), PTS), PTS)
    b2 = jnp.concatenate([ordered[0, :, cols], ordered[1, :, cols]], axis=1)
    c = dot(b2, a2, 1, 1, HIGHEST) * scale
    packed = jnp.concatenate([c[0:128], c[128:256]], axis=1)
    own = dot(a2, a2, 1, 1, HIGHEST) * scale
    own = jnp.concatenate([own[0:32], own[32:64]], axis=1)
    g = gsum[0]
    for d in range(1, gsum.shape[0]):
        g = g + gsum[d]
    n = part.shape[0]
    a, b, w = 128 // n, 32 // n, g.shape[0] // n
    for d in range(n):
        part[d] = jnp.concatenate(
            [
                packed[a * d : a * d + a],
                own[b * d : b * d + b],
                g[w * d : w * d + w],
                jnp.zeros((part.shape[1] - a - b - w, PTS), F32),
            ],
            axis=0,
        )


def first_sum_kernel(part, out):
    total = part[0]
    for d in range(1, part.shape[0]):
        total = total + part[d]
    out[...] = jnp.broadcast_to(total[None], out.shape)


def second_sum_kernel(rows, width, part, out):
    n = part.shape[0]
    total = part[0]
    for d in range(1, n):
        total = total + part[d]
    out[:, 0 : part.shape[1], :] = jnp.broadcast_to(
        total[None], (out.shape[0],) + total.shape
    )
    g = [part[:, rows + e, :] for e in range(width)]
    g = jnp.concatenate(g, axis=0)
    out[:, part.shape[1] :, :] = jnp.broadcast_to(g[None], (out.shape[0],) + g.shape)


def finish_kernel(width, summed, ordered, *refs):
    applied, (out, coupling, factor, inv) = refs[:-4], refs[-4:]
    n = summed.shape[0]
    a, b = 128 // n, 32 // n
    packed = jnp.concatenate([summed[d, 0:a, :] for d in range(n)], axis=0)
    c = jnp.concatenate([packed[:, 0:64], packed[:, 64:128]], axis=0)
    for k in range(4):
        coupling[k] = c[64 * k : 64 * k + 64]
    both = jnp.concatenate([summed[d, a : a + b, :] for d in range(n)], axis=0)
    g = jnp.concatenate([both[:, 0:64], both[:, 64:128]], axis=0)
    base = summed.shape[1] - width
    lines = jnp.concatenate([summed[d, base:, :] for d in range(n)], axis=0)
    bb = jnp.concatenate([lines[0:256], lines[256:512]], axis=1)
    gc = dot(bb, c, 1, 0, HIGHEST) - 2.0 * c
    g = g + dot(c, gc, 0, 0, HIGHEST)
    row = lax.broadcasted_iota(jnp.int32, (64, 64), 0)
    col = lax.broadcasted_iota(jnp.int32, (64, 64), 1)
    eye = row == col
    diag = jnp.where(eye, g, 0.0)
    trace = jnp.sum(jnp.sum(diag, axis=1, keepdims=True), axis=0, keepdims=True)
    g = g + jnp.where(eye, SHIFT_SCALE * trace / 64.0 + EPSILON, 0.0)
    m = jnp.concatenate([g, eye.astype(F32)], axis=1)
    sub = lax.broadcasted_iota(jnp.int32, (64, 1), 0)
    for j in range(63):
        line = m[j : j + 1, :]
        f = jnp.where(sub > j, m[:, j : j + 1] / line[:, j : j + 1], 0.0)
        m = m - f * line
    pivots = jnp.sum(jnp.where(eye, m[:, 0:64], 0.0), axis=1, keepdims=True)
    root = 1.0 / jnp.sqrt(pivots)
    m = m * root
    factor[...] = jnp.where(row <= col, m[:, 0:64], 0.0)
    inv[...] = m[:, 64:128]
    mine = inv[pl.ds(pl.multiple_of(16 * lax.axis_index("x"), 16), 16), :]
    back = dot(mine, c, 1, 1, HIGHEST)
    for p in range(2):
        out[p] = -dot(back, ordered[p], 1, 0, HIGHEST)
    for r, ref in enumerate(applied):
        rows = dot(mine, ref[...], 1, 0, HIGHEST)
        cols = pl.ds(pl.multiple_of(PTS * from_x(r), PTS), PTS)
        out[0, :, cols] += rows[:, 0:PTS]
        out[1, :, cols] += rows[:, PTS : 2 * PTS]


def around(blocks):
    n = lax.axis_size("x")
    return [blocks[0]] + [
        lax.ppermute(blocks[r], "x", [(i, (i + r) % n) for i in range(n)]) for r in range(1, n)
    ]


def trade(value, axes):
    return lax.all_to_all(value, axes, split_axis=0, concat_axis=0, tiled=True)


def shards(dims, basis, offsets, weights, interp, skeleton, near_boxes, near_count):
    nz, ny, nk, nx = dims
    groups = nz * ny * nk
    targets = ny * nk
    sources = nz * nx
    points = BOX_DEV * PTS
    scale = 1.0 / (groups * points)
    shape = lambda *s: jax.ShapeDtypeStruct(s, F32)

    info, skelpos = call(
        functools.partial(place_kernel, dims),
        (shape(targets, 8, PTS), shape(8, PTS)),
        [SMEM, SMEM, VMEM, VMEM],
    )(near_boxes, near_count, offsets, skeleton)
    info_all = trade(info, YK)
    halo, charge = call(
        functools.partial(prep_kernel, dims), (shape(40, points), shape(32, PTS)), [VMEM] * 4
    )(basis, weights[None], offsets, interp)
    charges = around([charge] * nx)
    far = call(pack_kernel, shape(nz, 32 * nx + 8, PTS), [VMEM] * (1 + nx))(skelpos, *charges)
    far_all = trade(far, "z")
    prev = lax.ppermute(halo, BOX, [(g, g + 1) for g in range(groups - 1)])
    nxt = lax.ppermute(halo, BOX, [(g + 1, g) for g in range(groups - 1)])
    bases = around([basis.reshape(4 * 32, points)] * nx)

    nears = call(
        functools.partial(near_kernel, dims),
        (shape(32, PTS),) * nx,
        [SMEM, SMEM] + [VMEM] * 4,
        [
            pltpu.VMEM((3 * BOX_DEV, 40, PTS), F32),
            pltpu.VMEM((BOX_DEV, 16, PTS), F32),
            pltpu.VMEM((BOX_DEV, 3, PTS, PTS), F32),
            pltpu.VMEM((BOX_DEV, 32, PTS), F32),
        ],
        flops=36 * 2 * 64 * 256 * 128 * 2,
    )(near_boxes, near_count, prev, halo, nxt, basis)
    nears = around(nears)
    ordered, pieces = call(
        functools.partial(basis_kernel, scale),
        (shape(2, 256, points), shape(sources, 512 // sources, PTS)),
        [VMEM] * nx,
    )(*bases)
    gsum = trade(pieces, ZX)

    far_part = call(
        functools.partial(far_kernel, dims),
        shape(targets, SKEL, 32 * nx),
        [VMEM, VMEM],
        [
            pltpu.VMEM((3, SKEL * targets, PTS), F32),
            pltpu.VMEM((nz, 32 * nx, 2 * PTS), BF16),
            pltpu.VMEM((nz, 32 * nx, 2 * PTS), BF16),
            pltpu.VMEM((SKEL * targets, PTS), F32),
            pltpu.VMEM((SKEL * targets, 32 * nx), F32),
        ],
        flops=3 * 2 * 512 * 2048 * 128,
    )(info_all, far_all)
    phi = trade(far_part, YK)

    used = 128 // targets + 32 // targets
    width = 512 // sources // targets
    tall = -(-(used + width) // 8) * 8
    applied, part = call(
        functools.partial(couple_kernel, scale),
        (shape(64, 2 * PTS), shape(targets, tall, PTS)),
        [VMEM] * (4 + nx),
        [pltpu.VMEM((nx, 32, PTS), F32)],
    )(phi, interp, ordered, gsum, *nears)
    part = trade(part, YK)
    applied = around([applied] * nx)
    part = call(first_sum_kernel, shape(sources, tall, PTS), [VMEM])(part)
    part = trade(part, ZX)
    part = call(
        functools.partial(second_sum_kernel, used, width),
        shape(targets, tall + width * sources, PTS),
        [VMEM],
    )(part)
    summed = trade(part, YK)

    new_block, coupling, factor = call(
        functools.partial(finish_kernel, width * sources),
        (shape(2, 16, points), shape(4, 64, 64), shape(64, 64)),
        [VMEM] * (2 + nx),
        [pltpu.VMEM((64, 64), F32)],
    )(summed, ordered, *applied)
    return new_block, coupling, factor


def solution(mesh):
    boxes, cols = mesh.devices.shape
    nk = GRID[2]
    ny = GRID[1] if boxes == math.prod(GRID) else 2
    nz = boxes // (ny * nk)
    dims = (nz, ny, nk, cols)
    fine = Mesh(mesh.devices.reshape(dims), ("z", "y", "k", "x"))
    return jax.shard_map(
        functools.partial(shards, dims),
        mesh=fine,
        in_specs=(
            P(None, None, "x", BOX),
            P(None, BOX),
            P(BOX),
            P(BOX, None, None),
            P(BOX, None),
            P(BOX, None),
            P(BOX),
        ),
        out_specs=(P(None, "x", BOX), P(), P()),
        check_vma=False,
    )
```

time: 204 us -> 194 us (0.951)
  blocking collectives: 107 us -> 37.9 us
  starting transfers between devices: 33.5 us -> 80.9 us
  Pallas kernels: 29.6 us -> 38.6 us
  waiting for transfers between devices: 24.4 us -> 28.6 us
    all_to_all x4 -> x0, blocking collectives: 54.7 us -> none  [share(): lax.all_to_all(jnp.broadcast_to(value[None], (count,) + value.shape), axe...]
    all_to_all x1 -> x5, starting transfers between devices: 4.43 us -> 42.9 us  [trade(): return lax.all_to_all(value, axes, split_axis=0, concat_axis=0, tiled=True)]
    ppermute x0 -> x12, starting transfers between devices: none -> 32.4 us  [around(): lax.ppermute(blocks[r], 'x', [(i, (i + r) % n) for i in range(n)])]
    all_to_all x3 -> x0, starting transfers between devices: 23.6 us -> none  [share(): lax.all_to_all(jnp.broadcast_to(value[None], (count,) + value.shape), axe...]
    all_to_all x3 -> x0, waiting for transfers between devices: 20.6 us -> none  [share(): lax.all_to_all(jnp.broadcast_to(value[None], (count,) + value.shape), axe...]
    ppermute x0 -> x12, waiting for transfers between devices: none -> 19.5 us  [around(): lax.ppermute(blocks[r], 'x', [(i, (i + r) % n) for i in range(n)])]
    all_to_all x4 -> x2, blocking collectives: 52.5 us -> 37.9 us  [trade(): return lax.all_to_all(value, axes, split_axis=0, concat_axis=0, tiled=True)]
    pallas_call x5 -> x9, Pallas kernels: 22 us -> 31.1 us  [the longest x1 9.24 us: shards(): call(functools.partial(finish_kernel, width * sources), (shape(2, 16, poi...]
  transfers between devices with their start and end apart: 6 -> 19, of which waited for: 3 -> 10; matrix products, arithmetic and copies ran while one was open for 1% -> 0% of each run, Pallas kernels for 8% -> 11%
where the time goes in v2:
time: 194 us; the launch traced here: 192 us
  starting transfers between devices  80.9 us (42%)
  Pallas kernels  38.6 us (20%)
  blocking collectives  37.9 us (20%)
  waiting for transfers between devices  28.6 us (15%)
  local copies, waits for them, and re-layouts  5.37 us (3%)
    all_to_all x5, starting transfers between devices, trade(): return lax.all_to_all(value, axes, split_axis=0, concat_axis=0, tiled=True)  42.9 us
    all_to_all x2, blocking collectives, trade(): return lax.all_to_all(value, axes, split_axis=0, concat_axis=0, tiled=True)  37.9 us
    ppermute x12, starting transfers between devices, around(): lax.ppermute(blocks[r], 'x', [(i, (i + r) % n) for i in range(n)])  32.4 us
    ppermute x12, waiting for transfers between devices, around(): lax.ppermute(blocks[r], 'x', [(i, (i + r) % n) for i in range(n)])  19.5 us
    pallas_call x1, Pallas kernels, shards(): call(functools.partial(finish_kernel, width * sources), (shape(2, 16, poi...  9.24 us
    pallas_call x1, Pallas kernels, shards(): call(functools.partial(near_kernel, dims), (shape(32, PTS),) * nx, [SMEM,...  7.81 us
    pallas_call x1, Pallas kernels, shards(): call(functools.partial(far_kernel, dims), shape(targets, SKEL, 32 * nx),...  7.56 us
    unnamed x44, local copies, waits for them, and re-layouts  5.37 us
  transfers between devices with their start and end apart: 19, of which 10 were waited for; matrix products, arithmetic and copies ran while one was open for 0% of the time, Pallas kernels for 11%

profile of v2, /device:TPU:1, one launch (start us, length us, event | category | flops | bytes accessed | tf_op | source)
XLA Modules:
  0.0 192.2 jit_solution(15971176443744450404)
XLA Ops:
  0.6 1.7 shard_map.94
  2.3 10.1 %all-to-all-start = ((f32[16,8,128]{2,1,0:T(8,128)}), f32[16,8,128]{2,1,0:T(8,128)S(1)}, u32[]{:S(2)}, u32[]{:S(2)}) async-start(f32[16,8,128]{2,1,0:T(8,128)} %get-tuple-element.15), calls=%async_computation | async-start | bytes 131072 | tf_op jit(solution)/shard_map/all_to_all | solution.py:414
  12.5 1.9 shard_map.95
  14.3 2.9 %collective-permute-start.2 = (f32[32,128]{1,0:T(8,128)}, f32[32,128]{1,0:T(8,128)S(1)}, u32[]{:S(2)}, u32[]{:S(2)}) collective-permute-start(f32[32,128]{1,0:T(8,128)} %get-tuple-element.17.refs_0_), channel_id=1, source_target_pairs={{0,3},{1,0},{2,1},{3,2},{4,7},{5,4},{6,5},{7,6},{8,11},{9,8},{10,9... | collective-permute-start | bytes 49160 | tf_op jit(solution)/shard_map/ppermute | solution.py:409
  17.2 2.4 %collective-permute-start.1 = (f32[32,128]{1,0:T(8,128)}, f32[32,128]{1,0:T(8,128)S(1)}, u32[]{:S(2)}, u32[]{:S(2)}) collective-permute-start(f32[32,128]{1,0:T(8,128)} %get-tuple-element.17.refs_0_), channel_id=1, source_target_pairs={{0,2},{1,3},{2,0},{3,1},{4,6},{5,7},{6,4},{7,5},{8,10},{9,11},{10,... | collective-permute-start | bytes 49160 | tf_op jit(solution)/shard_map/ppermute | solution.py:409
  19.6 2.5 %collective-permute-start = (f32[32,128]{1,0:T(8,128)}, f32[32,128]{1,0:T(8,128)S(1)}, u32[]{:S(2)}, u32[]{:S(2)}) collective-permute-start(f32[32,128]{1,0:T(8,128)} %get-tuple-element.17.refs_0_), channel_id=1, source_target_pairs={{0,1},{1,2},{2,3},{3,0},{4,5},{5,6},{6,7},{7,4},{8,9},{9,10},{10,1... | collective-permute-start | bytes 49160 | tf_op jit(solution)/shard_map/ppermute | solution.py:409
  22.2 1.2 collective-permute-done.1.refs_2_
  23.4 2.1 %collective-permute-done.refs_1_ = f32[32,128]{1,0:T(8,128)S(1)} collective-permute-done((f32[32,128]{1,0:T(8,128)}, f32[32,128]{1,0:T(8,128)S(1)}, u32[]{:S(2)}, u32[]{:S(2)}) %collective-permute-start) | collective-permute-done | bytes 16416 | tf_op jit(solution)/shard_map/ppermute | solution.py:409
  25.5 0.6 copy-done.15
  26.1 1.6 shard_map.96
  27.8 0.6 copy-done.8
  28.4 10.0 %all-to-all-start.1 = ((f32[8,136,128]{2,1,0:T(8,128)}), f32[8,136,128]{2,1,0:T(8,128)S(1)}, u32[]{:S(2)}, u32[]{:S(2)}) async-start(f32[8,136,128]{2,1,0:T(8,128)} %shard_map.96), calls=%async_computation.1 | async-start | bytes 1114112 | tf_op jit(solution)/shard_map/all_to_all | solution.py:414
  38.5 2.0 %collective-permute-start.5 = (f32[128,512]{1,0:T(8,128)S(1)}, f32[128,512]{1,0:T(8,128)S(1)}, u32[]{:S(2)}, u32[]{:S(2)}) collective-permute-start(f32[128,512]{1,0:T(8,128)S(1)} %bitcast.3), channel_id=1, source_target_pairs={{0,3},{1,0},{2,1},{3,2},{4,7},{5,4},{6,5},{7,6},{8,11},{9,8},{10,9... | collective-permute-start | bytes 786440 | tf_op jit(solution)/shard_map/ppermute | solution.py:409
  40.4 3.1 %collective-permute-start.4 = (f32[128,512]{1,0:T(8,128)S(1)}, f32[128,512]{1,0:T(8,128)S(1)}, u32[]{:S(2)}, u32[]{:S(2)}) collective-permute-start(f32[128,512]{1,0:T(8,128)S(1)} %bitcast.4), channel_id=1, source_target_pairs={{0,2},{1,3},{2,0},{3,1},{4,6},{5,7},{6,4},{7,5},{8,10},{9,11},{10,... | collective-permute-start | bytes 786440 | tf_op jit(solution)/shard_map/ppermute | solution.py:409
  43.5 2.8 %collective-permute-start.3 = (f32[128,512]{1,0:T(8,128)S(1)}, f32[128,512]{1,0:T(8,128)S(1)}, u32[]{:S(2)}, u32[]{:S(2)}) collective-permute-start(f32[128,512]{1,0:T(8,128)S(1)} %bitcast.5), channel_id=1, source_target_pairs={{0,1},{1,2},{2,3},{3,0},{4,5},{5,6},{6,7},{7,4},{8,9},{9,10},{10,1... | collective-permute-start | bytes 786440 | tf_op jit(solution)/shard_map/ppermute | solution.py:409
  46.3 3.3 %collective-permute-done.4.refs_2_ = f32[128,512]{1,0:T(8,128)S(1)} collective-permute-done((f32[128,512]{1,0:T(8,128)S(1)}, f32[128,512]{1,0:T(8,128)S(1)}, u32[]{:S(2)}, u32[]{:S(2)}) %collective-permute-start.4) | collective-permute-done | bytes 262176 | tf_op jit(solution)/shard_map/ppermute | solution.py:409
  49.6 7.2 %collective-permute-done.3.refs_1_ = f32[128,512]{1,0:T(8,128)S(1)} collective-permute-done((f32[128,512]{1,0:T(8,128)S(1)}, f32[128,512]{1,0:T(8,128)S(1)}, u32[]{:S(2)}, u32[]{:S(2)}) %collective-permute-start.3) | collective-permute-done | bytes 262176 | tf_op jit(solution)/shard_map/ppermute | solution.py:409
  56.8 0.7 copy-done.7
  57.5 2.5 %shard_map.98 = (f32[2,256,512]{2,1,0:T(8,128)}, f32[32,16,128]{2,1,0:T(8,128)}) custom-call(f32[128,512]{1,0:T(8,128)} %bitcast.2, f32[128,512]{1,0:T(8,128)} %copy-done.7, f32[128,512]{1,0:T(8,128)} %copy-done.6, f32[128,512]{1,0:T(8,128)} %copy-done.5), custom_call_target="tpu_custom_call" | custom-call | bytes 524288 | tf_op jit(solution)/shard_map/pallas_call | solution.py:455
  60.0 7.5 %all-to-all-start.3 = ((f32[32,16,128]{2,1,0:T(8,128)}), f32[32,16,128]{2,1,0:T(8,128)S(1)}, u32[]{:S(2)}, u32[]{:S(2)}) async-start(f32[32,16,128]{2,1,0:T(8,128)} %get-tuple-element.19), calls=%async_computation.3 | async-start | bytes 524288 | tf_op jit(solution)/shard_map/all_to_all | solution.py:414
  67.5 7.6 %shard_map.97 = f32[16,32,128]{2,1,0:T(8,128)} custom-call(f32[16,8,128]{2,1,0:T(8,128)} %copy-done.8, f32[8,136,128]{2,1,0:T(8,128)} %copy-done.4), custom_call_target="tpu_custom_call" | custom-call | flops 805306368 | bytes 524288 | tf_op jit(solution)/shard_map/pallas_call | solution.py:462
  75.1 2.8 %all-to-all-done.3.gsum = f32[32,16,128]{2,1,0:T(8,128)S(1)} async-done(((f32[32,16,128]{2,1,0:T(8,128)}), f32[32,16,128]{2,1,0:T(8,128)S(1)}, u32[]{:S(2)}, u32[]{:S(2)}) %all-to-all-start.3) | async-done | bytes 262176 | tf_op jit(solution)/shard_map/all_to_all | solution.py:414
  77.9 0.7 copy-done.2
  78.6 10.3 %all-to-all-start.2 = ((f32[16,32,128]{2,1,0:T(8,128)}), f32[16,32,128]{2,1,0:T(8,128)S(1)}, u32[]{:S(2)}, u32[]{:S(2)}) async-start(f32[16,32,128]{2,1,0:T(8,128)} %shard_map.97), calls=%async_computation.2 | async-start | bytes 524288 | tf_op jit(solution)/shard_map/all_to_all | solution.py:414
  88.9 2.0 %collective-permute-start.7 = (f32[40,512]{1,0:T(8,128)S(1)}, f32[40,512]{1,0:T(8,128)S(1)}, u32[]{:S(2)}, u32[]{:S(2)}) collective-permute-start(f32[40,512]{1,0:T(8,128)S(1)} %copy-done.19), channel_id=1, source_target_pairs={{4,0},{8,4},{12,8},{16,12},{20,16},{24,20},{28,24},{32,28},{36,32}... | collective-permute-start | bytes 245768 | tf_op jit(solution)/shard_map/ppermute | solution.py:439
  91.0 3.5 %collective-permute-start.6 = (f32[40,512]{1,0:T(8,128)S(1)}, f32[40,512]{1,0:T(8,128)S(1)}, u32[]{:S(2)}, u32[]{:S(2)}) collective-permute-start(f32[40,512]{1,0:T(8,128)S(1)} %copy-done.19), channel_id=1, source_target_pairs={{0,4},{4,8},{8,12},{12,16},{16,20},{20,24},{24,28},{28,32},{32,36}... | collective-permute-start | bytes 245768 | tf_op jit(solution)/shard_map/ppermute | solution.py:438
  94.5 3.7 %collective-permute-done.7.nxt = f32[40,512]{1,0:T(8,128)S(1)} collective-permute-done((f32[40,512]{1,0:T(8,128)S(1)}, f32[40,512]{1,0:T(8,128)S(1)}, u32[]{:S(2)}, u32[]{:S(2)}) %collective-permute-start.7) | collective-permute-done | bytes 81952 | tf_op jit(solution)/shard_map/ppermute | solution.py:439
  98.2 0.6 copy-done.20
  98.9 0.6 copy-done.21
  99.5 7.8 %shard_map.99 = (f32[32,128]{1,0:T(8,128)}, f32[32,128]{1,0:T(8,128)}, f32[32,128]{1,0:T(8,128)}, f32[32,128]{1,0:T(8,128)}) custom-call(s32[4,27]{1,0:T(4,128)} %near.3, s32[4]{0:T(128)} %count.3, f32[40,512]{1,0:T(8,128)} %copy-done.21, f32[40,512]{1,0:T(8,128)} %get-tuple-element.20.own, f32[40,512]{1,0:T(8,128)} %copy-done.20, f32[4,2,16,512]{3,2,1,0:T(8,128)} %cur.3), custom_call_target="tpu_custom_call" | custom-call | flops 301989888 | bytes 524288 | tf_op jit(solution)/shard_map/pallas_call | solution.py:442
  107.3 1.9 collective-permute-start.8
  109.2 3.9 %collective-permute-start.9 = (f32[32,128]{1,0:T(8,128)}, f32[32,128]{1,0:T(8,128)S(1)}, u32[]{:S(2)}, u32[]{:S(2)}) collective-permute-start(f32[32,128]{1,0:T(8,128)} %get-tuple-element.23), channel_id=1, source_target_pairs={{0,2},{1,3},{2,0},{3,1},{4,6},{5,7},{6,4},{7,5},{8,10},{9,11},{10,... | collective-permute-start | bytes 49160 | tf_op jit(solution)/shard_map/ppermute | solution.py:409
  113.1 3.0 %collective-permute-start.10 = (f32[32,128]{1,0:T(8,128)}, f32[32,128]{1,0:T(8,128)S(1)}, u32[]{:S(2)}, u32[]{:S(2)}) collective-permute-start(f32[32,128]{1,0:T(8,128)} %get-tuple-element.24), channel_id=1, source_target_pairs={{0,3},{1,0},{2,1},{3,2},{4,7},{5,4},{6,5},{7,6},{8,11},{9,8},{10,9... | collective-permute-start | bytes 49160 | tf_op jit(solution)/shard_map/ppermute | solution.py:409
  116.2 1.7 collective-permute-done.10.refs_3_
  118.6 2.9 %shard_map.100 = (f32[64,256]{1,0:T(8,128)}, f32[16,16,128]{2,1,0:T(8,128)}) custom-call(f32[16,32,128]{2,1,0:T(8,128)} %copy-done.3, f32[4,32,128]{2,1,0:T(8,128)} %interp.3, f32[2,256,512]{2,1,0:T(8,128)} %get-tuple-element.18.ordered, f32[32,16,128]{2,1,0:T(8,128)} %copy-done.2, f32[32,128]{1,0:T(8,128)} %get-tuple-element.21.refs_0_, ...), custom_call_target="tpu_custom_call" | custom-call | bytes 524288 | tf_op jit(solution)/shard_map/pallas_call | solution.py:480
  121.5 17.2 %all_to_all.35.part = f32[16,16,128]{2,1,0:T(8,128)} all-to-all(f32[16,16,128]{2,1,0:T(8,128)} %get-tuple-element.25), channel_id=1, replica_groups=mesh['z'=8,'y'=8,'k'=2,'x'=4] {'y','k'}, dimensions={0} | all-to-all | bytes 262144 | tf_op jit(solution)/shard_map/all_to_all | solution.py:414
  138.7 1.6 shard_map.101
  140.3 20.7 %all_to_all.36.part = f32[32,16,128]{2,1,0:T(8,128)} all-to-all(f32[32,16,128]{2,1,0:T(8,128)} %shard_map.101), channel_id=1, replica_groups=mesh['z'=8,'y'=8,'k'=2,'x'=4] {'z','x'}, dimensions={0} | all-to-all | bytes 524288 | tf_op jit(solution)/shard_map/all_to_all | solution.py:414
  161.0 1.8 shard_map.102
  162.8 4.9 %all-to-all-start.6 = ((f32[16,48,128]{2,1,0:T(8,128)}), f32[16,48,128]{2,1,0:T(8,128)S(1)}, u32[]{:S(2)}, u32[]{:S(2)}) async-start(f32[16,48,128]{2,1,0:T(8,128)} %shard_map.102), calls=%async_computation.6 | async-start | bytes 786432 | tf_op jit(solution)/shard_map/all_to_all | solution.py:414
  167.7 3.0 %collective-permute-start.13 = (f32[64,256]{1,0:T(8,128)S(1)}, f32[64,256]{1,0:T(8,128)S(1)}, u32[]{:S(2)}, u32[]{:S(2)}) collective-permute-start(f32[64,256]{1,0:T(8,128)S(1)} %copy-done.9), channel_id=1, source_target_pairs={{0,3},{1,0},{2,1},{3,2},{4,7},{5,4},{6,5},{7,6},{8,11},{9,8},{10,9... | collective-permute-start | bytes 196616 | tf_op jit(solution)/shard_map/ppermute | solution.py:409
  170.7 2.5 %collective-permute-start.12 = (f32[64,256]{1,0:T(8,128)S(1)}, f32[64,256]{1,0:T(8,128)S(1)}, u32[]{:S(2)}, u32[]{:S(2)}) collective-permute-start(f32[64,256]{1,0:T(8,128)S(1)} %copy-done.9), channel_id=1, source_target_pairs={{0,2},{1,3},{2,0},{3,1},{4,6},{5,7},{6,4},{7,5},{8,10},{9,11},{10,... | collective-permute-start | bytes 196616 | tf_op jit(solution)/shard_map/ppermute | solution.py:409
  173.2 2.5 %collective-permute-start.11 = (f32[64,256]{1,0:T(8,128)S(1)}, f32[64,256]{1,0:T(8,128)S(1)}, u32[]{:S(2)}, u32[]{:S(2)}) collective-permute-start(f32[64,256]{1,0:T(8,128)S(1)} %copy-done.9), channel_id=1, source_target_pairs={{0,1},{1,2},{2,3},{3,0},{4,5},{5,6},{6,7},{7,4},{8,9},{9,10},{10,1... | collective-permute-start | bytes 196616 | tf_op jit(solution)/shard_map/ppermute | solution.py:409
  175.7 1.8 collective-permute-done.12.refs_2_
  177.5 2.2 %collective-permute-done.11.refs_1_ = f32[64,256]{1,0:T(8,128)S(1)} collective-permute-done((f32[64,256]{1,0:T(8,128)S(1)}, f32[64,256]{1,0:T(8,128)S(1)}, u32[]{:S(2)}, u32[]{:S(2)}) %collective-permute-start.11) | collective-permute-done | bytes 65568 | tf_op jit(solution)/shard_map/ppermute | solution.py:409
  179.7 2.5 %all-to-all-done.6.summed = f32[16,48,128]{2,1,0:T(8,128)S(1)} async-done(((f32[16,48,128]{2,1,0:T(8,128)}), f32[16,48,128]{2,1,0:T(8,128)S(1)}, u32[]{:S(2)}, u32[]{:S(2)}) %all-to-all-start.6) | async-done | bytes 393248 | tf_op jit(solution)/shard_map/all_to_all | solution.py:414
  182.2 0.8 copy-done
  183.0 9.2 %shard_map.103 = (f32[2,16,512]{2,1,0:T(8,128)}, f32[4,64,64]{2,1,0:T(8,128)}, f32[64,64]{1,0:T(8,128)}) custom-call(f32[16,48,128]{2,1,0:T(8,128)} %copy-done, f32[2,256,512]{2,1,0:T(8,128)} %get-tuple-element.18.ordered, f32[64,256]{1,0:T(8,128)} %get-tuple-element.26.refs_0_, f32[64,256]{1,0:T(8,128)} %copy-done.12, f32[64,256]{1,0:T(8,128)} %copy-done.11, ...), custom_call_target="tpu_custom_call" | custom-call | bytes 524288 | tf_op jit(solution)/shard_map/pallas_call | solution.py:497
  (46 shorter events, 0.8 us)
Async XLA Ops:
  2.3 25.5 %all-to-all-start = ((f32[16,8,128]{2,1,0:T(8,128)}), f32[16,8,128]{2,1,0:T(8,128)S(1)}, u32[]{:S(2)}, u32[]{:S(2)}) async-start(f32[16,8,128]{2,1,0:T(8,128)} %get-tuple-element.15), calls=%async_computation | async-start | bytes 131072 | tf_op jit(solution)/shard_map/all_to_all | solution.py:414
  14.3 7.8 %collective-permute-start.2 = (f32[32,128]{1,0:T(8,128)}, f32[32,128]{1,0:T(8,128)S(1)}, u32[]{:S(2)}, u32[]{:S(2)}) collective-permute-start(f32[32,128]{1,0:T(8,128)} %get-tuple-element.17.refs_0_), channel_id=1, source_target_pairs={{0,3},{1,0},{2,1},{3,2},{4,7},{5,4},{6,5},{7,6},{8,11},{9,8},{10,9... | collective-permute-start | bytes 49160 | tf_op jit(solution)/shard_map/ppermute | solution.py:409
  17.2 6.2 %collective-permute-start.1 = (f32[32,128]{1,0:T(8,128)}, f32[32,128]{1,0:T(8,128)S(1)}, u32[]{:S(2)}, u32[]{:S(2)}) collective-permute-start(f32[32,128]{1,0:T(8,128)} %get-tuple-element.17.refs_0_), channel_id=1, source_target_pairs={{0,2},{1,3},{2,0},{3,1},{4,6},{5,7},{6,4},{7,5},{8,10},{9,11},{10,... | collective-permute-start | bytes 49160 | tf_op jit(solution)/shard_map/ppermute | solution.py:409
  19.6 5.9 %collective-permute-start = (f32[32,128]{1,0:T(8,128)}, f32[32,128]{1,0:T(8,128)S(1)}, u32[]{:S(2)}, u32[]{:S(2)}) collective-permute-start(f32[32,128]{1,0:T(8,128)} %get-tuple-element.17.refs_0_), channel_id=1, source_target_pairs={{0,1},{1,2},{2,3},{3,0},{4,5},{5,6},{6,7},{7,4},{8,9},{9,10},{10,1... | collective-permute-start | bytes 49160 | tf_op jit(solution)/shard_map/ppermute | solution.py:409
  22.2 3.4 %copy-start.13 = (f32[32,128]{1,0:T(8,128)}, f32[32,128]{1,0:T(8,128)S(1)}, u32[]{:S(2)}) copy-start(f32[32,128]{1,0:T(8,128)S(1)} %collective-permute-done.2.refs_3_) | copy-start | bytes 49156
  23.4 2.1 %copy-start.14 = (f32[32,128]{1,0:T(8,128)}, f32[32,128]{1,0:T(8,128)S(1)}, u32[]{:S(2)}) copy-start(f32[32,128]{1,0:T(8,128)S(1)} %collective-permute-done.1.refs_2_) | copy-start | bytes 49156
  25.5 0.6 copy-start.15
  27.8 10.7 %copy-start.1 = (f32[4,2,16,512]{3,2,1,0:T(8,128)S(1)}, f32[4,2,16,512]{3,2,1,0:T(8,128)}, u32[]{:S(2)}) copy-start(f32[4,2,16,512]{3,2,1,0:T(8,128)} %cur.3) | copy-start | bytes 786436
  27.8 0.6 copy-start.8
  28.4 31.6 %all-to-all-start.1 = ((f32[8,136,128]{2,1,0:T(8,128)}), f32[8,136,128]{2,1,0:T(8,128)S(1)}, u32[]{:S(2)}, u32[]{:S(2)}) async-start(f32[8,136,128]{2,1,0:T(8,128)} %shard_map.96), calls=%async_computation.1 | async-start | bytes 1114112 | tf_op jit(solution)/shard_map/all_to_all | solution.py:414
  38.5 7.9 %collective-permute-start.5 = (f32[128,512]{1,0:T(8,128)S(1)}, f32[128,512]{1,0:T(8,128)S(1)}, u32[]{:S(2)}, u32[]{:S(2)}) collective-permute-start(f32[128,512]{1,0:T(8,128)S(1)} %bitcast.3), channel_id=1, source_target_pairs={{0,3},{1,0},{2,1},{3,2},{4,7},{5,4},{6,5},{7,6},{8,11},{9,8},{10,9... | collective-permute-start | bytes 786440 | tf_op jit(solution)/shard_map/ppermute | solution.py:409
  40.4 9.2 %collective-permute-start.4 = (f32[128,512]{1,0:T(8,128)S(1)}, f32[128,512]{1,0:T(8,128)S(1)}, u32[]{:S(2)}, u32[]{:S(2)}) collective-permute-start(f32[128,512]{1,0:T(8,128)S(1)} %bitcast.4), channel_id=1, source_target_pairs={{0,2},{1,3},{2,0},{3,1},{4,6},{5,7},{6,4},{7,5},{8,10},{9,11},{10,... | collective-permute-start | bytes 786440 | tf_op jit(solution)/shard_map/ppermute | solution.py:409
  43.5 13.3 %collective-permute-start.3 = (f32[128,512]{1,0:T(8,128)S(1)}, f32[128,512]{1,0:T(8,128)S(1)}, u32[]{:S(2)}, u32[]{:S(2)}) collective-permute-start(f32[128,512]{1,0:T(8,128)S(1)} %bitcast.5), channel_id=1, source_target_pairs={{0,1},{1,2},{2,3},{3,0},{4,5},{5,6},{6,7},{7,4},{8,9},{9,10},{10,1... | collective-permute-start | bytes 786440 | tf_op jit(solution)/shard_map/ppermute | solution.py:409
  46.3 10.5 %copy-start.5 = (f32[128,512]{1,0:T(8,128)}, f32[128,512]{1,0:T(8,128)S(1)}, u32[]{:S(2)}) copy-start(f32[128,512]{1,0:T(8,128)S(1)} %collective-permute-done.5.refs_3_) | copy-start | bytes 786436
  49.6 7.2 %copy-start.6 = (f32[128,512]{1,0:T(8,128)}, f32[128,512]{1,0:T(8,128)S(1)}, u32[]{:S(2)}) copy-start(f32[128,512]{1,0:T(8,128)S(1)} %collective-permute-done.4.refs_2_) | copy-start | bytes 786436
  56.8 0.7 copy-start.7
  60.0 7.5 %copy-start.4 = (f32[8,136,128]{2,1,0:T(8,128)}, f32[8,136,128]{2,1,0:T(8,128)S(1)}, u32[]{:S(2)}) copy-start(f32[8,136,128]{2,1,0:T(8,128)S(1)} %all-to-all-done.1.gathered) | copy-start | bytes 1671172
  60.0 17.9 %all-to-all-start.3 = ((f32[32,16,128]{2,1,0:T(8,128)}), f32[32,16,128]{2,1,0:T(8,128)S(1)}, u32[]{:S(2)}, u32[]{:S(2)}) async-start(f32[32,16,128]{2,1,0:T(8,128)} %get-tuple-element.19), calls=%async_computation.3 | async-start | bytes 524288 | tf_op jit(solution)/shard_map/all_to_all | solution.py:414
  75.1 13.8 %copy-start.19 = (f32[40,512]{1,0:T(8,128)S(1)}, f32[40,512]{1,0:T(8,128)}, u32[]{:S(2)}) copy-start(f32[40,512]{1,0:T(8,128)} %get-tuple-element.20.own) | copy-start | bytes 245764
  77.9 0.7 copy-start.2
  78.6 39.2 %all-to-all-start.2 = ((f32[16,32,128]{2,1,0:T(8,128)}), f32[16,32,128]{2,1,0:T(8,128)S(1)}, u32[]{:S(2)}, u32[]{:S(2)}) async-start(f32[16,32,128]{2,1,0:T(8,128)} %shard_map.97), calls=%async_computation.2 | async-start | bytes 524288 | tf_op jit(solution)/shard_map/all_to_all | solution.py:414
  88.9 9.3 %collective-permute-start.7 = (f32[40,512]{1,0:T(8,128)S(1)}, f32[40,512]{1,0:T(8,128)S(1)}, u32[]{:S(2)}, u32[]{:S(2)}) collective-permute-start(f32[40,512]{1,0:T(8,128)S(1)} %copy-done.19), channel_id=1, source_target_pairs={{4,0},{8,4},{12,8},{16,12},{20,16},{24,20},{28,24},{32,28},{36,32}... | collective-permute-start | bytes 245768 | tf_op jit(solution)/shard_map/ppermute | solution.py:439
  91.0 7.3 %collective-permute-start.6 = (f32[40,512]{1,0:T(8,128)S(1)}, f32[40,512]{1,0:T(8,128)S(1)}, u32[]{:S(2)}, u32[]{:S(2)}) collective-permute-start(f32[40,512]{1,0:T(8,128)S(1)} %copy-done.19), channel_id=1, source_target_pairs={{0,4},{4,8},{8,12},{12,16},{16,20},{20,24},{24,28},{28,32},{32,36}... | collective-permute-start | bytes 245768 | tf_op jit(solution)/shard_map/ppermute | solution.py:438
  98.2 0.6 copy-start.20
  98.9 0.6 copy-start.21
  107.3 8.8 %collective-permute-start.8 = (f32[32,128]{1,0:T(8,128)}, f32[32,128]{1,0:T(8,128)S(1)}, u32[]{:S(2)}, u32[]{:S(2)}) collective-permute-start(f32[32,128]{1,0:T(8,128)} %get-tuple-element.22), channel_id=1, source_target_pairs={{0,1},{1,2},{2,3},{3,0},{4,5},{5,6},{6,7},{7,4},{8,9},{9,10},{10,1... | collective-permute-start | bytes 49160 | tf_op jit(solution)/shard_map/ppermute | solution.py:409
  109.2 6.9 %collective-permute-start.9 = (f32[32,128]{1,0:T(8,128)}, f32[32,128]{1,0:T(8,128)S(1)}, u32[]{:S(2)}, u32[]{:S(2)}) collective-permute-start(f32[32,128]{1,0:T(8,128)} %get-tuple-element.23), channel_id=1, source_target_pairs={{0,2},{1,3},{2,0},{3,1},{4,6},{5,7},{6,4},{7,5},{8,10},{9,11},{10,... | collective-permute-start | bytes 49160 | tf_op jit(solution)/shard_map/ppermute | solution.py:409
  113.1 4.7 %collective-permute-start.10 = (f32[32,128]{1,0:T(8,128)}, f32[32,128]{1,0:T(8,128)S(1)}, u32[]{:S(2)}, u32[]{:S(2)}) collective-permute-start(f32[32,128]{1,0:T(8,128)} %get-tuple-element.24), channel_id=1, source_target_pairs={{0,3},{1,0},{2,1},{3,2},{4,7},{5,4},{6,5},{7,6},{8,11},{9,8},{10,9... | collective-permute-start | bytes 49160 | tf_op jit(solution)/shard_map/ppermute | solution.py:409
  116.1 1.7 copy-start.16
  116.2 1.7 copy-start.17
  117.8 0.6 copy-start.18
  117.8 0.7 copy-start.3
  162.8 4.9 %copy-start.9 = (f32[64,256]{1,0:T(8,128)S(1)}, f32[64,256]{1,0:T(8,128)}, u32[]{:S(2)}) copy-start(f32[64,256]{1,0:T(8,128)} %get-tuple-element.26.refs_0_) | copy-start | bytes 196612
  162.8 19.5 %all-to-all-start.6 = ((f32[16,48,128]{2,1,0:T(8,128)}), f32[16,48,128]{2,1,0:T(8,128)S(1)}, u32[]{:S(2)}, u32[]{:S(2)}) async-start(f32[16,48,128]{2,1,0:T(8,128)} %shard_map.102), calls=%async_computation.6 | async-start | bytes 786432 | tf_op jit(solution)/shard_map/all_to_all | solution.py:414
  167.7 8.0 %collective-permute-start.13 = (f32[64,256]{1,0:T(8,128)S(1)}, f32[64,256]{1,0:T(8,128)S(1)}, u32[]{:S(2)}, u32[]{:S(2)}) collective-permute-start(f32[64,256]{1,0:T(8,128)S(1)} %copy-done.9), channel_id=1, source_target_pairs={{0,3},{1,0},{2,1},{3,2},{4,7},{5,4},{6,5},{7,6},{8,11},{9,8},{10,9... | collective-permute-start | bytes 196616 | tf_op jit(solution)/shard_map/ppermute | solution.py:409
  170.7 6.8 %collective-permute-start.12 = (f32[64,256]{1,0:T(8,128)S(1)}, f32[64,256]{1,0:T(8,128)S(1)}, u32[]{:S(2)}, u32[]{:S(2)}) collective-permute-start(f32[64,256]{1,0:T(8,128)S(1)} %copy-done.9), channel_id=1, source_target_pairs={{0,2},{1,3},{2,0},{3,1},{4,6},{5,7},{6,4},{7,5},{8,10},{9,11},{10,... | collective-permute-start | bytes 196616 | tf_op jit(solution)/shard_map/ppermute | solution.py:409
  173.2 6.5 %collective-permute-start.11 = (f32[64,256]{1,0:T(8,128)S(1)}, f32[64,256]{1,0:T(8,128)S(1)}, u32[]{:S(2)}, u32[]{:S(2)}) collective-permute-start(f32[64,256]{1,0:T(8,128)S(1)} %copy-done.9), channel_id=1, source_target_pairs={{0,1},{1,2},{2,3},{3,0},{4,5},{5,6},{6,7},{7,4},{8,9},{9,10},{10,1... | collective-permute-start | bytes 196616 | tf_op jit(solution)/shard_map/ppermute | solution.py:409
  175.7 6.5 %copy-start.10 = (f32[64,256]{1,0:T(8,128)}, f32[64,256]{1,0:T(8,128)S(1)}, u32[]{:S(2)}) copy-start(f32[64,256]{1,0:T(8,128)S(1)} %collective-permute-done.13.refs_3_) | copy-start | bytes 196612
  177.5 4.7 %copy-start.11 = (f32[64,256]{1,0:T(8,128)}, f32[64,256]{1,0:T(8,128)S(1)}, u32[]{:S(2)}) copy-start(f32[64,256]{1,0:T(8,128)S(1)} %collective-permute-done.12.refs_2_) | copy-start | bytes 196612
  179.7 2.5 %copy-start.12 = (f32[64,256]{1,0:T(8,128)}, f32[64,256]{1,0:T(8,128)S(1)}, u32[]{:S(2)}) copy-start(f32[64,256]{1,0:T(8,128)S(1)} %collective-permute-done.11.refs_1_) | copy-start | bytes 196612
  182.2 0.8 copy-start

commit v3 on v2

--- a/solution.py
+++ b/solution.py
@@ -87,7 +87,7 @@
     return (lax.axis_index("z") * dims[1] + lax.axis_index("y")) * dims[2] + lax.axis_index("k")
 
 
-def call(kernel, out_shape, in_specs, scratch=(), flops=0):
+def call(kernel, out_shape, in_specs, scratch=(), flops=0, limit=16 << 20):
     vmem = pl.BlockSpec(memory_space=pltpu.VMEM)
     single = not isinstance(out_shape, (tuple, list))
     return pl.pallas_call(
@@ -97,6 +97,7 @@
         out_specs=vmem if single else [vmem] * len(out_shape),
         scratch_shapes=list(scratch),
         cost_estimate=pl.CostEstimate(flops=flops, bytes_accessed=1 << 19, transcendentals=0),
+        compiler_params=pltpu.CompilerParams(vmem_limit_bytes=limit),
         interpret=INTERPRET,
     )
 
@@ -142,7 +143,7 @@
     info[...] = jnp.broadcast_to(about[None], info.shape)
 
 
-def prep_kernel(dims, cur, weights, offsets, interp, halo, charge):
+def prep_kernel(dims, cur, weights, offsets, interp, skelpos, halo, far):
     group = group_index(dims)
     src = jnp.concatenate([cur[3, 0], cur[3, 1]], axis=0) * weights[...]
     halo[0:32, :] = src
@@ -151,22 +152,13 @@
         cols = slice(PTS * b, PTS * b + PTS)
         halo[32:40, cols] = centred(offsets, b, group)
         charges.append(dot(src[:, cols], interp[b], 1, 1, HIGHEST))
-    charge[...] = jnp.concatenate(charges, axis=1)
+    payload = jnp.concatenate([jnp.concatenate(charges, axis=1), skelpos[...]], axis=0)
+    far[...] = jnp.broadcast_to(payload[None], far.shape)
 
 
 def from_x(r):
     n = lax.axis_size("x")
     return lax.rem(lax.axis_index("x") + n - r, n)
-
-
-def pack_kernel(skelpos, *refs):
-    charges, far = refs[:-1], refs[-1]
-    n = 32 * len(charges)
-    for r, ref in enumerate(charges):
-        at = pl.multiple_of(32 * from_x(r), 32)
-        far[0, pl.ds(at, 32), :] = ref[...]
-    far[0, n : n + 8, :] = skelpos[...]
-    far[1:] = jnp.broadcast_to(far[0][None], (far.shape[0] - 1,) + far.shape[1:])
 
 
 def near_kernel(dims, near, count, prev, own, nxt, cur, *refs):
@@ -220,7 +212,16 @@
         acc[t] += 0.5 * jnp.concatenate([cur[3, 0, :, cols], cur[3, 1, :, cols]], axis=0)
     n = len(outs)
     for r, out in enumerate(outs):
-        out[...] = acc[lax.rem(lax.axis_index("x") + r, n)]
+        block = acc[lax.rem(lax.axis_index("x") + r, n)]
+        if r == 0:
+            out[...] = block
+            continue
+        for k in range(4):
+            for p in range(2):
+                out[32 * k + 16 * p : 32 * k + 16 * p + 16, :] = cur[k, p]
+        out[PTS : PTS + 8, :] = jnp.concatenate(
+            [block[8 * g : 8 * g + 8] for g in range(4)], axis=1
+        )
 
 
 def far_kernel(dims, info, gathered, out, tpos, rhi, rlo, weight, acc):
@@ -238,7 +239,7 @@
                 turned[0:SKEL, 8 * d + c : 8 * d + c + 1], (SKEL, PTS)
             )
     for g in range(nz):
-        rows = gathered[g, 0 : 32 * nx, :]
+        rows = jnp.concatenate([gathered[nx * g + c, 0:32, :] for c in range(nx)], axis=0)
         hi, lo = split(jnp.concatenate([rows, rotate(rows)], axis=1))
         rhi[g] = hi
         rlo[g] = lo
@@ -246,9 +247,9 @@
     per = min(4, targets)
 
     def step(g, carry):
-        sx = gathered[g, 32 * nx + 0 : 32 * nx + 1, :]
-        sy = gathered[g, 32 * nx + 1 : 32 * nx + 2, :]
-        sz = gathered[g, 32 * nx + 2 : 32 * nx + 3, :]
+        sx = gathered[nx * g, 32:33, :]
+        sy = gathered[nx * g, 33:34, :]
+        sz = gathered[nx * g, 34:35, :]
         source_group = g * targets + mine
         for d in range(targets):
             delta = source_group - (first + d)
@@ -286,35 +287,46 @@
     return jnp.concatenate([re, im], axis=1)
 
 
-def basis_kernel(scale, *refs):
-    parts, (ordered, pieces) = refs[:-2], refs[-2:]
-    nx = len(parts)
-    for r, ref in enumerate(parts):
+def basis_kernel(scale, first, basis, *refs):
+    others, (ordered, nears, blocks) = refs[:-3], refs[-3:]
+    nx = 1 + len(others)
+    for r, ref in enumerate((basis,) + others):
         c = from_x(r)
         for k in range(4):
             at = pl.ds(pl.multiple_of(16 * (nx * k + c), 16), 16)
             for p in range(2):
                 ordered[p, at, :] = ref[32 * k + 16 * p : 32 * k + 16 * p + 16, :]
-    cols = pl.ds(pl.multiple_of(PTS * lax.axis_index("x"), PTS), PTS)
-    b2 = jnp.concatenate([ordered[0, :, cols], ordered[1, :, cols]], axis=1)
-    gram = dot(b2, b2, 1, 1, HIGHEST) * scale
-    n = pieces.shape[0]
-    per = 256 // n
-    for e in range(per):
-        pieces[:, e, :] = gram[n * e : n * e + n, 0:PTS]
-        pieces[:, per + e, :] = gram[n * e : n * e + n, PTS : 2 * PTS]
-
-
-def couple_kernel(scale, phi, interp, ordered, gsum, *refs):
-    nears, (applied, part, held) = refs[:-3], refs[-3:]
-    nx = len(nears)
-    for r, ref in enumerate(nears):
-        held[from_x(r)] = ref[...]
+        block = first[...] if r == 0 else ref[PTS : PTS + 8, :]
+        if r > 0:
+            block = jnp.concatenate(
+                [block[:, PTS * g : PTS * g + PTS] for g in range(4)], axis=0
+            )
+        nears[pl.ds(pl.multiple_of(32 * c, 32), 32), :] = block
+    x = lax.axis_index("x")
+    half = lax.rem(x, 2)
+
+    def product(left, right, rows):
+        total = None
+        for p in range(2):
+            a = ordered[p, pl.ds(pl.multiple_of(64 * left, 64), 64), :]
+            b = ordered[p, pl.ds(pl.multiple_of(right, 32), rows), :]
+            part = dot(a, b, 1, 1, HIGHEST)
+            total = part if total is None else total + part
+        return total * scale
+
+    blocks[0:64, :] = jnp.concatenate(
+        [product(x, 64 * x, 64), product(x, 64 * lax.rem(x + 1, nx), 64)], axis=1
+    )
+    far = product(half, 64 * (half + 2) + 32 * (x // 2), 32)
+    blocks[64:80, :] = jnp.concatenate([far[16 * g : 16 * g + 16] for g in range(4)], axis=1)
+
+
+def couple_kernel(scale, phi, interp, ordered, nears, blocks, applied, part):
+    nx = nears.shape[0] // 32
     total = phi[0]
     for d in range(1, phi.shape[0]):
         total = total + phi[d]
-    rows = dot(total, interp[lax.axis_index("x")], 0, 0, HIGHEST)
-    rows = rows + jnp.concatenate([held[c] for c in range(nx)], axis=0)
+    rows = dot(total, interp[lax.axis_index("x")], 0, 0, HIGHEST) + nears[...]
     a2 = halves(rows, nx)
     applied[...] = a2
     cols = pl.ds(pl.multiple_of(PTS * lax.axis_index("x"), PTS), PTS)
@@ -322,59 +334,53 @@
     c = dot(b2, a2, 1, 1, HIGHEST) * scale
     packed = jnp.concatenate([c[0:128], c[128:256]], axis=1)
     own = dot(a2, a2, 1, 1, HIGHEST) * scale
-    own = jnp.concatenate([own[0:32], own[32:64]], axis=1)
-    g = gsum[0]
-    for d in range(1, gsum.shape[0]):
-        g = g + gsum[d]
     n = part.shape[0]
-    a, b, w = 128 // n, 32 // n, g.shape[0] // n
+    lead = 128 // n
     for d in range(n):
-        part[d] = jnp.concatenate(
-            [
-                packed[a * d : a * d + a],
-                own[b * d : b * d + b],
-                g[w * d : w * d + w],
-                jnp.zeros((part.shape[1] - a - b - w, PTS), F32),
-            ],
-            axis=0,
-        )
-
-
-def first_sum_kernel(part, out):
-    total = part[0]
-    for d in range(1, part.shape[0]):
-        total = total + part[d]
-    out[...] = jnp.broadcast_to(total[None], out.shape)
-
-
-def second_sum_kernel(rows, width, part, out):
-    n = part.shape[0]
-    total = part[0]
-    for d in range(1, n):
-        total = total + part[d]
-    out[:, 0 : part.shape[1], :] = jnp.broadcast_to(
-        total[None], (out.shape[0],) + total.shape
-    )
-    g = [part[:, rows + e, :] for e in range(width)]
-    g = jnp.concatenate(g, axis=0)
-    out[:, part.shape[1] :, :] = jnp.broadcast_to(g[None], (out.shape[0],) + g.shape)
-
-
-def finish_kernel(width, summed, ordered, *refs):
+        part[d, 0:lead, :] = packed[lead * d : lead * d + lead]
+    rest = jnp.concatenate(
+        [
+            jnp.concatenate([own[0:32], own[32:64]], axis=1),
+            blocks[...],
+            jnp.zeros((16, PTS), F32),
+        ],
+        axis=0,
+    )
+    for e in range(part.shape[1] - lead):
+        part[:, lead + e, :] = rest[n * e : n * e + n]
+
+
+def finish_kernel(nx, summed, ordered, *refs):
     applied, (out, coupling, factor, inv) = refs[:-4], refs[-4:]
     n = summed.shape[0]
-    a, b = 128 // n, 32 // n
-    packed = jnp.concatenate([summed[d, 0:a, :] for d in range(n)], axis=0)
+    lead = 128 // n
+    tail = 128 // n
+    packed = jnp.concatenate([summed[d, 0:lead, :] for d in range(n)], axis=0)
     c = jnp.concatenate([packed[:, 0:64], packed[:, 64:128]], axis=0)
     for k in range(4):
         coupling[k] = c[64 * k : 64 * k + 64]
-    both = jnp.concatenate([summed[d, a : a + b, :] for d in range(n)], axis=0)
-    g = jnp.concatenate([both[:, 0:64], both[:, 64:128]], axis=0)
-    base = summed.shape[1] - width
-    lines = jnp.concatenate([summed[d, base:, :] for d in range(n)], axis=0)
-    bb = jnp.concatenate([lines[0:256], lines[256:512]], axis=1)
-    gc = dot(bb, c, 1, 0, HIGHEST) - 2.0 * c
-    g = g + dot(c, gc, 0, 0, HIGHEST)
+    own = None
+    de, h = [], []
+    for x in range(nx):
+        rest = [summed[:, lead + tail * x + e, :] for e in range(112 // n)]
+        rest = jnp.concatenate(rest, axis=0)
+        own = rest[0:32] if own is None else own + rest[0:32]
+        de.append(rest[32:96])
+        h.append(
+            jnp.concatenate([rest[96:112, 32 * g : 32 * g + 32] for g in range(4)], axis=0)
+        )
+    g = jnp.concatenate([own[:, 0:64], own[:, 64:128]], axis=0)
+    blocks = [c[64 * k : 64 * k + 64] for k in range(4)]
+    lines = []
+    for k in range(4):
+        right = jnp.concatenate([0.5 * blocks[k], blocks[(k + 1) % 4]], axis=0)
+        left = de[k]
+        if k < 2:
+            right = jnp.concatenate([right, blocks[k + 2]], axis=0)
+            left = jnp.concatenate([left, h[k], h[k + 2]], axis=1)
+        lines.append(dot(left, right, 1, 0, HIGHEST) - blocks[k])
+    halfq = dot(c, jnp.concatenate(lines, axis=0), 0, 0, HIGHEST)
+    g = g + (halfq + halfq.T)
     row = lax.broadcasted_iota(jnp.int32, (64, 64), 0)
     col = lax.broadcasted_iota(jnp.int32, (64, 64), 1)
     eye = row == col
@@ -383,13 +389,18 @@
     g = g + jnp.where(eye, SHIFT_SCALE * trace / 64.0 + EPSILON, 0.0)
     m = jnp.concatenate([g, eye.astype(F32)], axis=1)
     sub = lax.broadcasted_iota(jnp.int32, (64, 1), 0)
-    for j in range(63):
-        line = m[j : j + 1, :]
-        f = jnp.where(sub > j, m[:, j : j + 1] / line[:, j : j + 1], 0.0)
-        m = m - f * line
+    for j in range(0, 64, 2):
+        one = m[j : j + 1, :]
+        two = m[j + 1 : j + 2, :]
+        p = 1.0 / one[:, j : j + 1]
+        f1 = m[:, j : j + 1] * p
+        two = two - (two[:, j : j + 1] * p) * one
+        f2 = (m[:, j + 1 : j + 2] - f1 * one[:, j + 1 : j + 2]) / two[:, j + 1 : j + 2]
+        f1 = jnp.where(sub > j, f1, 0.0)
+        f2 = jnp.where(sub > j + 1, f2, 0.0)
+        m = m - f1 * one - f2 * two
     pivots = jnp.sum(jnp.where(eye, m[:, 0:64], 0.0), axis=1, keepdims=True)
-    root = 1.0 / jnp.sqrt(pivots)
-    m = m * root
+    m = m * (1.0 / jnp.sqrt(pivots))
     factor[...] = jnp.where(row <= col, m[:, 0:64], 0.0)
     inv[...] = m[:, 64:128]
     mine = inv[pl.ds(pl.multiple_of(16 * lax.axis_index("x"), 16), 16), :]
@@ -429,19 +440,18 @@
         [SMEM, SMEM, VMEM, VMEM],
     )(near_boxes, near_count, offsets, skeleton)
     info_all = trade(info, YK)
-    halo, charge = call(
-        functools.partial(prep_kernel, dims), (shape(40, points), shape(32, PTS)), [VMEM] * 4
-    )(basis, weights[None], offsets, interp)
-    charges = around([charge] * nx)
-    far = call(pack_kernel, shape(nz, 32 * nx + 8, PTS), [VMEM] * (1 + nx))(skelpos, *charges)
-    far_all = trade(far, "z")
+    halo, far = call(
+        functools.partial(prep_kernel, dims),
+        (shape(40, points), shape(sources, 40, PTS)),
+        [VMEM] * 5,
+    )(basis, weights[None], offsets, interp, skelpos)
     prev = lax.ppermute(halo, BOX, [(g, g + 1) for g in range(groups - 1)])
     nxt = lax.ppermute(halo, BOX, [(g + 1, g) for g in range(groups - 1)])
-    bases = around([basis.reshape(4 * 32, points)] * nx)
+    far_all = trade(far, ZX)
 
     nears = call(
         functools.partial(near_kernel, dims),
-        (shape(32, PTS),) * nx,
+        (shape(32, PTS),) + (shape(PTS + 8, points),) * (nx - 1),
         [SMEM, SMEM] + [VMEM] * 4,
         [
             pltpu.VMEM((3 * BOX_DEV, 40, PTS), F32),
@@ -452,12 +462,11 @@
         flops=36 * 2 * 64 * 256 * 128 * 2,
     )(near_boxes, near_count, prev, halo, nxt, basis)
     nears = around(nears)
-    ordered, pieces = call(
+    ordered, near_rows, blocks = call(
         functools.partial(basis_kernel, scale),
-        (shape(2, 256, points), shape(sources, 512 // sources, PTS)),
-        [VMEM] * nx,
-    )(*bases)
-    gsum = trade(pieces, ZX)
+        (shape(2, 256, points), shape(32 * nx, PTS), shape(80, PTS)),
+        [VMEM] * (1 + nx),
+    )(nears[0], basis.reshape(4 * 32, points), *nears[1:])
 
     far_part = call(
         functools.partial(far_kernel, dims),
@@ -474,28 +483,25 @@
     )(info_all, far_all)
     phi = trade(far_part, YK)
 
-    used = 128 // targets + 32 // targets
-    width = 512 // sources // targets
-    tall = -(-(used + width) // 8) * 8
+    lead = 128 // targets
+    tall = 2 * lead
     applied, part = call(
         functools.partial(couple_kernel, scale),
         (shape(64, 2 * PTS), shape(targets, tall, PTS)),
-        [VMEM] * (4 + nx),
-        [pltpu.VMEM((nx, 32, PTS), F32)],
-    )(phi, interp, ordered, gsum, *nears)
-    part = trade(part, YK)
+        [VMEM] * 5,
+    )(phi, interp, ordered, near_rows, blocks)
+    part = jnp.sum(trade(part, YK), axis=0)
     applied = around([applied] * nx)
-    part = call(first_sum_kernel, shape(sources, tall, PTS), [VMEM])(part)
-    part = trade(part, ZX)
-    part = call(
-        functools.partial(second_sum_kernel, used, width),
-        shape(targets, tall + width * sources, PTS),
-        [VMEM],
-    )(part)
-    summed = trade(part, YK)
+    part = trade(jnp.broadcast_to(part[None], (sources, tall, PTS)), ZX)
+    part = jnp.sum(part.reshape(nz, nx, tall, PTS), axis=0)
+    part = jnp.concatenate(
+        [jnp.sum(part[:, :lead], axis=0), part[:, lead:].reshape(nx * (tall - lead), PTS)],
+        axis=0,
+    )
+    summed = trade(jnp.broadcast_to(part[None], (targets,) + part.shape), YK)
 
     new_block, coupling, factor = call(
-        functools.partial(finish_kernel, width * sources),
+        functools.partial(finish_kernel, nx),
         (shape(2, 16, points), shape(4, 64, 64), shape(64, 64)),
         [VMEM] * (2 + nx),
         [pltpu.VMEM((64, 64), F32)],

time: 194 us -> 165 us (0.85)
  starting transfers between devices: 80.9 us -> 44.6 us
  blocking collectives: 37.9 us -> 65.6 us
  Pallas kernels: 38.6 us -> 26.1 us
  waiting for transfers between devices: 28.6 us -> 21.9 us
    all_to_all x2 -> x3, blocking collectives: 37.9 us -> 65.6 us  [trade(): return lax.all_to_all(value, axes, split_axis=0, concat_axis=0, tiled=True)]
    all_to_all x5 -> x3, starting transfers between devices: 42.9 us -> 21.2 us  [trade(): return lax.all_to_all(value, axes, split_axis=0, concat_axis=0, tiled=True)]
    ppermute x12 -> x6, starting transfers between devices: 32.4 us -> 17.8 us  [around(): lax.ppermute(blocks[r], 'x', [(i, (i + r) % n) for i in range(n)])]
    ppermute x12 -> x6, waiting for transfers between devices: 19.5 us -> 10.9 us  [around(): lax.ppermute(blocks[r], 'x', [(i, (i + r) % n) for i in range(n)])]
    pallas_call x6 -> x3, Pallas kernels: 24 us -> 16.3 us  [the longest x1 9.25 us: shards(): call(functools.partial(finish_kernel, nx), (shape(2, 16, points), shape(4...]
    pallas_call x1, Pallas kernels: 2.94 us -> 0.84 us  [shards(): call(functools.partial(couple_kernel, scale), (shape(64, 2 * PTS), shape(...]
    all_to_all x5 -> x3, waiting for transfers between devices: 5.35 us -> 7.31 us  [trade(): return lax.all_to_all(value, axes, split_axis=0, concat_axis=0, tiled=True)]
    unnamed x44 -> x22, local copies, waits for them, and re-layouts: 5.37 us -> 4.33 us
  transfers between devices with their start and end apart: 19 -> 11, of which waited for: 10 -> 8; matrix products, arithmetic and copies ran while one was open for 0% -> 0% of each run, Pallas kernels for 11% -> 5%
where the time goes in v3:
time: 165 us; the launch traced here: 164 us
  blocking collectives  65.6 us (40%)
  starting transfers between devices  44.6 us (27%)
  Pallas kernels  26.1 us (16%)
  waiting for transfers between devices  21.9 us (13%)
  local copies, waits for them, and re-layouts  5.1 us (3%)
    all_to_all x3, blocking collectives, trade(): return lax.all_to_all(value, axes, split_axis=0, concat_axis=0, tiled=True)  65.6 us
    all_to_all x3, starting transfers between devices, trade(): return lax.all_to_all(value, axes, split_axis=0, concat_axis=0, tiled=True)  21.2 us
    ppermute x6, starting transfers between devices, around(): lax.ppermute(blocks[r], 'x', [(i, (i + r) % n) for i in range(n)])  17.8 us
    ppermute x6, waiting for transfers between devices, around(): lax.ppermute(blocks[r], 'x', [(i, (i + r) % n) for i in range(n)])  10.9 us
    pallas_call x1, Pallas kernels, shards(): call(functools.partial(finish_kernel, nx), (shape(2, 16, points), shape(4...  9.25 us
    all_to_all x3, waiting for transfers between devices, trade(): return lax.all_to_all(value, axes, split_axis=0, concat_axis=0, tiled=True)  7.31 us
    pallas_call x1, Pallas kernels, shards(): call(functools.partial(near_kernel, dims), (shape(32, PTS),) + (shape(PTS...  6.71 us
    pallas_call x1, Pallas kernels, shards(): call(functools.partial(far_kernel, dims), shape(targets, SKEL, 32 * nx),...  6.47 us
  transfers between devices with their start and end apart: 11, of which 8 were waited for; matrix products, arithmetic and copies ran while one was open for 0% of the time, Pallas kernels for 5%

profile of v3, /device:TPU:1, one launch (start us, length us, event | category | flops | bytes accessed | tf_op | source)
XLA Modules:
  0.0 164.1 jit_solution(5269839572669915845)
XLA Ops:
  0.6 0.0 copy-start.3
  0.6 0.7 copy-done.3
  1.3 0.0 copy-start.6
  1.3 0.7 copy-done.6
  2.0 0.0 copy-start.7
  2.0 0.7 copy-done.7
  2.7 0.0 copy-start.9
  2.7 0.7 copy-done.9
  3.4 1.5 shard_map.94
  4.9 10.3 %all-to-all-start = ((f32[16,8,128]{2,1,0:T(8,128)}), f32[16,8,128]{2,1,0:T(8,128)S(1)}, u32[]{:S(2)}, u32[]{:S(2)}) async-start(f32[16,8,128]{2,1,0:T(8,128)} %get-tuple-element.16), calls=%async_computation | async-start | bytes 131072 | tf_op jit(solution)/shard_map/all_to_all | solution.py:425
  15.2 0.0 copy-done.2
  15.2 0.0 copy-done.4
  15.2 0.7 copy-done.5
  15.8 0.9 copy-done
  16.8 0.3 shard_map.95
  17.1 5.9 %all-to-all-done.info = f32[16,8,128]{2,1,0:T(8,128)S(1)} async-done(((f32[16,8,128]{2,1,0:T(8,128)}), f32[16,8,128]{2,1,0:T(8,128)S(1)}, u32[]{:S(2)}, u32[]{:S(2)}) %all-to-all-start) | async-done | bytes 65568 | tf_op jit(solution)/shard_map/all_to_all | solution.py:425
  23.0 30.1 %all_to_all.30.gathered = f32[32,40,128]{2,1,0:T(8,128)S(1)} all-to-all(f32[32,40,128]{2,1,0:T(8,128)S(1)} %get-tuple-element.18), channel_id=1, replica_groups=mesh['z'=8,'y'=8,'k'=2,'x'=4] {'z','x'}, dimensions={0} | all-to-all | bytes 1310720 | tf_op jit(solution)/shard_map/all_to_all | solution.py:425
  53.1 6.5 %shard_map.96 = f32[16,32,128]{2,1,0:T(8,128)} custom-call(f32[16,8,128]{2,1,0:T(8,128)S(1)} %all-to-all-done.info, f32[32,40,128]{2,1,0:T(8,128)S(1)} %all_to_all.30.gathered), custom_call_target="tpu_custom_call" | custom-call | flops 805306368 | bytes 524288 | tf_op jit(solution)/shard_map/pallas_call | solution.py:471
  59.5 5.8 %all-to-all-start.2 = ((f32[16,32,128]{2,1,0:T(8,128)}), f32[16,32,128]{2,1,0:T(8,128)S(1)}, u32[]{:S(2)}, u32[]{:S(2)}) async-start(f32[16,32,128]{2,1,0:T(8,128)} %shard_map.96), calls=%async_computation.2 | async-start | bytes 524288 | tf_op jit(solution)/shard_map/all_to_all | solution.py:425
  65.4 2.1 %collective-permute-start.1 = (f32[40,512]{1,0:T(8,128)S(1)}, f32[40,512]{1,0:T(8,128)S(1)}, u32[]{:S(2)}, u32[]{:S(2)}) collective-permute-start(f32[40,512]{1,0:T(8,128)S(1)} %get-tuple-element.19.own), channel_id=1, source_target_pairs={{4,0},{8,4},{12,8},{16,12},{20,16},{24,20},{28,24},{32,28},{36,32}... | collective-permute-start | bytes 245768 | tf_op jit(solution)/shard_map/ppermute | solution.py:449
  67.5 3.4 %collective-permute-start = (f32[40,512]{1,0:T(8,128)S(1)}, f32[40,512]{1,0:T(8,128)S(1)}, u32[]{:S(2)}, u32[]{:S(2)}) collective-permute-start(f32[40,512]{1,0:T(8,128)S(1)} %get-tuple-element.19.own), channel_id=1, source_target_pairs={{0,4},{4,8},{8,12},{12,16},{16,20},{20,24},{24,28},{28,32},{32,36}... | collective-permute-start | bytes 245768 | tf_op jit(solution)/shard_map/ppermute | solution.py:448
  70.9 3.7 %collective-permute-done.1.nxt = f32[40,512]{1,0:T(8,128)S(1)} collective-permute-done((f32[40,512]{1,0:T(8,128)S(1)}, f32[40,512]{1,0:T(8,128)S(1)}, u32[]{:S(2)}, u32[]{:S(2)}) %collective-permute-start.1) | collective-permute-done | bytes 81952 | tf_op jit(solution)/shard_map/ppermute | solution.py:449
  74.7 0.0 collective-permute-done.prev
  74.7 0.0 copy-done.1
  74.7 0.0 copy-done.8
  74.7 0.0 copy-done.10
  74.7 6.7 %shard_map.97 = (f32[32,128]{1,0:T(8,128)S(1)}, f32[136,512]{1,0:T(8,128)S(1)}, f32[136,512]{1,0:T(8,128)S(1)}, f32[136,512]{1,0:T(8,128)S(1)}) custom-call(s32[4,27]{1,0:T(4,128)S(1)} %copy-done.8, s32[4]{0:T(128)S(1)} %copy-done.10, f32[40,512]{1,0:T(8,128)S(1)} %collective-permute-done.prev, f32[40,512]{1,0:T(8,128)S(1)} %get-tuple-element.19.own, ...), custom_call_target="tpu_custom_call" | custom-call | flops 301989888 | bytes 524288 | tf_op jit(solution)/shard_map/pallas_call | solution.py:452
  81.4 2.7 %collective-permute-start.2 = (f32[136,512]{1,0:T(8,128)S(1)}, f32[136,512]{1,0:T(8,128)S(1)}, u32[]{:S(2)}, u32[]{:S(2)}) collective-permute-start(f32[136,512]{1,0:T(8,128)S(1)} %get-tuple-element.21), channel_id=1, source_target_pairs={{0,1},{1,2},{2,3},{3,0},{4,5},{5,6},{6,7},{7,4},{8,9},{9,10},{10,1... | collective-permute-start | bytes 835592 | tf_op jit(solution)/shard_map/ppermute | solution.py:420
  84.1 4.3 %collective-permute-start.3 = (f32[136,512]{1,0:T(8,128)S(1)}, f32[136,512]{1,0:T(8,128)S(1)}, u32[]{:S(2)}, u32[]{:S(2)}) collective-permute-start(f32[136,512]{1,0:T(8,128)S(1)} %get-tuple-element.22), channel_id=1, source_target_pairs={{0,2},{1,3},{2,0},{3,1},{4,6},{5,7},{6,4},{7,5},{8,10},{9,11},{10,... | collective-permute-start | bytes 835592 | tf_op jit(solution)/shard_map/ppermute | solution.py:420
  88.4 3.1 %collective-permute-start.4 = (f32[136,512]{1,0:T(8,128)S(1)}, f32[136,512]{1,0:T(8,128)S(1)}, u32[]{:S(2)}, u32[]{:S(2)}) collective-permute-start(f32[136,512]{1,0:T(8,128)S(1)} %get-tuple-element.23), channel_id=1, source_target_pairs={{0,3},{1,0},{2,1},{3,2},{4,7},{5,4},{6,5},{7,6},{8,11},{9,8},{10,9... | collective-permute-start | bytes 835592 | tf_op jit(solution)/shard_map/ppermute | solution.py:420
  91.5 1.4 collective-permute-done.2.refs_0_
  92.9 3.0 %collective-permute-done.3.refs_1_ = f32[136,512]{1,0:T(8,128)S(1)} collective-permute-done((f32[136,512]{1,0:T(8,128)S(1)}, f32[136,512]{1,0:T(8,128)S(1)}, u32[]{:S(2)}, u32[]{:S(2)}) %collective-permute-start.3) | collective-permute-done | bytes 278560 | tf_op jit(solution)/shard_map/ppermute | solution.py:420
  95.9 2.4 %collective-permute-done.4.refs_2_ = f32[136,512]{1,0:T(8,128)S(1)} collective-permute-done((f32[136,512]{1,0:T(8,128)S(1)}, f32[136,512]{1,0:T(8,128)S(1)}, u32[]{:S(2)}, u32[]{:S(2)}) %collective-permute-start.4) | collective-permute-done | bytes 278560 | tf_op jit(solution)/shard_map/ppermute | solution.py:420
  98.4 0.9 shard_map.98
  99.3 0.0 all-to-all-done.2.phi
  99.3 0.8 shard_map.99
  100.2 17.9 %all_to_all.31 = f32[16,16,128]{2,1,0:T(8,128)S(1)} all-to-all(f32[16,16,128]{2,1,0:T(8,128)S(1)} %get-tuple-element.27), channel_id=1, replica_groups=mesh['z'=8,'y'=8,'k'=2,'x'=4] {'y','k'}, dimensions={0} | all-to-all | bytes 262144 | tf_op jit(solution)/shard_map/all_to_all | solution.py:425
  118.1 17.6 %all_to_all.32 = f32[32,16,128]{2,1,0:T(8,128)S(1)} all-to-all(f32[32,16,128]{2,1,0:T(8,128)S(1)} %broadcast_in_dim.7), channel_id=1, replica_groups=mesh['z'=8,'y'=8,'k'=2,'x'=4] {'z','x'}, dimensions={0} | all-to-all | bytes 524288 | tf_op jit(solution)/shard_map/all_to_all | solution.py:425
  135.7 0.7 broadcast_in_dim.8
  136.5 5.1 %all-to-all-start.5 = ((f32[16,40,128]{2,1,0:T(8,128)}), f32[16,40,128]{2,1,0:T(8,128)S(1)}, u32[]{:S(2)}, u32[]{:S(2)}) async-start(f32[16,40,128]{2,1,0:T(8,128)} %broadcast_in_dim.8), calls=%async_computation.5 | async-start | bytes 655360 | tf_op jit(solution)/shard_map/all_to_all | solution.py:425
  141.6 2.8 %collective-permute-start.7 = (f32[64,256]{1,0:T(8,128)S(1)}, f32[64,256]{1,0:T(8,128)S(1)}, u32[]{:S(2)}, u32[]{:S(2)}) collective-permute-start(f32[64,256]{1,0:T(8,128)S(1)} %get-tuple-element.28.refs_0_), channel_id=1, source_target_pairs={{0,3},{1,0},{2,1},{3,2},{4,7},{5,4},{6,5},{7,6},{8,11},{9,8},{10,9... | collective-permute-start | bytes 196616 | tf_op jit(solution)/shard_map/ppermute | solution.py:420
  144.4 2.5 %collective-permute-start.6 = (f32[64,256]{1,0:T(8,128)S(1)}, f32[64,256]{1,0:T(8,128)S(1)}, u32[]{:S(2)}, u32[]{:S(2)}) collective-permute-start(f32[64,256]{1,0:T(8,128)S(1)} %get-tuple-element.28.refs_0_), channel_id=1, source_target_pairs={{0,2},{1,3},{2,0},{3,1},{4,6},{5,7},{6,4},{7,5},{8,10},{9,11},{10,... | collective-permute-start | bytes 196616 | tf_op jit(solution)/shard_map/ppermute | solution.py:420
  146.9 2.5 %collective-permute-start.5 = (f32[64,256]{1,0:T(8,128)S(1)}, f32[64,256]{1,0:T(8,128)S(1)}, u32[]{:S(2)}, u32[]{:S(2)}) collective-permute-start(f32[64,256]{1,0:T(8,128)S(1)} %get-tuple-element.28.refs_0_), channel_id=1, source_target_pairs={{0,1},{1,2},{2,3},{3,0},{4,5},{5,6},{6,7},{7,4},{8,9},{9,10},{10,1... | collective-permute-start | bytes 196616 | tf_op jit(solution)/shard_map/ppermute | solution.py:420
  149.4 0.0 collective-permute-done.7.refs_3_
  149.4 1.8 %collective-permute-done.6.refs_2_ = f32[64,256]{1,0:T(8,128)S(1)} collective-permute-done((f32[64,256]{1,0:T(8,128)S(1)}, f32[64,256]{1,0:T(8,128)S(1)}, u32[]{:S(2)}, u32[]{:S(2)}) %collective-permute-start.6) | collective-permute-done | bytes 65568 | tf_op jit(solution)/shard_map/ppermute | solution.py:420
  151.2 2.2 %collective-permute-done.5.refs_1_ = f32[64,256]{1,0:T(8,128)S(1)} collective-permute-done((f32[64,256]{1,0:T(8,128)S(1)}, f32[64,256]{1,0:T(8,128)S(1)}, u32[]{:S(2)}, u32[]{:S(2)}) %collective-permute-start.5) | collective-permute-done | bytes 65568 | tf_op jit(solution)/shard_map/ppermute | solution.py:420
  153.4 1.5 all-to-all-done.5.summed
  154.8 9.3 %shard_map.100 = (f32[2,16,512]{2,1,0:T(8,128)}, f32[4,64,64]{2,1,0:T(8,128)}, f32[64,64]{1,0:T(8,128)}) custom-call(f32[16,40,128]{2,1,0:T(8,128)S(1)} %all-to-all-done.5.summed, f32[2,256,512]{2,1,0:T(8,128)S(1)} %get-tuple-element.24.ordered, f32[64,256]{1,0:T(8,128)S(1)} %get-tuple-element.28.refs_0_, f32[64,256]{1,0:T(8,128)S(1)} %collective-permute-done.5.refs_1_, ...), custom_call_target="tpu_custom_call" | custom-call | bytes 524288 | tf_op jit(solution)/shard_map/pallas_call | solution.py:503
  (12 shorter events, 0.1 us)
Async XLA Ops:
  0.6 0.7 copy-start.3
  1.3 0.7 copy-start.6
  2.0 0.7 copy-start.7
  2.7 0.7 copy-start.9
  4.9 10.3 %copy-start.2 = (f32[4,32,128]{2,1,0:T(8,128)S(1)}, f32[4,32,128]{2,1,0:T(8,128)}, u32[]{:S(2)}) copy-start(f32[4,32,128]{2,1,0:T(8,128)} %interp.3) | copy-start | bytes 196612
  4.9 10.3 %copy-start.4 = (f32[3,512]{1,0:T(4,128)S(1)}, f32[3,512]{1,0:T(4,128)}, u32[]{:S(2)}) copy-start(f32[3,512]{1,0:T(4,128)} %offsets.3) | copy-start | bytes 18436
  4.9 18.1 %all-to-all-start = ((f32[16,8,128]{2,1,0:T(8,128)}), f32[16,8,128]{2,1,0:T(8,128)S(1)}, u32[]{:S(2)}, u32[]{:S(2)}) async-start(f32[16,8,128]{2,1,0:T(8,128)} %get-tuple-element.16), calls=%async_computation | async-start | bytes 131072 | tf_op jit(solution)/shard_map/all_to_all | solution.py:425
  15.1 0.7 copy-start.5
  15.8 0.9 copy-start
  59.5 15.1 %copy-start.1 = (f32[4,2,16,512]{3,2,1,0:T(8,128)S(1)}, f32[4,2,16,512]{3,2,1,0:T(8,128)}, u32[]{:S(2)}) copy-start(f32[4,2,16,512]{3,2,1,0:T(8,128)} %cur.3) | copy-start | bytes 786436
  59.5 15.1 %copy-start.8 = (s32[4,27]{1,0:T(4,128)S(1)}, s32[4,27]{1,0:T(4,128)}, u32[]{:S(2)}) copy-start(s32[4,27]{1,0:T(4,128)} %near.3) | copy-start | bytes 1300
  59.5 39.8 %all-to-all-start.2 = ((f32[16,32,128]{2,1,0:T(8,128)}), f32[16,32,128]{2,1,0:T(8,128)S(1)}, u32[]{:S(2)}, u32[]{:S(2)}) async-start(f32[16,32,128]{2,1,0:T(8,128)} %shard_map.96), calls=%async_computation.2 | async-start | bytes 524288 | tf_op jit(solution)/shard_map/all_to_all | solution.py:425
  65.4 9.3 %copy-start.10 = (s32[4]{0:T(128)S(1)}, s32[4]{0:T(128)}, u32[]{:S(2)}) copy-start(s32[4]{0:T(128)} %count.3) | copy-start | bytes 52
  65.4 9.3 %collective-permute-start.1 = (f32[40,512]{1,0:T(8,128)S(1)}, f32[40,512]{1,0:T(8,128)S(1)}, u32[]{:S(2)}, u32[]{:S(2)}) collective-permute-start(f32[40,512]{1,0:T(8,128)S(1)} %get-tuple-element.19.own), channel_id=1, source_target_pairs={{4,0},{8,4},{12,8},{16,12},{20,16},{24,20},{28,24},{32,28},{36,32}... | collective-permute-start | bytes 245768 | tf_op jit(solution)/shard_map/ppermute | solution.py:449
  67.5 7.2 %collective-permute-start = (f32[40,512]{1,0:T(8,128)S(1)}, f32[40,512]{1,0:T(8,128)S(1)}, u32[]{:S(2)}, u32[]{:S(2)}) collective-permute-start(f32[40,512]{1,0:T(8,128)S(1)} %get-tuple-element.19.own), channel_id=1, source_target_pairs={{0,4},{4,8},{8,12},{12,16},{16,20},{20,24},{24,28},{28,32},{32,36}... | collective-permute-start | bytes 245768 | tf_op jit(solution)/shard_map/ppermute | solution.py:448
  81.4 11.5 %collective-permute-start.2 = (f32[136,512]{1,0:T(8,128)S(1)}, f32[136,512]{1,0:T(8,128)S(1)}, u32[]{:S(2)}, u32[]{:S(2)}) collective-permute-start(f32[136,512]{1,0:T(8,128)S(1)} %get-tuple-element.21), channel_id=1, source_target_pairs={{0,1},{1,2},{2,3},{3,0},{4,5},{5,6},{6,7},{7,4},{8,9},{9,10},{10,1... | collective-permute-start | bytes 835592 | tf_op jit(solution)/shard_map/ppermute | solution.py:420
  84.1 11.9 %collective-permute-start.3 = (f32[136,512]{1,0:T(8,128)S(1)}, f32[136,512]{1,0:T(8,128)S(1)}, u32[]{:S(2)}, u32[]{:S(2)}) collective-permute-start(f32[136,512]{1,0:T(8,128)S(1)} %get-tuple-element.22), channel_id=1, source_target_pairs={{0,2},{1,3},{2,0},{3,1},{4,6},{5,7},{6,4},{7,5},{8,10},{9,11},{10,... | collective-permute-start | bytes 835592 | tf_op jit(solution)/shard_map/ppermute | solution.py:420
  88.4 10.0 %collective-permute-start.4 = (f32[136,512]{1,0:T(8,128)S(1)}, f32[136,512]{1,0:T(8,128)S(1)}, u32[]{:S(2)}, u32[]{:S(2)}) collective-permute-start(f32[136,512]{1,0:T(8,128)S(1)} %get-tuple-element.23), channel_id=1, source_target_pairs={{0,3},{1,0},{2,1},{3,2},{4,7},{5,4},{6,5},{7,6},{8,11},{9,8},{10,9... | collective-permute-start | bytes 835592 | tf_op jit(solution)/shard_map/ppermute | solution.py:420
  136.5 18.4 %all-to-all-start.5 = ((f32[16,40,128]{2,1,0:T(8,128)}), f32[16,40,128]{2,1,0:T(8,128)S(1)}, u32[]{:S(2)}, u32[]{:S(2)}) async-start(f32[16,40,128]{2,1,0:T(8,128)} %broadcast_in_dim.8), calls=%async_computation.5 | async-start | bytes 655360 | tf_op jit(solution)/shard_map/all_to_all | solution.py:425
  141.6 7.8 %collective-permute-start.7 = (f32[64,256]{1,0:T(8,128)S(1)}, f32[64,256]{1,0:T(8,128)S(1)}, u32[]{:S(2)}, u32[]{:S(2)}) collective-permute-start(f32[64,256]{1,0:T(8,128)S(1)} %get-tuple-element.28.refs_0_), channel_id=1, source_target_pairs={{0,3},{1,0},{2,1},{3,2},{4,7},{5,4},{6,5},{7,6},{8,11},{9,8},{10,9... | collective-permute-start | bytes 196616 | tf_op jit(solution)/shard_map/ppermute | solution.py:420
  144.4 6.8 %collective-permute-start.6 = (f32[64,256]{1,0:T(8,128)S(1)}, f32[64,256]{1,0:T(8,128)S(1)}, u32[]{:S(2)}, u32[]{:S(2)}) collective-permute-start(f32[64,256]{1,0:T(8,128)S(1)} %get-tuple-element.28.refs_0_), channel_id=1, source_target_pairs={{0,2},{1,3},{2,0},{3,1},{4,6},{5,7},{6,4},{7,5},{8,10},{9,11},{10,... | collective-permute-start | bytes 196616 | tf_op jit(solution)/shard_map/ppermute | solution.py:420
  146.9 6.5 %collective-permute-start.5 = (f32[64,256]{1,0:T(8,128)S(1)}, f32[64,256]{1,0:T(8,128)S(1)}, u32[]{:S(2)}, u32[]{:S(2)}) collective-permute-start(f32[64,256]{1,0:T(8,128)S(1)} %get-tuple-element.28.refs_0_), channel_id=1, source_target_pairs={{0,1},{1,2},{2,3},{3,0},{4,5},{5,6},{6,7},{7,4},{8,9},{9,10},{10,1... | collective-permute-start | bytes 196616 | tf_op jit(solution)/shard_map/ppermute | solution.py:420

commit v4 on v3

--- a/solution.py
+++ b/solution.py
@@ -224,7 +224,7 @@
         )
 
 
-def far_kernel(dims, info, gathered, out, tpos, rhi, rlo, weight, acc):
+def far_kernel(dims, info, far_z, far_x, out, tpos, rhi, rlo, weight, acc):
     nz, ny, nk, nx = dims
     targets = ny * nk
     mine = lax.axis_index("y") * nk + lax.axis_index("k")
@@ -239,7 +239,7 @@
                 turned[0:SKEL, 8 * d + c : 8 * d + c + 1], (SKEL, PTS)
             )
     for g in range(nz):
-        rows = jnp.concatenate([gathered[nx * g + c, 0:32, :] for c in range(nx)], axis=0)
+        rows = jnp.concatenate([far_x[c, g] for c in range(nx)], axis=0)
         hi, lo = split(jnp.concatenate([rows, rotate(rows)], axis=1))
         rhi[g] = hi
         rlo[g] = lo
@@ -247,9 +247,9 @@
     per = min(4, targets)
 
     def step(g, carry):
-        sx = gathered[nx * g, 32:33, :]
-        sy = gathered[nx * g, 33:34, :]
-        sz = gathered[nx * g, 34:35, :]
+        sx = far_z[g, 32:33, :]
+        sy = far_z[g, 33:34, :]
+        sz = far_z[g, 34:35, :]
         source_group = g * targets + mine
         for d in range(targets):
             delta = source_group - (first + d)
@@ -392,13 +392,18 @@
     for j in range(0, 64, 2):
         one = m[j : j + 1, :]
         two = m[j + 1 : j + 2, :]
-        p = 1.0 / one[:, j : j + 1]
-        f1 = m[:, j : j + 1] * p
-        two = two - (two[:, j : j + 1] * p) * one
-        f2 = (m[:, j + 1 : j + 2] - f1 * one[:, j + 1 : j + 2]) / two[:, j + 1 : j + 2]
+        c1 = jnp.broadcast_to(m[:, j : j + 1], m.shape)
+        c2 = jnp.broadcast_to(m[:, j + 1 : j + 2], m.shape)
+        p1, a = c1[j : j + 1], c1[j + 1 : j + 2]
+        p2 = c2[j + 1 : j + 2]
+        det = p1 * p2 - a * a
+        r1 = 1.0 / p1
+        q = p1 / det
+        lower = a * r1
+        f1 = c1 * r1
+        f2 = jnp.where(sub > j + 1, (c2 - f1 * a) * q, 0.0)
         f1 = jnp.where(sub > j, f1, 0.0)
-        f2 = jnp.where(sub > j + 1, f2, 0.0)
-        m = m - f1 * one - f2 * two
+        m = m - f1 * one - f2 * (two - lower * one)
     pivots = jnp.sum(jnp.where(eye, m[:, 0:64], 0.0), axis=1, keepdims=True)
     m = m * (1.0 / jnp.sqrt(pivots))
     factor[...] = jnp.where(row <= col, m[:, 0:64], 0.0)
@@ -416,9 +421,10 @@
 
 def around(blocks):
     n = lax.axis_size("x")
-    return [blocks[0]] + [
-        lax.ppermute(blocks[r], "x", [(i, (i + r) % n) for i in range(n)]) for r in range(1, n)
-    ]
+    out = [blocks[0]]
+    for r in range(1, n):
+        out.append(lax.ppermute(blocks[r], "x", [(i, (i + r) % n) for i in range(n)]))
+    return out
 
 
 def trade(value, axes):
@@ -438,16 +444,19 @@
         functools.partial(place_kernel, dims),
         (shape(targets, 8, PTS), shape(8, PTS)),
         [SMEM, SMEM, VMEM, VMEM],
+        limit=None,
     )(near_boxes, near_count, offsets, skeleton)
     info_all = trade(info, YK)
     halo, far = call(
         functools.partial(prep_kernel, dims),
-        (shape(40, points), shape(sources, 40, PTS)),
+        (shape(40, points), shape(nz, 40, PTS)),
         [VMEM] * 5,
+        limit=None,
     )(basis, weights[None], offsets, interp, skelpos)
+    far_z = trade(far, "z")
     prev = lax.ppermute(halo, BOX, [(g, g + 1) for g in range(groups - 1)])
     nxt = lax.ppermute(halo, BOX, [(g + 1, g) for g in range(groups - 1)])
-    far_all = trade(far, ZX)
+    far_x = trade(jnp.broadcast_to(far_z[None, :, :32], (nx, nz, 32, PTS)), "x")
 
     nears = call(
         functools.partial(near_kernel, dims),
@@ -471,7 +480,7 @@
     far_part = call(
         functools.partial(far_kernel, dims),
         shape(targets, SKEL, 32 * nx),
-        [VMEM, VMEM],
+        [VMEM] * 3,
         [
             pltpu.VMEM((3, SKEL * targets, PTS), F32),
             pltpu.VMEM((nz, 32 * nx, 2 * PTS), BF16),
@@ -480,7 +489,7 @@
             pltpu.VMEM((SKEL * targets, 32 * nx), F32),
         ],
         flops=3 * 2 * 512 * 2048 * 128,
-    )(info_all, far_all)
+    )(info_all, far_z, far_x)
     phi = trade(far_part, YK)
 
     lead = 128 // targets

time: 165 us -> 160 us (0.970)
  local copies, waits for them, and re-layouts: 5.1 us -> 0.84 us
  waiting for transfers between devices: 21.9 us -> 25.4 us
  starting transfers between devices: 44.6 us -> 41.2 us
    unnamed x22 -> x10, local copies, waits for them, and re-layouts: 4.33 us -> 0.02 us
    pallas_call x1, Pallas kernels: 9.25 us -> 6.55 us  [shards(): call(functools.partial(finish_kernel, nx), (shape(2, 16, points), shape(4...]
    all_to_all x3, waiting for transfers between devices: 7.31 us -> 9.21 us  [trade(): return lax.all_to_all(value, axes, split_axis=0, concat_axis=0, tiled=True)]
    all_to_all x3, starting transfers between devices: 21.2 us -> 19.4 us  [trade(): return lax.all_to_all(value, axes, split_axis=0, concat_axis=0, tiled=True)]
    pallas_call x1, Pallas kernels: 0.32 us -> 1.99 us  [shards(): call(functools.partial(prep_kernel, dims), (shape(40, points), shape(nz,...]
    all_to_all x3 -> x4, blocking collectives: 65.6 us -> 66.1 us  [trade(): return lax.all_to_all(value, axes, split_axis=0, concat_axis=0, tiled=True)]
  transfers between devices with their start and end apart: 11 -> 11, of which waited for: 8 -> 7; matrix products, arithmetic and copies ran while one was open for 0% -> 0% of each run, Pallas kernels for 5% -> 5%
where the time goes in v4:
time: 160 us
  blocking collectives  66.1 us (41%)
  starting transfers between devices  41.2 us (26%)
  waiting for transfers between devices  25.4 us (16%)
  Pallas kernels  25.2 us (16%)
    all_to_all x4, blocking collectives, trade(): return lax.all_to_all(value, axes, split_axis=0, concat_axis=0, tiled=True)  66.1 us
    all_to_all x3, starting transfers between devices, trade(): return lax.all_to_all(value, axes, split_axis=0, concat_axis=0, tiled=True)  19.4 us
    ppermute x6, starting transfers between devices, around(): lax.ppermute(blocks[r], 'x', [(i, (i + r) % n) for i in range(n)])  16.2 us
    ppermute x6, waiting for transfers between devices, around(): lax.ppermute(blocks[r], 'x', [(i, (i + r) % n) for i in range(n)])  12.4 us
    all_to_all x3, waiting for transfers between devices, trade(): return lax.all_to_all(value, axes, split_axis=0, concat_axis=0, tiled=True)  9.21 us
    pallas_call x1, Pallas kernels, shards(): call(functools.partial(near_kernel, dims), (shape(32, PTS),) + (shape(PTS...  6.71 us
    pallas_call x1, Pallas kernels, shards(): call(functools.partial(finish_kernel, nx), (shape(2, 16, points), shape(4...  6.55 us
    pallas_call x1, Pallas kernels, shards(): call(functools.partial(far_kernel, dims), shape(targets, SKEL, 32 * nx),...  6.47 us
  transfers between devices with their start and end apart: 11, of which 7 were waited for; matrix products, arithmetic and copies ran while one was open for 0% of the time, Pallas kernels for 5%

profile of v4, /device:TPU:1, one launch (start us, length us, event | category | flops | bytes accessed | tf_op | source)
XLA Modules:
  0.0 159.6 jit_solution(9269038578654090288)
XLA Ops:
  0.6 1.7 %shard_map.94 = (f32[16,8,128]{2,1,0:T(8,128)}, f32[8,128]{1,0:T(8,128)}) custom-call(s32[4,27]{1,0:T(4,128)} %near.3, s32[4]{0:T(128)} %count.3, f32[3,512]{1,0:T(4,128)} %offsets.3, s32[4,32]{1,0:T(4,128)} %skel.1), custom_call_target="tpu_custom_call" | custom-call | bytes 524288 | tf_op jit(solution)/shard_map/pallas_call | solution.py:443
  2.3 2.0 %shard_map.95 = (f32[40,512]{1,0:T(8,128)}, f32[8,40,128]{2,1,0:T(8,128)}) custom-call(f32[4,2,16,512]{3,2,1,0:T(8,128)} %cur.3, f32[1,512]{1,0:T(1,128)} %bitcast.7, f32[3,512]{1,0:T(4,128)} %offsets.3, f32[4,32,128]{2,1,0:T(8,128)} %interp.3, f32[8,128]{1,0:T(8,128)} %get-tuple-element.17.skelpos), custom_call_target="tpu_custom_call" | custom-call | bytes 524288 | tf_op jit(solution)/shard_map/pallas_call | solution.py:450
  4.3 19.1 %all_to_all.35.far_z = f32[8,40,128]{2,1,0:T(8,128)S(1)} all-to-all(f32[8,40,128]{2,1,0:T(8,128)} %get-tuple-element.18), channel_id=1, replica_groups=mesh['z'=8,'y'=8,'k'=2,'x'=4] {'z'}, dimensions={0} | all-to-all | bytes 327680 | tf_op jit(solution)/shard_map/all_to_all | solution.py:431
  23.4 9.6 %all-to-all-start = ((f32[16,8,128]{2,1,0:T(8,128)}), f32[16,8,128]{2,1,0:T(8,128)S(1)}, u32[]{:S(2)}, u32[]{:S(2)}) async-start(f32[16,8,128]{2,1,0:T(8,128)} %get-tuple-element.16), calls=%async_computation | async-start | bytes 131072 | tf_op jit(solution)/shard_map/all_to_all | solution.py:431
  33.0 7.8 %all-to-all-done.info = f32[16,8,128]{2,1,0:T(8,128)S(1)} async-done(((f32[16,8,128]{2,1,0:T(8,128)}), f32[16,8,128]{2,1,0:T(8,128)S(1)}, u32[]{:S(2)}, u32[]{:S(2)}) %all-to-all-start) | async-done | bytes 65568 | tf_op jit(solution)/shard_map/all_to_all | solution.py:431
  40.8 13.0 %all_to_all.36.far_x = f32[4,8,32,128]{3,2,1,0:T(8,128)S(1)} all-to-all(f32[4,8,32,128]{3,2,1,0:T(8,128)S(1)} %broadcast_in_dim.9), channel_id=1, replica_groups=mesh['z'=8,'y'=8,'k'=2,'x'=4] {'x'}, dimensions={0} | all-to-all | bytes 1048576 | tf_op jit(solution)/shard_map/all_to_all | solution.py:431
  53.8 6.5 %shard_map.96 = f32[16,32,128]{2,1,0:T(8,128)} custom-call(f32[16,8,128]{2,1,0:T(8,128)S(1)} %all-to-all-done.info, f32[8,40,128]{2,1,0:T(8,128)S(1)} %all_to_all.35.far_z, f32[4,8,32,128]{3,2,1,0:T(8,128)S(1)} %all_to_all.36.far_x), custom_call_target="tpu_custom_call" | custom-call | flops 805306368 | bytes 524288 | tf_op jit(solution)/shard_map/pallas_call | solution.py:480
  60.3 0.0 copy-start.4
  60.3 0.0 copy-start
  60.3 0.0 copy-start.2
  60.3 4.7 %all-to-all-start.3 = ((f32[16,32,128]{2,1,0:T(8,128)}), f32[16,32,128]{2,1,0:T(8,128)S(1)}, u32[]{:S(2)}, u32[]{:S(2)}) async-start(f32[16,32,128]{2,1,0:T(8,128)} %shard_map.96), calls=%async_computation.3 | async-start | bytes 524288 | tf_op jit(solution)/shard_map/all_to_all | solution.py:431
  65.0 0.0 copy-start.3
  65.0 0.0 copy-done.4
  65.0 2.1 %collective-permute-start.1 = (f32[40,512]{1,0:T(8,128)S(1)}, f32[40,512]{1,0:T(8,128)S(1)}, u32[]{:S(2)}, u32[]{:S(2)}) collective-permute-start(f32[40,512]{1,0:T(8,128)S(1)} %copy-done.4), channel_id=1, source_target_pairs={{4,0},{8,4},{12,8},{16,12},{20,16},{24,20},{28,24},{32,28},{36,32}... | collective-permute-start | bytes 245768 | tf_op jit(solution)/shard_map/ppermute | solution.py:458
  67.2 3.4 %collective-permute-start = (f32[40,512]{1,0:T(8,128)S(1)}, f32[40,512]{1,0:T(8,128)S(1)}, u32[]{:S(2)}, u32[]{:S(2)}) collective-permute-start(f32[40,512]{1,0:T(8,128)S(1)} %copy-done.4), channel_id=1, source_target_pairs={{0,4},{4,8},{8,12},{12,16},{16,20},{20,24},{24,28},{28,32},{32,36}... | collective-permute-start | bytes 245768 | tf_op jit(solution)/shard_map/ppermute | solution.py:457
  70.6 3.7 %collective-permute-done.1.nxt = f32[40,512]{1,0:T(8,128)S(1)} collective-permute-done((f32[40,512]{1,0:T(8,128)S(1)}, f32[40,512]{1,0:T(8,128)S(1)}, u32[]{:S(2)}, u32[]{:S(2)}) %collective-permute-start.1) | collective-permute-done | bytes 81952 | tf_op jit(solution)/shard_map/ppermute | solution.py:458
  74.3 0.0 collective-permute-done.prev
  74.3 0.0 copy-done
  74.3 0.0 copy-done.2
  74.3 0.0 copy-done.3
  74.3 6.7 %shard_map.97 = (f32[32,128]{1,0:T(8,128)S(1)}, f32[136,512]{1,0:T(8,128)S(1)}, f32[136,512]{1,0:T(8,128)S(1)}, f32[136,512]{1,0:T(8,128)S(1)}) custom-call(s32[4,27]{1,0:T(4,128)S(1)} %copy-done.2, s32[4]{0:T(128)S(1)} %copy-done.3, f32[40,512]{1,0:T(8,128)S(1)} %collective-permute-done.prev, f32[40,512]{1,0:T(8,128)S(1)} %copy-done.4, ...), custom_call_target="tpu_custom_call" | custom-call | flops 301989888 | bytes 524288 | tf_op jit(solution)/shard_map/pallas_call | solution.py:461
  81.1 2.2 %collective-permute-start.2 = (f32[136,512]{1,0:T(8,128)S(1)}, f32[136,512]{1,0:T(8,128)S(1)}, u32[]{:S(2)}, u32[]{:S(2)}) collective-permute-start(f32[136,512]{1,0:T(8,128)S(1)} %get-tuple-element.21), channel_id=1, source_target_pairs={{0,1},{1,2},{2,3},{3,0},{4,5},{5,6},{6,7},{7,4},{8,9},{9,10},{10,1... | collective-permute-start | bytes 835592 | tf_op jit(solution)/shard_map/ppermute | solution.py:426
  83.3 3.7 %collective-permute-start.3 = (f32[136,512]{1,0:T(8,128)S(1)}, f32[136,512]{1,0:T(8,128)S(1)}, u32[]{:S(2)}, u32[]{:S(2)}) collective-permute-start(f32[136,512]{1,0:T(8,128)S(1)} %get-tuple-element.22), channel_id=1, source_target_pairs={{0,2},{1,3},{2,0},{3,1},{4,6},{5,7},{6,4},{7,5},{8,10},{9,11},{10,... | collective-permute-start | bytes 835592 | tf_op jit(solution)/shard_map/ppermute | solution.py:426
  87.0 2.5 %collective-permute-start.4 = (f32[136,512]{1,0:T(8,128)S(1)}, f32[136,512]{1,0:T(8,128)S(1)}, u32[]{:S(2)}, u32[]{:S(2)}) collective-permute-start(f32[136,512]{1,0:T(8,128)S(1)} %get-tuple-element.23), channel_id=1, source_target_pairs={{0,3},{1,0},{2,1},{3,2},{4,7},{5,4},{6,5},{7,6},{8,11},{9,8},{10,9... | collective-permute-start | bytes 835592 | tf_op jit(solution)/shard_map/ppermute | solution.py:426
  89.5 5.7 %collective-permute-done.2.refs_0_ = f32[136,512]{1,0:T(8,128)S(1)} collective-permute-done((f32[136,512]{1,0:T(8,128)S(1)}, f32[136,512]{1,0:T(8,128)S(1)}, u32[]{:S(2)}, u32[]{:S(2)}) %collective-permute-start.2) | collective-permute-done | bytes 278560 | tf_op jit(solution)/shard_map/ppermute | solution.py:426
  95.2 0.0 collective-permute-done.3.refs_1_
  95.2 2.7 %collective-permute-done.4.refs_2_ = f32[136,512]{1,0:T(8,128)S(1)} collective-permute-done((f32[136,512]{1,0:T(8,128)S(1)}, f32[136,512]{1,0:T(8,128)S(1)}, u32[]{:S(2)}, u32[]{:S(2)}) %collective-permute-start.4) | collective-permute-done | bytes 278560 | tf_op jit(solution)/shard_map/ppermute | solution.py:426
  97.9 0.0 copy-start.1
  97.9 0.9 shard_map.98
  98.9 0.0 all-to-all-done.3.phi
  98.9 0.0 copy-done.1
  98.9 0.8 shard_map.99
  99.7 18.0 %all_to_all.37 = f32[16,16,128]{2,1,0:T(8,128)S(1)} all-to-all(f32[16,16,128]{2,1,0:T(8,128)S(1)} %get-tuple-element.27), channel_id=1, replica_groups=mesh['z'=8,'y'=8,'k'=2,'x'=4] {'y','k'}, dimensions={0} | all-to-all | bytes 262144 | tf_op jit(solution)/shard_map/all_to_all | solution.py:431
  117.8 16.0 %all_to_all.38 = f32[32,16,128]{2,1,0:T(8,128)S(1)} all-to-all(f32[32,16,128]{2,1,0:T(8,128)S(1)} %broadcast_in_dim.10), channel_id=1, replica_groups=mesh['z'=8,'y'=8,'k'=2,'x'=4] {'z','x'}, dimensions={0} | all-to-all | bytes 524288 | tf_op jit(solution)/shard_map/all_to_all | solution.py:431
  133.9 0.7 broadcast_in_dim.11
  134.6 5.1 %all-to-all-start.6 = ((f32[16,40,128]{2,1,0:T(8,128)}), f32[16,40,128]{2,1,0:T(8,128)S(1)}, u32[]{:S(2)}, u32[]{:S(2)}) async-start(f32[16,40,128]{2,1,0:T(8,128)} %broadcast_in_dim.11), calls=%async_computation.6 | async-start | bytes 655360 | tf_op jit(solution)/shard_map/all_to_all | solution.py:431
  139.7 2.8 %collective-permute-start.7 = (f32[64,256]{1,0:T(8,128)S(1)}, f32[64,256]{1,0:T(8,128)S(1)}, u32[]{:S(2)}, u32[]{:S(2)}) collective-permute-start(f32[64,256]{1,0:T(8,128)S(1)} %get-tuple-element.28.refs_0_), channel_id=1, source_target_pairs={{0,3},{1,0},{2,1},{3,2},{4,7},{5,4},{6,5},{7,6},{8,11},{9,8},{10,9... | collective-permute-start | bytes 196616 | tf_op jit(solution)/shard_map/ppermute | solution.py:426
  142.5 2.5 %collective-permute-start.6 = (f32[64,256]{1,0:T(8,128)S(1)}, f32[64,256]{1,0:T(8,128)S(1)}, u32[]{:S(2)}, u32[]{:S(2)}) collective-permute-start(f32[64,256]{1,0:T(8,128)S(1)} %get-tuple-element.28.refs_0_), channel_id=1, source_target_pairs={{0,2},{1,3},{2,0},{3,1},{4,6},{5,7},{6,4},{7,5},{8,10},{9,11},{10,... | collective-permute-start | bytes 196616 | tf_op jit(solution)/shard_map/ppermute | solution.py:426
  145.0 2.5 %collective-permute-start.5 = (f32[64,256]{1,0:T(8,128)S(1)}, f32[64,256]{1,0:T(8,128)S(1)}, u32[]{:S(2)}, u32[]{:S(2)}) collective-permute-start(f32[64,256]{1,0:T(8,128)S(1)} %get-tuple-element.28.refs_0_), channel_id=1, source_target_pairs={{0,1},{1,2},{2,3},{3,0},{4,5},{5,6},{6,7},{7,4},{8,9},{9,10},{10,1... | collective-permute-start | bytes 196616 | tf_op jit(solution)/shard_map/ppermute | solution.py:426
  147.5 0.0 collective-permute-done.7.refs_3_
  147.5 1.8 %collective-permute-done.6.refs_2_ = f32[64,256]{1,0:T(8,128)S(1)} collective-permute-done((f32[64,256]{1,0:T(8,128)S(1)}, f32[64,256]{1,0:T(8,128)S(1)}, u32[]{:S(2)}, u32[]{:S(2)}) %collective-permute-start.6) | collective-permute-done | bytes 65568 | tf_op jit(solution)/shard_map/ppermute | solution.py:426
  149.4 2.2 %collective-permute-done.5.refs_1_ = f32[64,256]{1,0:T(8,128)S(1)} collective-permute-done((f32[64,256]{1,0:T(8,128)S(1)}, f32[64,256]{1,0:T(8,128)S(1)}, u32[]{:S(2)}, u32[]{:S(2)}) %collective-permute-start.5) | collective-permute-done | bytes 65568 | tf_op jit(solution)/shard_map/ppermute | solution.py:426
  151.6 1.5 all-to-all-done.6.summed
  153.0 6.5 %shard_map.100 = (f32[2,16,512]{2,1,0:T(8,128)}, f32[4,64,64]{2,1,0:T(8,128)}, f32[64,64]{1,0:T(8,128)}) custom-call(f32[16,40,128]{2,1,0:T(8,128)S(1)} %all-to-all-done.6.summed, f32[2,256,512]{2,1,0:T(8,128)S(1)} %get-tuple-element.24.ordered, f32[64,256]{1,0:T(8,128)S(1)} %get-tuple-element.28.refs_0_, f32[64,256]{1,0:T(8,128)S(1)} %collective-permute-done.5.refs_1_, ...), custom_call_target="tpu_custom_call" | custom-call | bytes 524288 | tf_op jit(solution)/shard_map/pallas_call | solution.py:512
  (7 shorter events, 0.1 us)
Async XLA Ops:
  23.4 17.4 %all-to-all-start = ((f32[16,8,128]{2,1,0:T(8,128)}), f32[16,8,128]{2,1,0:T(8,128)S(1)}, u32[]{:S(2)}, u32[]{:S(2)}) async-start(f32[16,8,128]{2,1,0:T(8,128)} %get-tuple-element.16), calls=%async_computation | async-start | bytes 131072 | tf_op jit(solution)/shard_map/all_to_all | solution.py:431
  60.3 4.7 %copy-start.4 = (f32[40,512]{1,0:T(8,128)S(1)}, f32[40,512]{1,0:T(8,128)}, u32[]{:S(2)}) copy-start(f32[40,512]{1,0:T(8,128)} %get-tuple-element.19.own) | copy-start | bytes 245764
  60.3 14.0 %copy-start = (f32[4,2,16,512]{3,2,1,0:T(8,128)S(1)}, f32[4,2,16,512]{3,2,1,0:T(8,128)}, u32[]{:S(2)}) copy-start(f32[4,2,16,512]{3,2,1,0:T(8,128)} %cur.3) | copy-start | bytes 786436
  60.3 14.0 %copy-start.2 = (s32[4,27]{1,0:T(4,128)S(1)}, s32[4,27]{1,0:T(4,128)}, u32[]{:S(2)}) copy-start(s32[4,27]{1,0:T(4,128)} %near.3) | copy-start | bytes 1300
  60.3 38.6 %all-to-all-start.3 = ((f32[16,32,128]{2,1,0:T(8,128)}), f32[16,32,128]{2,1,0:T(8,128)S(1)}, u32[]{:S(2)}, u32[]{:S(2)}) async-start(f32[16,32,128]{2,1,0:T(8,128)} %shard_map.96), calls=%async_computation.3 | async-start | bytes 524288 | tf_op jit(solution)/shard_map/all_to_all | solution.py:431
  65.0 9.3 %copy-start.3 = (s32[4]{0:T(128)S(1)}, s32[4]{0:T(128)}, u32[]{:S(2)}) copy-start(s32[4]{0:T(128)} %count.3) | copy-start | bytes 52
  65.0 9.3 %collective-permute-start.1 = (f32[40,512]{1,0:T(8,128)S(1)}, f32[40,512]{1,0:T(8,128)S(1)}, u32[]{:S(2)}, u32[]{:S(2)}) collective-permute-start(f32[40,512]{1,0:T(8,128)S(1)} %copy-done.4), channel_id=1, source_target_pairs={{4,0},{8,4},{12,8},{16,12},{20,16},{24,20},{28,24},{32,28},{36,32}... | collective-permute-start | bytes 245768 | tf_op jit(solution)/shard_map/ppermute | solution.py:458
  67.2 7.2 %collective-permute-start = (f32[40,512]{1,0:T(8,128)S(1)}, f32[40,512]{1,0:T(8,128)S(1)}, u32[]{:S(2)}, u32[]{:S(2)}) collective-permute-start(f32[40,512]{1,0:T(8,128)S(1)} %copy-done.4), channel_id=1, source_target_pairs={{0,4},{4,8},{8,12},{12,16},{16,20},{20,24},{24,28},{28,32},{32,36}... | collective-permute-start | bytes 245768 | tf_op jit(solution)/shard_map/ppermute | solution.py:457
  81.1 14.2 %collective-permute-start.2 = (f32[136,512]{1,0:T(8,128)S(1)}, f32[136,512]{1,0:T(8,128)S(1)}, u32[]{:S(2)}, u32[]{:S(2)}) collective-permute-start(f32[136,512]{1,0:T(8,128)S(1)} %get-tuple-element.21), channel_id=1, source_target_pairs={{0,1},{1,2},{2,3},{3,0},{4,5},{5,6},{6,7},{7,4},{8,9},{9,10},{10,1... | collective-permute-start | bytes 835592 | tf_op jit(solution)/shard_map/ppermute | solution.py:426
  83.3 12.0 %collective-permute-start.3 = (f32[136,512]{1,0:T(8,128)S(1)}, f32[136,512]{1,0:T(8,128)S(1)}, u32[]{:S(2)}, u32[]{:S(2)}) collective-permute-start(f32[136,512]{1,0:T(8,128)S(1)} %get-tuple-element.22), channel_id=1, source_target_pairs={{0,2},{1,3},{2,0},{3,1},{4,6},{5,7},{6,4},{7,5},{8,10},{9,11},{10,... | collective-permute-start | bytes 835592 | tf_op jit(solution)/shard_map/ppermute | solution.py:426
  87.0 10.9 %collective-permute-start.4 = (f32[136,512]{1,0:T(8,128)S(1)}, f32[136,512]{1,0:T(8,128)S(1)}, u32[]{:S(2)}, u32[]{:S(2)}) collective-permute-start(f32[136,512]{1,0:T(8,128)S(1)} %get-tuple-element.23), channel_id=1, source_target_pairs={{0,3},{1,0},{2,1},{3,2},{4,7},{5,4},{6,5},{7,6},{8,11},{9,8},{10,9... | collective-permute-start | bytes 835592 | tf_op jit(solution)/shard_map/ppermute | solution.py:426
  97.9 1.0 copy-start.1
  134.6 18.4 %all-to-all-start.6 = ((f32[16,40,128]{2,1,0:T(8,128)}), f32[16,40,128]{2,1,0:T(8,128)S(1)}, u32[]{:S(2)}, u32[]{:S(2)}) async-start(f32[16,40,128]{2,1,0:T(8,128)} %broadcast_in_dim.11), calls=%async_computation.6 | async-start | bytes 655360 | tf_op jit(solution)/shard_map/all_to_all | solution.py:431
  139.7 7.8 %collective-permute-start.7 = (f32[64,256]{1,0:T(8,128)S(1)}, f32[64,256]{1,0:T(8,128)S(1)}, u32[]{:S(2)}, u32[]{:S(2)}) collective-permute-start(f32[64,256]{1,0:T(8,128)S(1)} %get-tuple-element.28.refs_0_), channel_id=1, source_target_pairs={{0,3},{1,0},{2,1},{3,2},{4,7},{5,4},{6,5},{7,6},{8,11},{9,8},{10,9... | collective-permute-start | bytes 196616 | tf_op jit(solution)/shard_map/ppermute | solution.py:426
  142.5 6.8 %collective-permute-start.6 = (f32[64,256]{1,0:T(8,128)S(1)}, f32[64,256]{1,0:T(8,128)S(1)}, u32[]{:S(2)}, u32[]{:S(2)}) collective-permute-start(f32[64,256]{1,0:T(8,128)S(1)} %get-tuple-element.28.refs_0_), channel_id=1, source_target_pairs={{0,2},{1,3},{2,0},{3,1},{4,6},{5,7},{6,4},{7,5},{8,10},{9,11},{10,... | collective-permute-start | bytes 196616 | tf_op jit(solution)/shard_map/ppermute | solution.py:426
  145.0 6.5 %collective-permute-start.5 = (f32[64,256]{1,0:T(8,128)S(1)}, f32[64,256]{1,0:T(8,128)S(1)}, u32[]{:S(2)}, u32[]{:S(2)}) collective-permute-start(f32[64,256]{1,0:T(8,128)S(1)} %get-tuple-element.28.refs_0_), channel_id=1, source_target_pairs={{0,1},{1,2},{2,3},{3,0},{4,5},{5,6},{6,7},{7,4},{8,9},{9,10},{10,1... | collective-permute-start | bytes 196616 | tf_op jit(solution)/shard_map/ppermute | solution.py:426

commit v5 on v4

--- a/solution.py
+++ b/solution.py
@@ -113,15 +113,25 @@
     return jnp.concatenate([offsets[:, cols], jnp.zeros((5, PTS), F32)], axis=0) + shift
 
 
-def place_kernel(dims, near, count, offsets, skel, info, skelpos):
+def prep_kernel(dims, near, count, cur, weights, offsets, interp, skel, halo, far, info):
     group = group_index(dims)
     x = lax.axis_index("x")
+    src = jnp.concatenate([cur[3, 0], cur[3, 1]], axis=0) * weights[...]
+    halo[0:32, :] = src
+    charges = []
     spots = []
     for b in range(BOX_DEV):
+        cols = slice(PTS * b, PTS * b + PTS)
+        pos = centred(offsets, b, group)
+        halo[32:40, cols] = pos
+        charges.append(dot(src[:, cols], interp[b], 1, 1, HIGHEST))
         q = lax.broadcasted_iota(jnp.int32, (PTS, SKEL), 0)
         pick = (q == skel[b : b + 1, :]).astype(F32)
-        spots.append(dot(centred(offsets, b, group), pick, 1, 0, HIGHEST))
-    skelpos[...] = jnp.concatenate(spots, axis=1)
+        spots.append(dot(pos, pick, 1, 0, HIGHEST))
+    payload = jnp.concatenate(
+        [jnp.concatenate(charges, axis=1), jnp.concatenate(spots, axis=1)], axis=0
+    )
+    far[...] = jnp.broadcast_to(payload[None], far.shape)
     row = lax.broadcasted_iota(jnp.int32, (8, PTS), 0)
     lane = lax.broadcasted_iota(jnp.int32, (8, PTS), 1)
     box_of = BOX_DEV * (group + row - 1) + lane // SKEL
@@ -132,7 +142,7 @@
     spot = spots[0]
     for b in range(1, BOX_DEV):
         spot = jnp.where(x == b, spots[b], spot)
-    about = jnp.concatenate(
+    info[...] = jnp.concatenate(
         [
             jnp.concatenate([spot[0:3], jnp.zeros((3, PTS - SKEL), F32)], axis=1),
             1.0 - listed[0:3],
@@ -140,20 +150,6 @@
         ],
         axis=0,
     )
-    info[...] = jnp.broadcast_to(about[None], info.shape)
-
-
-def prep_kernel(dims, cur, weights, offsets, interp, skelpos, halo, far):
-    group = group_index(dims)
-    src = jnp.concatenate([cur[3, 0], cur[3, 1]], axis=0) * weights[...]
-    halo[0:32, :] = src
-    charges = []
-    for b in range(BOX_DEV):
-        cols = slice(PTS * b, PTS * b + PTS)
-        halo[32:40, cols] = centred(offsets, b, group)
-        charges.append(dot(src[:, cols], interp[b], 1, 1, HIGHEST))
-    payload = jnp.concatenate([jnp.concatenate(charges, axis=1), skelpos[...]], axis=0)
-    far[...] = jnp.broadcast_to(payload[None], far.shape)
 
 
 def from_x(r):
@@ -224,12 +220,12 @@
         )
 
 
-def far_kernel(dims, info, far_z, far_x, out, tpos, rhi, rlo, weight, acc):
+def far_kernel(dims, info, gathered, out, tpos, rhi, rlo, weight, acc):
     nz, ny, nk, nx = dims
     targets = ny * nk
     mine = lax.axis_index("y") * nk + lax.axis_index("k")
     first = lax.axis_index("z") * targets
-    stack = jnp.concatenate([info[d] for d in range(targets)], axis=0)
+    stack = info[...]
     if targets * 8 < PTS:
         stack = jnp.concatenate([stack, jnp.zeros((PTS - targets * 8, PTS), F32)], axis=0)
     turned = stack.T
@@ -239,7 +235,7 @@
                 turned[0:SKEL, 8 * d + c : 8 * d + c + 1], (SKEL, PTS)
             )
     for g in range(nz):
-        rows = jnp.concatenate([far_x[c, g] for c in range(nx)], axis=0)
+        rows = jnp.concatenate([gathered[nx * g + c, 0:32, :] for c in range(nx)], axis=0)
         hi, lo = split(jnp.concatenate([rows, rotate(rows)], axis=1))
         rhi[g] = hi
         rlo[g] = lo
@@ -247,15 +243,15 @@
     per = min(4, targets)
 
     def step(g, carry):
-        sx = far_z[g, 32:33, :]
-        sy = far_z[g, 33:34, :]
-        sz = far_z[g, 34:35, :]
+        sx = gathered[nx * g, 32:33, :]
+        sy = gathered[nx * g, 33:34, :]
+        sz = gathered[nx * g, 34:35, :]
         source_group = g * targets + mine
         for d in range(targets):
-            delta = source_group - (first + d)
-            w = jnp.where(delta == -1, info[d, 3:4, :], 1.0)
-            w = jnp.where(delta == 0, info[d, 4:5, :], w)
-            w = jnp.where(delta == 1, info[d, 5:6, :], w)
+            delta = source_group - (first + lax.bitwise_xor(mine, d))
+            w = jnp.where(delta == -1, info[8 * d + 3 : 8 * d + 4, :], 1.0)
+            w = jnp.where(delta == 0, info[8 * d + 4 : 8 * d + 5, :], w)
+            w = jnp.where(delta == 1, info[8 * d + 5 : 8 * d + 6, :], w)
             weight[SKEL * d : SKEL * d + SKEL, :] = jnp.broadcast_to(
                 w * (0.25 / math.pi), (SKEL, PTS)
             )
@@ -278,7 +274,7 @@
 
     lax.fori_loop(0, nz, step, 0)
     for d in range(targets):
-        out[d] = acc[SKEL * d : SKEL * d + SKEL, :]
+        out[lax.bitwise_xor(mine, d)] = acc[SKEL * d : SKEL * d + SKEL, :]
 
 
 def halves(rows, nx):
@@ -440,23 +436,19 @@
     scale = 1.0 / (groups * points)
     shape = lambda *s: jax.ShapeDtypeStruct(s, F32)
 
-    info, skelpos = call(
-        functools.partial(place_kernel, dims),
-        (shape(targets, 8, PTS), shape(8, PTS)),
-        [SMEM, SMEM, VMEM, VMEM],
+    halo, far, info = call(
+        functools.partial(prep_kernel, dims),
+        (shape(40, points), shape(sources, 40, PTS), shape(8, PTS)),
+        [SMEM, SMEM] + [VMEM] * 5,
         limit=None,
-    )(near_boxes, near_count, offsets, skeleton)
-    info_all = trade(info, YK)
-    halo, far = call(
-        functools.partial(prep_kernel, dims),
-        (shape(40, points), shape(nz, 40, PTS)),
-        [VMEM] * 5,
-        limit=None,
-    )(basis, weights[None], offsets, interp, skelpos)
-    far_z = trade(far, "z")
+    )(near_boxes, near_count, basis, weights[None], offsets, interp, skeleton)
+    far_all = trade(far, ZX)
     prev = lax.ppermute(halo, BOX, [(g, g + 1) for g in range(groups - 1)])
     nxt = lax.ppermute(halo, BOX, [(g + 1, g) for g in range(groups - 1)])
-    far_x = trade(jnp.broadcast_to(far_z[None, :, :32], (nx, nz, 32, PTS)), "x")
+    steps = [("k", 1, nk)] + [("y", 1 << b, ny) for b in range(ny.bit_length() - 1)]
+    for axis, bit, size in steps:
+        other = lax.ppermute(info, axis, [(i, i ^ bit) for i in range(size)])
+        info = jnp.concatenate([info, other], axis=0)
 
     nears = call(
         functools.partial(near_kernel, dims),
@@ -480,7 +472,7 @@
     far_part = call(
         functools.partial(far_kernel, dims),
         shape(targets, SKEL, 32 * nx),
-        [VMEM] * 3,
+        [VMEM] * 2,
         [
             pltpu.VMEM((3, SKEL * targets, PTS), F32),
             pltpu.VMEM((nz, 32 * nx, 2 * PTS), BF16),
@@ -489,7 +481,7 @@
             pltpu.VMEM((SKEL * targets, 32 * nx), F32),
         ],
         flops=3 * 2 * 512 * 2048 * 128,
-    )(info_all, far_z, far_x)
+    )(info, far_all)
     phi = trade(far_part, YK)
 
     lead = 128 // targets

time: 160 us -> 157 us (0.981)
  starting transfers between devices: 41.2 us -> 71.3 us
  blocking collectives: 66.1 us -> 39.3 us
  waiting for transfers between devices: 25.4 us -> 20.4 us
    all_to_all x4 -> x2, blocking collectives: 66.1 us -> 39.3 us  [trade(): return lax.all_to_all(value, axes, split_axis=0, concat_axis=0, tiled=True)]
    ppermute x0 -> x4, starting transfers between devices: none -> 17.7 us  [shards(): other = lax.ppermute(info, axis, [(i, i ^ bit) for i in range(size)])]
    all_to_all x3, starting transfers between devices: 19.4 us -> 29.4 us  [trade(): return lax.all_to_all(value, axes, split_axis=0, concat_axis=0, tiled=True)]
    all_to_all x3, waiting for transfers between devices: 9.21 us -> 1.46 us  [trade(): return lax.all_to_all(value, axes, split_axis=0, concat_axis=0, tiled=True)]
    ppermute x0 -> x4, waiting for transfers between devices: none -> 5.01 us  [shards(): other = lax.ppermute(info, axis, [(i, i ^ bit) for i in range(size)])]
    ppermute x6, starting transfers between devices: 16.2 us -> 18.6 us  [around(): lax.ppermute(blocks[r], 'x', [(i, (i + r) % n) for i in range(n)])]
    ppermute x6, waiting for transfers between devices: 12.4 us -> 10.2 us  [around(): lax.ppermute(blocks[r], 'x', [(i, (i + r) % n) for i in range(n)])]
    pallas_call x2 -> x1, Pallas kernels: 3.69 us -> 2.38 us  [shards(): call(functools.partial(prep_kernel, dims), (shape(40, points), shape(sour...]
  transfers between devices with their start and end apart: 11 -> 15, of which waited for: 7 -> 11; matrix products, arithmetic and copies ran while one was open for 0% -> 0% of each run, Pallas kernels for 5% -> 5%
where the time goes in v5:
time: 157 us
  starting transfers between devices  71.3 us (45%)
  blocking collectives  39.3 us (25%)
  Pallas kernels  23.9 us (15%)
  waiting for transfers between devices  20.4 us (13%)
    all_to_all x2, blocking collectives, trade(): return lax.all_to_all(value, axes, split_axis=0, concat_axis=0, tiled=True)  39.3 us
    all_to_all x3, starting transfers between devices, trade(): return lax.all_to_all(value, axes, split_axis=0, concat_axis=0, tiled=True)  29.4 us
    ppermute x6, starting transfers between devices, around(): lax.ppermute(blocks[r], 'x', [(i, (i + r) % n) for i in range(n)])  18.6 us
    ppermute x4, starting transfers between devices, shards(): other = lax.ppermute(info, axis, [(i, i ^ bit) for i in range(size)])  17.7 us
    ppermute x6, waiting for transfers between devices, around(): lax.ppermute(blocks[r], 'x', [(i, (i + r) % n) for i in range(n)])  10.2 us
    pallas_call x1, Pallas kernels, shards(): call(functools.partial(near_kernel, dims), (shape(32, PTS),) + (shape(PTS...  6.71 us
    pallas_call x1, Pallas kernels, shards(): call(functools.partial(finish_kernel, nx), (shape(2, 16, points), shape(4...  6.54 us
    pallas_call x1, Pallas kernels, shards(): call(functools.partial(far_kernel, dims), shape(targets, SKEL, 32 * nx),...  6.49 us
  transfers between devices with their start and end apart: 15, of which 11 were waited for; matrix products, arithmetic and copies ran while one was open for 0% of the time, Pallas kernels for 5%

profile of v5, /device:TPU:1, one launch (start us, length us, event | category | flops | bytes accessed | tf_op | source)
XLA Modules:
  0.0 156.6 jit_solution(11091956891142509980)
XLA Ops:
  0.6 2.4 %shard_map.94 = (f32[40,512]{1,0:T(8,128)}, f32[32,40,128]{2,1,0:T(8,128)}, f32[8,128]{1,0:T(8,128)}) custom-call(s32[4,27]{1,0:T(4,128)} %near.3, s32[4]{0:T(128)} %count.3, f32[4,2,16,512]{3,2,1,0:T(8,128)} %cur.3, f32[1,512]{1,0:T(1,128)} %bitcast.7, f32[3,512]{1,0:T(4,128)} %offsets.1, f32[4,32,128]{2,1,0:T(8,128)} %interp.3, s32[4,32]{1,0:T(4,128)} %skel.1), custom_call_target="tpu_custom_call" | custom-call | bytes 524288 | tf_op jit(solution)/shard_map/pallas_call | solution.py:439
  3.0 0.0 copy-start.5
  3.0 13.8 %all-to-all-start = ((f32[32,40,128]{2,1,0:T(8,128)}), f32[32,40,128]{2,1,0:T(8,128)S(1)}, u32[]{:S(2)}, u32[]{:S(2)}) async-start(f32[32,40,128]{2,1,0:T(8,128)} %get-tuple-element.16), calls=%async_computation | async-start | bytes 1310720 | tf_op jit(solution)/shard_map/all_to_all | solution.py:427
  16.9 0.0 copy-done.5
  16.9 2.9 %collective-permute-start = (f32[8,128]{1,0:T(8,128)S(1)}, f32[8,128]{1,0:T(8,128)S(1)}, u32[]{:S(2)}, u32[]{:S(2)}) collective-permute-start(f32[8,128]{1,0:T(8,128)S(1)} %copy-done.5), channel_id=1, source_target_pairs={{0,4},{4,0},{1,5},{5,1},{2,6},{6,2},{3,7},{7,3},{8,12},{12,8},{9,1... | collective-permute-start | bytes 12296 | tf_op jit(solution)/shard_map/ppermute | solution.py:450
  19.8 0.8 collective-permute-done
  20.5 3.2 %collective-permute-start.1 = (f32[16,128]{1,0:T(8,128)S(1)}, f32[16,128]{1,0:T(8,128)S(1)}, u32[]{:S(2)}, u32[]{:S(2)}) collective-permute-start(f32[16,128]{1,0:T(8,128)S(1)} %pad_maximum_fusion.3), channel_id=1, source_target_pairs={{0,8},{8,0},{16,24},{24,16},{32,40},{40,32},{48,56},{56,48},{1,9},... | collective-permute-start | bytes 24584 | tf_op jit(solution)/shard_map/ppermute | solution.py:450
  23.8 1.5 collective-permute-done.1
  25.2 4.2 %collective-permute-start.2 = (f32[32,128]{1,0:T(8,128)S(1)}, f32[32,128]{1,0:T(8,128)S(1)}, u32[]{:S(2)}, u32[]{:S(2)}) collective-permute-start(f32[32,128]{1,0:T(8,128)S(1)} %pad_maximum_fusion.2), channel_id=1, source_target_pairs={{0,16},{8,24},{16,0},{24,8},{32,48},{40,56},{48,32},{56,40},{1,17}... | collective-permute-start | bytes 49160 | tf_op jit(solution)/shard_map/ppermute | solution.py:450
  29.5 1.4 collective-permute-done.2
  30.9 7.5 %collective-permute-start.3 = (f32[64,128]{1,0:T(8,128)S(1)}, f32[64,128]{1,0:T(8,128)S(1)}, u32[]{:S(2)}, u32[]{:S(2)}) collective-permute-start(f32[64,128]{1,0:T(8,128)S(1)} %pad_maximum_fusion), channel_id=1, source_target_pairs={{0,32},{8,40},{16,48},{24,56},{32,0},{40,8},{48,16},{56,24},{1,33}... | collective-permute-start | bytes 98312 | tf_op jit(solution)/shard_map/ppermute | solution.py:450
  38.4 1.3 collective-permute-done.3
  39.7 0.0 all-to-all-done.gathered
  39.7 6.5 %shard_map.95 = f32[16,32,128]{2,1,0:T(8,128)} custom-call(f32[128,128]{1,0:T(8,128)S(1)} %constant_dynamic-update-slice_fusion.info, f32[32,40,128]{2,1,0:T(8,128)S(1)} %all-to-all-done.gathered), custom_call_target="tpu_custom_call" | custom-call | flops 805306368 | bytes 524288 | tf_op jit(solution)/shard_map/pallas_call | solution.py:472
  46.2 0.0 copy-start.4
  46.2 0.0 copy-start
  46.2 10.5 %all-to-all-start.1 = ((f32[16,32,128]{2,1,0:T(8,128)}), f32[16,32,128]{2,1,0:T(8,128)S(1)}, u32[]{:S(2)}, u32[]{:S(2)}) async-start(f32[16,32,128]{2,1,0:T(8,128)} %shard_map.95), calls=%async_computation.1 | async-start | bytes 524288 | tf_op jit(solution)/shard_map/all_to_all | solution.py:427
  56.7 0.0 copy-done.4
  56.7 2.0 %collective-permute-start.5 = (f32[40,512]{1,0:T(8,128)S(1)}, f32[40,512]{1,0:T(8,128)S(1)}, u32[]{:S(2)}, u32[]{:S(2)}) collective-permute-start(f32[40,512]{1,0:T(8,128)S(1)} %copy-done.4), channel_id=1, source_target_pairs={{4,0},{8,4},{12,8},{16,12},{20,16},{24,20},{28,24},{32,28},{36,32}... | collective-permute-start | bytes 245768 | tf_op jit(solution)/shard_map/ppermute | solution.py:447
  58.7 3.5 %collective-permute-start.4 = (f32[40,512]{1,0:T(8,128)S(1)}, f32[40,512]{1,0:T(8,128)S(1)}, u32[]{:S(2)}, u32[]{:S(2)}) collective-permute-start(f32[40,512]{1,0:T(8,128)S(1)} %copy-done.4), channel_id=1, source_target_pairs={{0,4},{4,8},{8,12},{12,16},{16,20},{20,24},{24,28},{28,32},{32,36}... | collective-permute-start | bytes 245768 | tf_op jit(solution)/shard_map/ppermute | solution.py:446
  62.2 3.7 %collective-permute-done.5.nxt = f32[40,512]{1,0:T(8,128)S(1)} collective-permute-done((f32[40,512]{1,0:T(8,128)S(1)}, f32[40,512]{1,0:T(8,128)S(1)}, u32[]{:S(2)}, u32[]{:S(2)}) %collective-permute-start.5) | collective-permute-done | bytes 81952 | tf_op jit(solution)/shard_map/ppermute | solution.py:447
  65.9 0.0 collective-permute-done.4.prev
  65.9 0.0 copy-done
  66.0 0.0 copy-done.2
  66.0 0.0 copy-done.3
  66.0 6.7 %shard_map.96 = (f32[32,128]{1,0:T(8,128)S(1)}, f32[136,512]{1,0:T(8,128)S(1)}, f32[136,512]{1,0:T(8,128)S(1)}, f32[136,512]{1,0:T(8,128)S(1)}) custom-call(s32[4,27]{1,0:T(4,128)S(1)} %copy-done.2, s32[4]{0:T(128)S(1)} %copy-done.3, f32[40,512]{1,0:T(8,128)S(1)} %collective-permute-done.4.prev, f32[40,512]{1,0:T(8,128)S(1)} %copy-done.4, ...), custom_call_target="tpu_custom_call" | custom-call | flops 301989888 | bytes 524288 | tf_op jit(solution)/shard_map/pallas_call | solution.py:453
  72.7 3.4 %collective-permute-start.6 = (f32[136,512]{1,0:T(8,128)S(1)}, f32[136,512]{1,0:T(8,128)S(1)}, u32[]{:S(2)}, u32[]{:S(2)}) collective-permute-start(f32[136,512]{1,0:T(8,128)S(1)} %get-tuple-element.19), channel_id=1, source_target_pairs={{0,1},{1,2},{2,3},{3,0},{4,5},{5,6},{6,7},{7,4},{8,9},{9,10},{10,1... | collective-permute-start | bytes 835592 | tf_op jit(solution)/shard_map/ppermute | solution.py:422
  76.1 4.3 %collective-permute-start.7 = (f32[136,512]{1,0:T(8,128)S(1)}, f32[136,512]{1,0:T(8,128)S(1)}, u32[]{:S(2)}, u32[]{:S(2)}) collective-permute-start(f32[136,512]{1,0:T(8,128)S(1)} %get-tuple-element.20), channel_id=1, source_target_pairs={{0,2},{1,3},{2,0},{3,1},{4,6},{5,7},{6,4},{7,5},{8,10},{9,11},{10,... | collective-permute-start | bytes 835592 | tf_op jit(solution)/shard_map/ppermute | solution.py:422
  80.4 3.1 %collective-permute-start.8 = (f32[136,512]{1,0:T(8,128)S(1)}, f32[136,512]{1,0:T(8,128)S(1)}, u32[]{:S(2)}, u32[]{:S(2)}) collective-permute-start(f32[136,512]{1,0:T(8,128)S(1)} %get-tuple-element.21), channel_id=1, source_target_pairs={{0,3},{1,0},{2,1},{3,2},{4,7},{5,4},{6,5},{7,6},{8,11},{9,8},{10,9... | collective-permute-start | bytes 835592 | tf_op jit(solution)/shard_map/ppermute | solution.py:422
  83.5 0.8 collective-permute-done.6.refs_0_
  84.3 3.5 %collective-permute-done.7.refs_1_ = f32[136,512]{1,0:T(8,128)S(1)} collective-permute-done((f32[136,512]{1,0:T(8,128)S(1)}, f32[136,512]{1,0:T(8,128)S(1)}, u32[]{:S(2)}, u32[]{:S(2)}) %collective-permute-start.7) | collective-permute-done | bytes 278560 | tf_op jit(solution)/shard_map/ppermute | solution.py:422
  87.9 1.8 %collective-permute-done.8.refs_2_ = f32[136,512]{1,0:T(8,128)S(1)} collective-permute-done((f32[136,512]{1,0:T(8,128)S(1)}, f32[136,512]{1,0:T(8,128)S(1)}, u32[]{:S(2)}, u32[]{:S(2)}) %collective-permute-start.8) | collective-permute-done | bytes 278560 | tf_op jit(solution)/shard_map/ppermute | solution.py:422
  89.7 0.9 shard_map.97
  90.6 0.0 all-to-all-done.1.phi
  90.7 0.0 copy-done.1
  90.7 0.8 shard_map.98
  91.5 17.8 %all_to_all.25 = f32[16,16,128]{2,1,0:T(8,128)S(1)} all-to-all(f32[16,16,128]{2,1,0:T(8,128)S(1)} %get-tuple-element.25), channel_id=1, replica_groups=mesh['z'=8,'y'=8,'k'=2,'x'=4] {'y','k'}, dimensions={0} | all-to-all | bytes 262144 | tf_op jit(solution)/shard_map/all_to_all | solution.py:427
  109.4 21.5 %all_to_all.26 = f32[32,16,128]{2,1,0:T(8,128)S(1)} all-to-all(f32[32,16,128]{2,1,0:T(8,128)S(1)} %broadcast_in_dim.7), channel_id=1, replica_groups=mesh['z'=8,'y'=8,'k'=2,'x'=4] {'z','x'}, dimensions={0} | all-to-all | bytes 524288 | tf_op jit(solution)/shard_map/all_to_all | solution.py:427
  130.9 0.8 broadcast_in_dim.8
  131.7 5.1 %all-to-all-start.4 = ((f32[16,40,128]{2,1,0:T(8,128)}), f32[16,40,128]{2,1,0:T(8,128)S(1)}, u32[]{:S(2)}, u32[]{:S(2)}) async-start(f32[16,40,128]{2,1,0:T(8,128)} %broadcast_in_dim.8), calls=%async_computation.4 | async-start | bytes 655360 | tf_op jit(solution)/shard_map/all_to_all | solution.py:427
  136.8 2.8 %collective-permute-start.11 = (f32[64,256]{1,0:T(8,128)S(1)}, f32[64,256]{1,0:T(8,128)S(1)}, u32[]{:S(2)}, u32[]{:S(2)}) collective-permute-start(f32[64,256]{1,0:T(8,128)S(1)} %get-tuple-element.26.refs_0_), channel_id=1, source_target_pairs={{0,3},{1,0},{2,1},{3,2},{4,7},{5,4},{6,5},{7,6},{8,11},{9,8},{10,9... | collective-permute-start | bytes 196616 | tf_op jit(solution)/shard_map/ppermute | solution.py:422
  139.6 2.5 %collective-permute-start.10 = (f32[64,256]{1,0:T(8,128)S(1)}, f32[64,256]{1,0:T(8,128)S(1)}, u32[]{:S(2)}, u32[]{:S(2)}) collective-permute-start(f32[64,256]{1,0:T(8,128)S(1)} %get-tuple-element.26.refs_0_), channel_id=1, source_target_pairs={{0,2},{1,3},{2,0},{3,1},{4,6},{5,7},{6,4},{7,5},{8,10},{9,11},{10,... | collective-permute-start | bytes 196616 | tf_op jit(solution)/shard_map/ppermute | solution.py:422
  142.1 2.5 %collective-permute-start.9 = (f32[64,256]{1,0:T(8,128)S(1)}, f32[64,256]{1,0:T(8,128)S(1)}, u32[]{:S(2)}, u32[]{:S(2)}) collective-permute-start(f32[64,256]{1,0:T(8,128)S(1)} %get-tuple-element.26.refs_0_), channel_id=1, source_target_pairs={{0,1},{1,2},{2,3},{3,0},{4,5},{5,6},{6,7},{7,4},{8,9},{9,10},{10,1... | collective-permute-start | bytes 196616 | tf_op jit(solution)/shard_map/ppermute | solution.py:422
  144.6 0.0 collective-permute-done.11.refs_3_
  144.6 1.8 %collective-permute-done.10.refs_2_ = f32[64,256]{1,0:T(8,128)S(1)} collective-permute-done((f32[64,256]{1,0:T(8,128)S(1)}, f32[64,256]{1,0:T(8,128)S(1)}, u32[]{:S(2)}, u32[]{:S(2)}) %collective-permute-start.10) | collective-permute-done | bytes 65568 | tf_op jit(solution)/shard_map/ppermute | solution.py:422
  146.4 2.2 %collective-permute-done.9.refs_1_ = f32[64,256]{1,0:T(8,128)S(1)} collective-permute-done((f32[64,256]{1,0:T(8,128)S(1)}, f32[64,256]{1,0:T(8,128)S(1)}, u32[]{:S(2)}, u32[]{:S(2)}) %collective-permute-start.9) | collective-permute-done | bytes 65568 | tf_op jit(solution)/shard_map/ppermute | solution.py:422
  148.6 1.5 all-to-all-done.4.summed
  150.1 6.5 %shard_map.99 = (f32[2,16,512]{2,1,0:T(8,128)}, f32[4,64,64]{2,1,0:T(8,128)}, f32[64,64]{1,0:T(8,128)}) custom-call(f32[16,40,128]{2,1,0:T(8,128)S(1)} %all-to-all-done.4.summed, f32[2,256,512]{2,1,0:T(8,128)S(1)} %get-tuple-element.22.ordered, f32[64,256]{1,0:T(8,128)S(1)} %get-tuple-element.26.refs_0_, f32[64,256]{1,0:T(8,128)S(1)} %collective-permute-done.9.refs_1_, ...), custom_call_target="tpu_custom_call" | custom-call | bytes 524288 | tf_op jit(solution)/shard_map/pallas_call | solution.py:504
  (16 shorter events, 0.1 us)
Async XLA Ops:
  3.0 13.8 %copy-start.5 = (f32[8,128]{1,0:T(8,128)S(1)}, f32[8,128]{1,0:T(8,128)}, u32[]{:S(2)}) copy-start(f32[8,128]{1,0:T(8,128)} %get-tuple-element.15) | copy-start | bytes 12292
  3.0 36.7 %all-to-all-start = ((f32[32,40,128]{2,1,0:T(8,128)}), f32[32,40,128]{2,1,0:T(8,128)S(1)}, u32[]{:S(2)}, u32[]{:S(2)}) async-start(f32[32,40,128]{2,1,0:T(8,128)} %get-tuple-element.16), calls=%async_computation | async-start | bytes 1310720 | tf_op jit(solution)/shard_map/all_to_all | solution.py:427
  16.9 3.7 %collective-permute-start = (f32[8,128]{1,0:T(8,128)S(1)}, f32[8,128]{1,0:T(8,128)S(1)}, u32[]{:S(2)}, u32[]{:S(2)}) collective-permute-start(f32[8,128]{1,0:T(8,128)S(1)} %copy-done.5), channel_id=1, source_target_pairs={{0,4},{4,0},{1,5},{5,1},{2,6},{6,2},{3,7},{7,3},{8,12},{12,8},{9,1... | collective-permute-start | bytes 12296 | tf_op jit(solution)/shard_map/ppermute | solution.py:450
  20.5 4.7 %collective-permute-start.1 = (f32[16,128]{1,0:T(8,128)S(1)}, f32[16,128]{1,0:T(8,128)S(1)}, u32[]{:S(2)}, u32[]{:S(2)}) collective-permute-start(f32[16,128]{1,0:T(8,128)S(1)} %pad_maximum_fusion.3), channel_id=1, source_target_pairs={{0,8},{8,0},{16,24},{24,16},{32,40},{40,32},{48,56},{56,48},{1,9},... | collective-permute-start | bytes 24584 | tf_op jit(solution)/shard_map/ppermute | solution.py:450
  25.2 5.7 %collective-permute-start.2 = (f32[32,128]{1,0:T(8,128)S(1)}, f32[32,128]{1,0:T(8,128)S(1)}, u32[]{:S(2)}, u32[]{:S(2)}) collective-permute-start(f32[32,128]{1,0:T(8,128)S(1)} %pad_maximum_fusion.2), channel_id=1, source_target_pairs={{0,16},{8,24},{16,0},{24,8},{32,48},{40,56},{48,32},{56,40},{1,17}... | collective-permute-start | bytes 49160 | tf_op jit(solution)/shard_map/ppermute | solution.py:450
  30.9 8.8 %collective-permute-start.3 = (f32[64,128]{1,0:T(8,128)S(1)}, f32[64,128]{1,0:T(8,128)S(1)}, u32[]{:S(2)}, u32[]{:S(2)}) collective-permute-start(f32[64,128]{1,0:T(8,128)S(1)} %pad_maximum_fusion), channel_id=1, source_target_pairs={{0,32},{8,40},{16,48},{24,56},{32,0},{40,8},{48,16},{56,24},{1,33}... | collective-permute-start | bytes 98312 | tf_op jit(solution)/shard_map/ppermute | solution.py:450
  46.2 10.5 %copy-start.4 = (f32[40,512]{1,0:T(8,128)S(1)}, f32[40,512]{1,0:T(8,128)}, u32[]{:S(2)}) copy-start(f32[40,512]{1,0:T(8,128)} %get-tuple-element.17.own) | copy-start | bytes 245764
  46.2 19.8 %copy-start = (f32[4,2,16,512]{3,2,1,0:T(8,128)S(1)}, f32[4,2,16,512]{3,2,1,0:T(8,128)}, u32[]{:S(2)}) copy-start(f32[4,2,16,512]{3,2,1,0:T(8,128)} %cur.3) | copy-start | bytes 786436
  46.2 19.8 %copy-start.2 = (s32[4,27]{1,0:T(4,128)S(1)}, s32[4,27]{1,0:T(4,128)}, u32[]{:S(2)}) copy-start(s32[4,27]{1,0:T(4,128)} %near.3) | copy-start | bytes 1300
  46.2 44.5 %all-to-all-start.1 = ((f32[16,32,128]{2,1,0:T(8,128)}), f32[16,32,128]{2,1,0:T(8,128)S(1)}, u32[]{:S(2)}, u32[]{:S(2)}) async-start(f32[16,32,128]{2,1,0:T(8,128)} %shard_map.95), calls=%async_computation.1 | async-start | bytes 524288 | tf_op jit(solution)/shard_map/all_to_all | solution.py:427
  56.6 9.3 %copy-start.3 = (s32[4]{0:T(128)S(1)}, s32[4]{0:T(128)}, u32[]{:S(2)}) copy-start(s32[4]{0:T(128)} %count.3) | copy-start | bytes 52
  56.7 9.3 %collective-permute-start.5 = (f32[40,512]{1,0:T(8,128)S(1)}, f32[40,512]{1,0:T(8,128)S(1)}, u32[]{:S(2)}, u32[]{:S(2)}) collective-permute-start(f32[40,512]{1,0:T(8,128)S(1)} %copy-done.4), channel_id=1, source_target_pairs={{4,0},{8,4},{12,8},{16,12},{20,16},{24,20},{28,24},{32,28},{36,32}... | collective-permute-start | bytes 245768 | tf_op jit(solution)/shard_map/ppermute | solution.py:447
  58.7 7.3 %collective-permute-start.4 = (f32[40,512]{1,0:T(8,128)S(1)}, f32[40,512]{1,0:T(8,128)S(1)}, u32[]{:S(2)}, u32[]{:S(2)}) collective-permute-start(f32[40,512]{1,0:T(8,128)S(1)} %copy-done.4), channel_id=1, source_target_pairs={{0,4},{4,8},{8,12},{12,16},{16,20},{20,24},{24,28},{28,32},{32,36}... | collective-permute-start | bytes 245768 | tf_op jit(solution)/shard_map/ppermute | solution.py:446
  72.7 11.7 %collective-permute-start.6 = (f32[136,512]{1,0:T(8,128)S(1)}, f32[136,512]{1,0:T(8,128)S(1)}, u32[]{:S(2)}, u32[]{:S(2)}) collective-permute-start(f32[136,512]{1,0:T(8,128)S(1)} %get-tuple-element.19), channel_id=1, source_target_pairs={{0,1},{1,2},{2,3},{3,0},{4,5},{5,6},{6,7},{7,4},{8,9},{9,10},{10,1... | collective-permute-start | bytes 835592 | tf_op jit(solution)/shard_map/ppermute | solution.py:422
  76.1 11.8 %collective-permute-start.7 = (f32[136,512]{1,0:T(8,128)S(1)}, f32[136,512]{1,0:T(8,128)S(1)}, u32[]{:S(2)}, u32[]{:S(2)}) collective-permute-start(f32[136,512]{1,0:T(8,128)S(1)} %get-tuple-element.20), channel_id=1, source_target_pairs={{0,2},{1,3},{2,0},{3,1},{4,6},{5,7},{6,4},{7,5},{8,10},{9,11},{10,... | collective-permute-start | bytes 835592 | tf_op jit(solution)/shard_map/ppermute | solution.py:422
  80.4 9.3 %collective-permute-start.8 = (f32[136,512]{1,0:T(8,128)S(1)}, f32[136,512]{1,0:T(8,128)S(1)}, u32[]{:S(2)}, u32[]{:S(2)}) collective-permute-start(f32[136,512]{1,0:T(8,128)S(1)} %get-tuple-element.21), channel_id=1, source_target_pairs={{0,3},{1,0},{2,1},{3,2},{4,7},{5,4},{6,5},{7,6},{8,11},{9,8},{10,9... | collective-permute-start | bytes 835592 | tf_op jit(solution)/shard_map/ppermute | solution.py:422
  89.7 1.0 copy-start.1
  131.7 18.4 %all-to-all-start.4 = ((f32[16,40,128]{2,1,0:T(8,128)}), f32[16,40,128]{2,1,0:T(8,128)S(1)}, u32[]{:S(2)}, u32[]{:S(2)}) async-start(f32[16,40,128]{2,1,0:T(8,128)} %broadcast_in_dim.8), calls=%async_computation.4 | async-start | bytes 655360 | tf_op jit(solution)/shard_map/all_to_all | solution.py:427
  136.8 7.8 %collective-permute-start.11 = (f32[64,256]{1,0:T(8,128)S(1)}, f32[64,256]{1,0:T(8,128)S(1)}, u32[]{:S(2)}, u32[]{:S(2)}) collective-permute-start(f32[64,256]{1,0:T(8,128)S(1)} %get-tuple-element.26.refs_0_), channel_id=1, source_target_pairs={{0,3},{1,0},{2,1},{3,2},{4,7},{5,4},{6,5},{7,6},{8,11},{9,8},{10,9... | collective-permute-start | bytes 196616 | tf_op jit(solution)/shard_map/ppermute | solution.py:422
  139.6 6.8 %collective-permute-start.10 = (f32[64,256]{1,0:T(8,128)S(1)}, f32[64,256]{1,0:T(8,128)S(1)}, u32[]{:S(2)}, u32[]{:S(2)}) collective-permute-start(f32[64,256]{1,0:T(8,128)S(1)} %get-tuple-element.26.refs_0_), channel_id=1, source_target_pairs={{0,2},{1,3},{2,0},{3,1},{4,6},{5,7},{6,4},{7,5},{8,10},{9,11},{10,... | collective-permute-start | bytes 196616 | tf_op jit(solution)/shard_map/ppermute | solution.py:422
  142.1 6.5 %collective-permute-start.9 = (f32[64,256]{1,0:T(8,128)S(1)}, f32[64,256]{1,0:T(8,128)S(1)}, u32[]{:S(2)}, u32[]{:S(2)}) collective-permute-start(f32[64,256]{1,0:T(8,128)S(1)} %get-tuple-element.26.refs_0_), channel_id=1, source_target_pairs={{0,1},{1,2},{2,3},{3,0},{4,5},{5,6},{6,7},{7,4},{8,9},{9,10},{10,1... | collective-permute-start | bytes 196616 | tf_op jit(solution)/shard_map/ppermute | solution.py:422

commit v6 on v5

--- a/solution.py
+++ b/solution.py
@@ -142,7 +142,7 @@
     spot = spots[0]
     for b in range(1, BOX_DEV):
         spot = jnp.where(x == b, spots[b], spot)
-    info[...] = jnp.concatenate(
+    about = jnp.concatenate(
         [
             jnp.concatenate([spot[0:3], jnp.zeros((3, PTS - SKEL), F32)], axis=1),
             1.0 - listed[0:3],
@@ -150,6 +150,7 @@
         ],
         axis=0,
     )
+    info[...] = jnp.broadcast_to(about[None], info.shape)
 
 
 def from_x(r):
@@ -248,7 +249,7 @@
         sz = gathered[nx * g, 34:35, :]
         source_group = g * targets + mine
         for d in range(targets):
-            delta = source_group - (first + lax.bitwise_xor(mine, d))
+            delta = source_group - (first + d)
             w = jnp.where(delta == -1, info[8 * d + 3 : 8 * d + 4, :], 1.0)
             w = jnp.where(delta == 0, info[8 * d + 4 : 8 * d + 5, :], w)
             w = jnp.where(delta == 1, info[8 * d + 5 : 8 * d + 6, :], w)
@@ -274,7 +275,7 @@
 
     lax.fori_loop(0, nz, step, 0)
     for d in range(targets):
-        out[lax.bitwise_xor(mine, d)] = acc[SKEL * d : SKEL * d + SKEL, :]
+        out[d] = acc[SKEL * d : SKEL * d + SKEL, :]
 
 
 def halves(rows, nx):
@@ -438,17 +439,14 @@
 
     halo, far, info = call(
         functools.partial(prep_kernel, dims),
-        (shape(40, points), shape(sources, 40, PTS), shape(8, PTS)),
+        (shape(40, points), shape(sources, 40, PTS), shape(targets, 8, PTS)),
         [SMEM, SMEM] + [VMEM] * 5,
         limit=None,
     )(near_boxes, near_count, basis, weights[None], offsets, interp, skeleton)
     far_all = trade(far, ZX)
     prev = lax.ppermute(halo, BOX, [(g, g + 1) for g in range(groups - 1)])
     nxt = lax.ppermute(halo, BOX, [(g + 1, g) for g in range(groups - 1)])
-    steps = [("k", 1, nk)] + [("y", 1 << b, ny) for b in range(ny.bit_length() - 1)]
-    for axis, bit, size in steps:
-        other = lax.ppermute(info, axis, [(i, i ^ bit) for i in range(size)])
-        info = jnp.concatenate([info, other], axis=0)
+    info = trade(info, YK).reshape(targets * 8, PTS)
 
     nears = call(
         functools.partial(near_kernel, dims),

time: 157 us -> 160 us (1.019)
  blocking collectives: 39.3 us -> 83.7 us
  starting transfers between devices: 71.3 us -> 34.3 us
  waiting for transfers between devices: 20.4 us -> 16.1 us
    all_to_all x2 -> x4, blocking collectives: 39.3 us -> 83.7 us  [trade(): return lax.all_to_all(value, axes, split_axis=0, concat_axis=0, tiled=True)]
    all_to_all x3 -> x2, starting transfers between devices: 29.4 us -> 10.9 us  [trade(): return lax.all_to_all(value, axes, split_axis=0, concat_axis=0, tiled=True)]
    ppermute x4 -> x0, starting transfers between devices: 17.7 us -> none  [shards(): other = lax.ppermute(info, axis, [(i, i ^ bit) for i in range(size)])]
    ppermute x4 -> x0, waiting for transfers between devices: 5.01 us -> none  [shards(): other = lax.ppermute(info, axis, [(i, i ^ bit) for i in range(size)])]
  transfers between devices with their start and end apart: 15 -> 10, of which waited for: 11 -> 7; matrix products, arithmetic and copies ran while one was open for 0% -> 0% of each run, Pallas kernels for 5% -> 5%
where the time goes in v6:
time: 160 us
  blocking collectives  83.7 us (52%)
  starting transfers between devices  34.3 us (21%)
  Pallas kernels  23.9 us (15%)
  waiting for transfers between devices  16.1 us (10%)
    all_to_all x4, blocking collectives, trade(): return lax.all_to_all(value, axes, split_axis=0, concat_axis=0, tiled=True)  83.7 us
    ppermute x6, starting transfers between devices, around(): lax.ppermute(blocks[r], 'x', [(i, (i + r) % n) for i in range(n)])  17.8 us
    all_to_all x2, starting transfers between devices, trade(): return lax.all_to_all(value, axes, split_axis=0, concat_axis=0, tiled=True)  10.9 us
    ppermute x6, waiting for transfers between devices, around(): lax.ppermute(blocks[r], 'x', [(i, (i + r) % n) for i in range(n)])  10.9 us
    pallas_call x1, Pallas kernels, shards(): call(functools.partial(near_kernel, dims), (shape(32, PTS),) + (shape(PTS...  6.71 us
    pallas_call x1, Pallas kernels, shards(): call(functools.partial(finish_kernel, nx), (shape(2, 16, points), shape(4...  6.55 us
    pallas_call x1, Pallas kernels, shards(): call(functools.partial(far_kernel, dims), shape(targets, SKEL, 32 * nx),...  6.47 us
    ppermute x1, waiting for transfers between devices, shards(): nxt = lax.ppermute(halo, BOX, [(g + 1, g) for g in range(groups - 1)])  3.71 us
  transfers between devices with their start and end apart: 10, of which 7 were waited for; matrix products, arithmetic and copies ran while one was open for 0% of the time, Pallas kernels for 5%

profile of v6, /device:TPU:1, one launch (start us, length us, event | category | flops | bytes accessed | tf_op | source)
XLA Modules:
  0.0 159.6 jit_solution(13452495052451553874)
XLA Ops:
  0.6 2.4 %shard_map.94 = (f32[40,512]{1,0:T(8,128)}, f32[32,40,128]{2,1,0:T(8,128)}, f32[16,8,128]{2,1,0:T(8,128)}) custom-call(s32[4,27]{1,0:T(4,128)} %near.3, s32[4]{0:T(128)} %count.3, f32[4,2,16,512]{3,2,1,0:T(8,128)} %cur.3, f32[1,512]{1,0:T(1,128)} %bitcast.9, f32[3,512]{1,0:T(4,128)} %offsets.1, f32[4,32,128]{2,1,0:T(8,128)} %interp.3, s32[4,32]{1,0:T(4,128)} %skel.1), custom_call_target="tpu_custom_call" | custom-call | bytes 524288 | tf_op jit(solution)/shard_map/pallas_call | solution.py:440
  3.0 17.9 %all_to_all.30 = f32[16,8,128]{2,1,0:T(8,128)S(1)} all-to-all(f32[16,8,128]{2,1,0:T(8,128)} %get-tuple-element.15), channel_id=1, replica_groups=mesh['z'=8,'y'=8,'k'=2,'x'=4] {'y','k'}, dimensions={0} | all-to-all | bytes 131072 | tf_op jit(solution)/shard_map/all_to_all | solution.py:428
  21.0 30.3 %all_to_all.31.gathered = f32[32,40,128]{2,1,0:T(8,128)S(1)} all-to-all(f32[32,40,128]{2,1,0:T(8,128)} %get-tuple-element.16), channel_id=1, replica_groups=mesh['z'=8,'y'=8,'k'=2,'x'=4] {'z','x'}, dimensions={0} | all-to-all | bytes 1310720 | tf_op jit(solution)/shard_map/all_to_all | solution.py:428
  51.3 6.5 %shard_map.95 = f32[16,32,128]{2,1,0:T(8,128)} custom-call(f32[128,128]{1,0:T(8,128)S(1)} %bitcast.7, f32[32,40,128]{2,1,0:T(8,128)S(1)} %all_to_all.31.gathered), custom_call_target="tpu_custom_call" | custom-call | flops 805306368 | bytes 524288 | tf_op jit(solution)/shard_map/pallas_call | solution.py:470
  57.7 0.0 copy-start.4
  57.7 0.0 copy-start
  57.7 0.0 copy-start.2
  57.7 5.8 %all-to-all-start.2 = ((f32[16,32,128]{2,1,0:T(8,128)}), f32[16,32,128]{2,1,0:T(8,128)S(1)}, u32[]{:S(2)}, u32[]{:S(2)}) async-start(f32[16,32,128]{2,1,0:T(8,128)} %shard_map.95), calls=%async_computation.2 | async-start | bytes 524288 | tf_op jit(solution)/shard_map/all_to_all | solution.py:428
  63.6 0.0 copy-start.3
  63.6 0.0 copy-done.4
  63.6 2.1 %collective-permute-start.1 = (f32[40,512]{1,0:T(8,128)S(1)}, f32[40,512]{1,0:T(8,128)S(1)}, u32[]{:S(2)}, u32[]{:S(2)}) collective-permute-start(f32[40,512]{1,0:T(8,128)S(1)} %copy-done.4), channel_id=1, source_target_pairs={{4,0},{8,4},{12,8},{16,12},{20,16},{24,20},{28,24},{32,28},{36,32}... | collective-permute-start | bytes 245768 | tf_op jit(solution)/shard_map/ppermute | solution.py:448
  65.7 3.4 %collective-permute-start = (f32[40,512]{1,0:T(8,128)S(1)}, f32[40,512]{1,0:T(8,128)S(1)}, u32[]{:S(2)}, u32[]{:S(2)}) collective-permute-start(f32[40,512]{1,0:T(8,128)S(1)} %copy-done.4), channel_id=1, source_target_pairs={{0,4},{4,8},{8,12},{12,16},{16,20},{20,24},{24,28},{28,32},{32,36}... | collective-permute-start | bytes 245768 | tf_op jit(solution)/shard_map/ppermute | solution.py:447
  69.2 3.7 %collective-permute-done.1.nxt = f32[40,512]{1,0:T(8,128)S(1)} collective-permute-done((f32[40,512]{1,0:T(8,128)S(1)}, f32[40,512]{1,0:T(8,128)S(1)}, u32[]{:S(2)}, u32[]{:S(2)}) %collective-permute-start.1) | collective-permute-done | bytes 81952 | tf_op jit(solution)/shard_map/ppermute | solution.py:448
  72.9 0.0 collective-permute-done.prev
  72.9 0.0 copy-done
  72.9 0.0 copy-done.2
  72.9 0.0 copy-done.3
  72.9 6.7 %shard_map.96 = (f32[32,128]{1,0:T(8,128)S(1)}, f32[136,512]{1,0:T(8,128)S(1)}, f32[136,512]{1,0:T(8,128)S(1)}, f32[136,512]{1,0:T(8,128)S(1)}) custom-call(s32[4,27]{1,0:T(4,128)S(1)} %copy-done.2, s32[4]{0:T(128)S(1)} %copy-done.3, f32[40,512]{1,0:T(8,128)S(1)} %collective-permute-done.prev, f32[40,512]{1,0:T(8,128)S(1)} %copy-done.4, ...), custom_call_target="tpu_custom_call" | custom-call | flops 301989888 | bytes 524288 | tf_op jit(solution)/shard_map/pallas_call | solution.py:451
  79.6 2.7 %collective-permute-start.2 = (f32[136,512]{1,0:T(8,128)S(1)}, f32[136,512]{1,0:T(8,128)S(1)}, u32[]{:S(2)}, u32[]{:S(2)}) collective-permute-start(f32[136,512]{1,0:T(8,128)S(1)} %get-tuple-element.19), channel_id=1, source_target_pairs={{0,1},{1,2},{2,3},{3,0},{4,5},{5,6},{6,7},{7,4},{8,9},{9,10},{10,1... | collective-permute-start | bytes 835592 | tf_op jit(solution)/shard_map/ppermute | solution.py:423
  82.3 4.3 %collective-permute-start.3 = (f32[136,512]{1,0:T(8,128)S(1)}, f32[136,512]{1,0:T(8,128)S(1)}, u32[]{:S(2)}, u32[]{:S(2)}) collective-permute-start(f32[136,512]{1,0:T(8,128)S(1)} %get-tuple-element.20), channel_id=1, source_target_pairs={{0,2},{1,3},{2,0},{3,1},{4,6},{5,7},{6,4},{7,5},{8,10},{9,11},{10,... | collective-permute-start | bytes 835592 | tf_op jit(solution)/shard_map/ppermute | solution.py:423
  86.6 3.1 %collective-permute-start.4 = (f32[136,512]{1,0:T(8,128)S(1)}, f32[136,512]{1,0:T(8,128)S(1)}, u32[]{:S(2)}, u32[]{:S(2)}) collective-permute-start(f32[136,512]{1,0:T(8,128)S(1)} %get-tuple-element.21), channel_id=1, source_target_pairs={{0,3},{1,0},{2,1},{3,2},{4,7},{5,4},{6,5},{7,6},{8,11},{9,8},{10,9... | collective-permute-start | bytes 835592 | tf_op jit(solution)/shard_map/ppermute | solution.py:423
  89.7 1.4 collective-permute-done.2.refs_0_
  91.1 3.1 %collective-permute-done.3.refs_1_ = f32[136,512]{1,0:T(8,128)S(1)} collective-permute-done((f32[136,512]{1,0:T(8,128)S(1)}, f32[136,512]{1,0:T(8,128)S(1)}, u32[]{:S(2)}, u32[]{:S(2)}) %collective-permute-start.3) | collective-permute-done | bytes 278560 | tf_op jit(solution)/shard_map/ppermute | solution.py:423
  94.2 2.4 %collective-permute-done.4.refs_2_ = f32[136,512]{1,0:T(8,128)S(1)} collective-permute-done((f32[136,512]{1,0:T(8,128)S(1)}, f32[136,512]{1,0:T(8,128)S(1)}, u32[]{:S(2)}, u32[]{:S(2)}) %collective-permute-start.4) | collective-permute-done | bytes 278560 | tf_op jit(solution)/shard_map/ppermute | solution.py:423
  96.6 0.0 copy-start.1
  96.6 0.9 shard_map.97
  97.5 0.0 all-to-all-done.2.phi
  97.5 0.0 copy-done.1
  97.5 0.8 shard_map.98
  98.4 17.9 %all_to_all.32 = f32[16,16,128]{2,1,0:T(8,128)S(1)} all-to-all(f32[16,16,128]{2,1,0:T(8,128)S(1)} %get-tuple-element.25), channel_id=1, replica_groups=mesh['z'=8,'y'=8,'k'=2,'x'=4] {'y','k'}, dimensions={0} | all-to-all | bytes 262144 | tf_op jit(solution)/shard_map/all_to_all | solution.py:428
  116.3 17.6 %all_to_all.33 = f32[32,16,128]{2,1,0:T(8,128)S(1)} all-to-all(f32[32,16,128]{2,1,0:T(8,128)S(1)} %broadcast_in_dim.7), channel_id=1, replica_groups=mesh['z'=8,'y'=8,'k'=2,'x'=4] {'z','x'}, dimensions={0} | all-to-all | bytes 524288 | tf_op jit(solution)/shard_map/all_to_all | solution.py:428
  133.9 0.7 broadcast_in_dim.8
  134.7 5.1 %all-to-all-start.5 = ((f32[16,40,128]{2,1,0:T(8,128)}), f32[16,40,128]{2,1,0:T(8,128)S(1)}, u32[]{:S(2)}, u32[]{:S(2)}) async-start(f32[16,40,128]{2,1,0:T(8,128)} %broadcast_in_dim.8), calls=%async_computation.5 | async-start | bytes 655360 | tf_op jit(solution)/shard_map/all_to_all | solution.py:428
  139.8 2.8 %collective-permute-start.7 = (f32[64,256]{1,0:T(8,128)S(1)}, f32[64,256]{1,0:T(8,128)S(1)}, u32[]{:S(2)}, u32[]{:S(2)}) collective-permute-start(f32[64,256]{1,0:T(8,128)S(1)} %get-tuple-element.26.refs_0_), channel_id=1, source_target_pairs={{0,3},{1,0},{2,1},{3,2},{4,7},{5,4},{6,5},{7,6},{8,11},{9,8},{10,9... | collective-permute-start | bytes 196616 | tf_op jit(solution)/shard_map/ppermute | solution.py:423
  142.6 2.5 %collective-permute-start.6 = (f32[64,256]{1,0:T(8,128)S(1)}, f32[64,256]{1,0:T(8,128)S(1)}, u32[]{:S(2)}, u32[]{:S(2)}) collective-permute-start(f32[64,256]{1,0:T(8,128)S(1)} %get-tuple-element.26.refs_0_), channel_id=1, source_target_pairs={{0,2},{1,3},{2,0},{3,1},{4,6},{5,7},{6,4},{7,5},{8,10},{9,11},{10,... | collective-permute-start | bytes 196616 | tf_op jit(solution)/shard_map/ppermute | solution.py:423
  145.1 2.5 %collective-permute-start.5 = (f32[64,256]{1,0:T(8,128)S(1)}, f32[64,256]{1,0:T(8,128)S(1)}, u32[]{:S(2)}, u32[]{:S(2)}) collective-permute-start(f32[64,256]{1,0:T(8,128)S(1)} %get-tuple-element.26.refs_0_), channel_id=1, source_target_pairs={{0,1},{1,2},{2,3},{3,0},{4,5},{5,6},{6,7},{7,4},{8,9},{9,10},{10,1... | collective-permute-start | bytes 196616 | tf_op jit(solution)/shard_map/ppermute | solution.py:423
  147.6 0.0 collective-permute-done.7.refs_3_
  147.6 1.8 %collective-permute-done.6.refs_2_ = f32[64,256]{1,0:T(8,128)S(1)} collective-permute-done((f32[64,256]{1,0:T(8,128)S(1)}, f32[64,256]{1,0:T(8,128)S(1)}, u32[]{:S(2)}, u32[]{:S(2)}) %collective-permute-start.6) | collective-permute-done | bytes 65568 | tf_op jit(solution)/shard_map/ppermute | solution.py:423
  149.4 2.2 %collective-permute-done.5.refs_1_ = f32[64,256]{1,0:T(8,128)S(1)} collective-permute-done((f32[64,256]{1,0:T(8,128)S(1)}, f32[64,256]{1,0:T(8,128)S(1)}, u32[]{:S(2)}, u32[]{:S(2)}) %collective-permute-start.5) | collective-permute-done | bytes 65568 | tf_op jit(solution)/shard_map/ppermute | solution.py:423
  151.6 1.5 all-to-all-done.5.summed
  153.0 6.5 %shard_map.99 = (f32[2,16,512]{2,1,0:T(8,128)}, f32[4,64,64]{2,1,0:T(8,128)}, f32[64,64]{1,0:T(8,128)}) custom-call(f32[16,40,128]{2,1,0:T(8,128)S(1)} %all-to-all-done.5.summed, f32[2,256,512]{2,1,0:T(8,128)S(1)} %get-tuple-element.22.ordered, f32[64,256]{1,0:T(8,128)S(1)} %get-tuple-element.26.refs_0_, f32[64,256]{1,0:T(8,128)S(1)} %collective-permute-done.5.refs_1_, ...), custom_call_target="tpu_custom_call" | custom-call | bytes 524288 | tf_op jit(solution)/shard_map/pallas_call | solution.py:502
  (5 shorter events, 0.1 us)
Async XLA Ops:
  57.7 5.8 %copy-start.4 = (f32[40,512]{1,0:T(8,128)S(1)}, f32[40,512]{1,0:T(8,128)}, u32[]{:S(2)}) copy-start(f32[40,512]{1,0:T(8,128)} %get-tuple-element.17.own) | copy-start | bytes 245764
  57.7 15.1 %copy-start = (f32[4,2,16,512]{3,2,1,0:T(8,128)S(1)}, f32[4,2,16,512]{3,2,1,0:T(8,128)}, u32[]{:S(2)}) copy-start(f32[4,2,16,512]{3,2,1,0:T(8,128)} %cur.3) | copy-start | bytes 786436
  57.7 15.1 %copy-start.2 = (s32[4,27]{1,0:T(4,128)S(1)}, s32[4,27]{1,0:T(4,128)}, u32[]{:S(2)}) copy-start(s32[4,27]{1,0:T(4,128)} %near.3) | copy-start | bytes 1300
  57.7 39.8 %all-to-all-start.2 = ((f32[16,32,128]{2,1,0:T(8,128)}), f32[16,32,128]{2,1,0:T(8,128)S(1)}, u32[]{:S(2)}, u32[]{:S(2)}) async-start(f32[16,32,128]{2,1,0:T(8,128)} %shard_map.95), calls=%async_computation.2 | async-start | bytes 524288 | tf_op jit(solution)/shard_map/all_to_all | solution.py:428
  63.6 9.3 %copy-start.3 = (s32[4]{0:T(128)S(1)}, s32[4]{0:T(128)}, u32[]{:S(2)}) copy-start(s32[4]{0:T(128)} %count.3) | copy-start | bytes 52
  63.6 9.3 %collective-permute-start.1 = (f32[40,512]{1,0:T(8,128)S(1)}, f32[40,512]{1,0:T(8,128)S(1)}, u32[]{:S(2)}, u32[]{:S(2)}) collective-permute-start(f32[40,512]{1,0:T(8,128)S(1)} %copy-done.4), channel_id=1, source_target_pairs={{4,0},{8,4},{12,8},{16,12},{20,16},{24,20},{28,24},{32,28},{36,32}... | collective-permute-start | bytes 245768 | tf_op jit(solution)/shard_map/ppermute | solution.py:448
  65.7 7.2 %collective-permute-start = (f32[40,512]{1,0:T(8,128)S(1)}, f32[40,512]{1,0:T(8,128)S(1)}, u32[]{:S(2)}, u32[]{:S(2)}) collective-permute-start(f32[40,512]{1,0:T(8,128)S(1)} %copy-done.4), channel_id=1, source_target_pairs={{0,4},{4,8},{8,12},{12,16},{16,20},{20,24},{24,28},{28,32},{32,36}... | collective-permute-start | bytes 245768 | tf_op jit(solution)/shard_map/ppermute | solution.py:447
  79.6 11.5 %collective-permute-start.2 = (f32[136,512]{1,0:T(8,128)S(1)}, f32[136,512]{1,0:T(8,128)S(1)}, u32[]{:S(2)}, u32[]{:S(2)}) collective-permute-start(f32[136,512]{1,0:T(8,128)S(1)} %get-tuple-element.19), channel_id=1, source_target_pairs={{0,1},{1,2},{2,3},{3,0},{4,5},{5,6},{6,7},{7,4},{8,9},{9,10},{10,1... | collective-permute-start | bytes 835592 | tf_op jit(solution)/shard_map/ppermute | solution.py:423
  82.3 11.9 %collective-permute-start.3 = (f32[136,512]{1,0:T(8,128)S(1)}, f32[136,512]{1,0:T(8,128)S(1)}, u32[]{:S(2)}, u32[]{:S(2)}) collective-permute-start(f32[136,512]{1,0:T(8,128)S(1)} %get-tuple-element.20), channel_id=1, source_target_pairs={{0,2},{1,3},{2,0},{3,1},{4,6},{5,7},{6,4},{7,5},{8,10},{9,11},{10,... | collective-permute-start | bytes 835592 | tf_op jit(solution)/shard_map/ppermute | solution.py:423
  86.6 10.0 %collective-permute-start.4 = (f32[136,512]{1,0:T(8,128)S(1)}, f32[136,512]{1,0:T(8,128)S(1)}, u32[]{:S(2)}, u32[]{:S(2)}) collective-permute-start(f32[136,512]{1,0:T(8,128)S(1)} %get-tuple-element.21), channel_id=1, source_target_pairs={{0,3},{1,0},{2,1},{3,2},{4,7},{5,4},{6,5},{7,6},{8,11},{9,8},{10,9... | collective-permute-start | bytes 835592 | tf_op jit(solution)/shard_map/ppermute | solution.py:423
  96.6 1.0 copy-start.1
  134.7 18.4 %all-to-all-start.5 = ((f32[16,40,128]{2,1,0:T(8,128)}), f32[16,40,128]{2,1,0:T(8,128)S(1)}, u32[]{:S(2)}, u32[]{:S(2)}) async-start(f32[16,40,128]{2,1,0:T(8,128)} %broadcast_in_dim.8), calls=%async_computation.5 | async-start | bytes 655360 | tf_op jit(solution)/shard_map/all_to_all | solution.py:428
  139.8 7.8 %collective-permute-start.7 = (f32[64,256]{1,0:T(8,128)S(1)}, f32[64,256]{1,0:T(8,128)S(1)}, u32[]{:S(2)}, u32[]{:S(2)}) collective-permute-start(f32[64,256]{1,0:T(8,128)S(1)} %get-tuple-element.26.refs_0_), channel_id=1, source_target_pairs={{0,3},{1,0},{2,1},{3,2},{4,7},{5,4},{6,5},{7,6},{8,11},{9,8},{10,9... | collective-permute-start | bytes 196616 | tf_op jit(solution)/shard_map/ppermute | solution.py:423
  142.6 6.8 %collective-permute-start.6 = (f32[64,256]{1,0:T(8,128)S(1)}, f32[64,256]{1,0:T(8,128)S(1)}, u32[]{:S(2)}, u32[]{:S(2)}) collective-permute-start(f32[64,256]{1,0:T(8,128)S(1)} %get-tuple-element.26.refs_0_), channel_id=1, source_target_pairs={{0,2},{1,3},{2,0},{3,1},{4,6},{5,7},{6,4},{7,5},{8,10},{9,11},{10,... | collective-permute-start | bytes 196616 | tf_op jit(solution)/shard_map/ppermute | solution.py:423
  145.1 6.5 %collective-permute-start.5 = (f32[64,256]{1,0:T(8,128)S(1)}, f32[64,256]{1,0:T(8,128)S(1)}, u32[]{:S(2)}, u32[]{:S(2)}) collective-permute-start(f32[64,256]{1,0:T(8,128)S(1)} %get-tuple-element.26.refs_0_), channel_id=1, source_target_pairs={{0,1},{1,2},{2,3},{3,0},{4,5},{5,6},{6,7},{7,4},{8,9},{9,10},{10,1... | collective-permute-start | bytes 196616 | tf_op jit(solution)/shard_map/ppermute | solution.py:423

commit v7 on v4

--- a/solution.py
+++ b/solution.py
@@ -29,6 +29,7 @@
 ZX = ("z", "x")
 
 TURNS = WAVENUMBER / (2.0 * math.pi)
+SCALE = TURNS / (4.0 * math.pi)
 SIN_C = (3.1415926401307073, -5.167710083507923, 2.5500775232148563, -0.5982912856211671, 0.07765766030589402)
 COS_C = (
     0.9999999997799043,
@@ -51,10 +52,9 @@
     dx = tx - sx
     dy = ty - sy
     dz = tz - sz
-    s = SMOOTHING * SMOOTHING + dx * dx + dy * dy + dz * dz
+    s = (SMOOTHING * TURNS) ** 2 + dx * dx + dy * dy + dz * dz
     r = lax.rsqrt(s)
-    r = r * (1.5 - (0.5 * s) * (r * r))
-    t = (s * r) * TURNS
+    t = s * r
     f = t - lax.round(t, lax.RoundingMethod.TO_NEAREST_EVEN)
     u = f * f
     sn = f * poly(SIN_C, u)
@@ -178,7 +178,9 @@
     erow = lax.broadcasted_iota(jnp.int32, (16, PTS), 0)
     for t in range(BOX_DEV):
         for c in range(3):
-            tpos[t, c] = jnp.broadcast_to(turned[:, 8 * t + c : 8 * t + c + 1], (PTS, PTS))
+            tpos[t, c] = TURNS * jnp.broadcast_to(
+                turned[:, 8 * t + c : 8 * t + c + 1], (PTS, PTS)
+            )
         m = jnp.zeros((16, PTS), F32)
         for s in range(SLOTS):
             box = jnp.where(s < count[t], near[t, s] - base, -1000)
@@ -194,10 +196,10 @@
                 tpos[t, 0],
                 tpos[t, 1],
                 tpos[t, 2],
-                ext[e, 32:33, :],
-                ext[e, 33:34, :],
-                ext[e, 34:35, :],
-                0.25 / math.pi,
+                TURNS * ext[e, 32:33, :],
+                TURNS * ext[e, 33:34, :],
+                TURNS * ext[e, 34:35, :],
+                SCALE,
             )
             khi, klo = split(jnp.concatenate([re, im], axis=1))
             rhi, rlo = split(jnp.concatenate([rows, rotate(rows)], axis=1))
@@ -224,22 +226,22 @@
         )
 
 
-def far_kernel(dims, info, far_z, far_x, out, tpos, rhi, rlo, weight, acc):
+def far_kernel(dims, info, gathered, out, tpos, rhi, rlo, weight, acc):
     nz, ny, nk, nx = dims
     targets = ny * nk
     mine = lax.axis_index("y") * nk + lax.axis_index("k")
     first = lax.axis_index("z") * targets
-    stack = jnp.concatenate([info[d] for d in range(targets)], axis=0)
+    stack = info[...]
     if targets * 8 < PTS:
         stack = jnp.concatenate([stack, jnp.zeros((PTS - targets * 8, PTS), F32)], axis=0)
     turned = stack.T
     for d in range(targets):
         for c in range(3):
-            tpos[c, SKEL * d : SKEL * d + SKEL, :] = jnp.broadcast_to(
+            tpos[c, SKEL * d : SKEL * d + SKEL, :] = TURNS * jnp.broadcast_to(
                 turned[0:SKEL, 8 * d + c : 8 * d + c + 1], (SKEL, PTS)
             )
     for g in range(nz):
-        rows = jnp.concatenate([far_x[c, g] for c in range(nx)], axis=0)
+        rows = jnp.concatenate([gathered[nx * g + c, 0:32, :] for c in range(nx)], axis=0)
         hi, lo = split(jnp.concatenate([rows, rotate(rows)], axis=1))
         rhi[g] = hi
         rlo[g] = lo
@@ -247,17 +249,17 @@
     per = min(4, targets)
 
     def step(g, carry):
-        sx = far_z[g, 32:33, :]
-        sy = far_z[g, 33:34, :]
-        sz = far_z[g, 34:35, :]
+        sx = TURNS * gathered[nx * g, 32:33, :]
+        sy = TURNS * gathered[nx * g, 33:34, :]
+        sz = TURNS * gathered[nx * g, 34:35, :]
         source_group = g * targets + mine
         for d in range(targets):
             delta = source_group - (first + d)
-            w = jnp.where(delta == -1, info[d, 3:4, :], 1.0)
-            w = jnp.where(delta == 0, info[d, 4:5, :], w)
-            w = jnp.where(delta == 1, info[d, 5:6, :], w)
+            w = jnp.where(delta == -1, info[8 * d + 3 : 8 * d + 4, :], 1.0)
+            w = jnp.where(delta == 0, info[8 * d + 4 : 8 * d + 5, :], w)
+            w = jnp.where(delta == 1, info[8 * d + 5 : 8 * d + 6, :], w)
             weight[SKEL * d : SKEL * d + SKEL, :] = jnp.broadcast_to(
-                w * (0.25 / math.pi), (SKEL, PTS)
+                w * SCALE, (SKEL, PTS)
             )
         for n in range(targets // per):
             span = slice(SKEL * per * n, SKEL * per * (n + 1))
@@ -388,22 +390,28 @@
     trace = jnp.sum(jnp.sum(diag, axis=1, keepdims=True), axis=0, keepdims=True)
     g = g + jnp.where(eye, SHIFT_SCALE * trace / 64.0 + EPSILON, 0.0)
     m = jnp.concatenate([g, eye.astype(F32)], axis=1)
-    sub = lax.broadcasted_iota(jnp.int32, (64, 1), 0)
+    tiles = [m[8 * i : 8 * i + 8] for i in range(8)]
+    sub = lax.broadcasted_iota(jnp.int32, (8, 1), 0)
     for j in range(0, 64, 2):
-        one = m[j : j + 1, :]
-        two = m[j + 1 : j + 2, :]
-        c1 = jnp.broadcast_to(m[:, j : j + 1], m.shape)
-        c2 = jnp.broadcast_to(m[:, j + 1 : j + 2], m.shape)
-        p1, a = c1[j : j + 1], c1[j + 1 : j + 2]
-        p2 = c2[j + 1 : j + 2]
+        at, top = divmod(j, 8)
+        ones = [jnp.broadcast_to(tile[:, j : j + 1], (8, PTS)) for tile in tiles[at:]]
+        twos = [jnp.broadcast_to(tile[:, j + 1 : j + 2], (8, PTS)) for tile in tiles[at:]]
+        one = tiles[at][top : top + 1]
+        two = tiles[at][top + 1 : top + 2]
+        p1, a = ones[0][top : top + 1], ones[0][top + 1 : top + 2]
+        p2 = twos[0][top + 1 : top + 2]
         det = p1 * p2 - a * a
         r1 = 1.0 / p1
         q = p1 / det
-        lower = a * r1
-        f1 = c1 * r1
-        f2 = jnp.where(sub > j + 1, (c2 - f1 * a) * q, 0.0)
-        f1 = jnp.where(sub > j, f1, 0.0)
-        m = m - f1 * one - f2 * (two - lower * one)
+        two = two - (a * r1) * one
+        for i, (c1, c2) in enumerate(zip(ones, twos)):
+            f1 = c1 * r1
+            f2 = (c2 - f1 * a) * q
+            if i == 0:
+                f1 = jnp.where(sub > top, f1, 0.0)
+                f2 = jnp.where(sub > top + 1, f2, 0.0)
+            tiles[at + i] = tiles[at + i] - f1 * one - f2 * two
+    m = jnp.concatenate(tiles, axis=0)
     pivots = jnp.sum(jnp.where(eye, m[:, 0:64], 0.0), axis=1, keepdims=True)
     m = m * (1.0 / jnp.sqrt(pivots))
     factor[...] = jnp.where(row <= col, m[:, 0:64], 0.0)
@@ -446,17 +454,16 @@
         [SMEM, SMEM, VMEM, VMEM],
         limit=None,
     )(near_boxes, near_count, offsets, skeleton)
-    info_all = trade(info, YK)
+    info = trade(info, YK).reshape(targets * 8, PTS)
     halo, far = call(
         functools.partial(prep_kernel, dims),
-        (shape(40, points), shape(nz, 40, PTS)),
+        (shape(40, points), shape(sources, 40, PTS)),
         [VMEM] * 5,
         limit=None,
     )(basis, weights[None], offsets, interp, skelpos)
-    far_z = trade(far, "z")
     prev = lax.ppermute(halo, BOX, [(g, g + 1) for g in range(groups - 1)])
     nxt = lax.ppermute(halo, BOX, [(g + 1, g) for g in range(groups - 1)])
-    far_x = trade(jnp.broadcast_to(far_z[None, :, :32], (nx, nz, 32, PTS)), "x")
+    far_all = trade(far, ZX)
 
     nears = call(
         functools.partial(near_kernel, dims),
@@ -480,7 +487,7 @@
     far_part = call(
         functools.partial(far_kernel, dims),
         shape(targets, SKEL, 32 * nx),
-        [VMEM] * 3,
+        [VMEM] * 2,
         [
             pltpu.VMEM((3, SKEL * targets, PTS), F32),
             pltpu.VMEM((nz, 32 * nx, 2 * PTS), BF16),
@@ -489,7 +496,7 @@
             pltpu.VMEM((SKEL * targets, 32 * nx), F32),
         ],
         flops=3 * 2 * 512 * 2048 * 128,
-    )(info_all, far_z, far_x)
+    )(info, far_all)
     phi = trade(far_part, YK)
 
     lead = 128 // targets
@@ -501,8 +508,8 @@
     )(phi, interp, ordered, near_rows, blocks)
     part = jnp.sum(trade(part, YK), axis=0)
     applied = around([applied] * nx)
-    part = trade(jnp.broadcast_to(part[None], (sources, tall, PTS)), ZX)
-    part = jnp.sum(part.reshape(nz, nx, tall, PTS), axis=0)
+    part = jnp.sum(trade(jnp.broadcast_to(part[None], (nz, tall, PTS)), "z"), axis=0)
+    part = trade(jnp.broadcast_to(part[None], (nx, tall, PTS)), "x")
     part = jnp.concatenate(
         [jnp.sum(part[:, :lead], axis=0), part[:, lead:].reshape(nx * (tall - lead), PTS)],
         axis=0,

time: 160 us -> 160 us (level)
  starting transfers between devices: 41.2 us -> 45.6 us
  waiting for transfers between devices: 25.4 us -> 21.7 us
    all_to_all x3, starting transfers between devices: 19.4 us -> 22.2 us  [trade(): return lax.all_to_all(value, axes, split_axis=0, concat_axis=0, tiled=True)]
    all_to_all x3, waiting for transfers between devices: 9.21 us -> 6.8 us  [trade(): return lax.all_to_all(value, axes, split_axis=0, concat_axis=0, tiled=True)]
    ppermute x6, starting transfers between devices: 16.2 us -> 17.8 us  [around(): lax.ppermute(blocks[r], 'x', [(i, (i + r) % n) for i in range(n)])]
  transfers between devices with their start and end apart: 11 -> 11, of which waited for: 7 -> 8; matrix products, arithmetic and copies ran while one was open for 0% -> 0% of each run, Pallas kernels for 5% -> 6%
where the time goes in v7:
time: 160 us; the launch traced here: 159 us
  blocking collectives  66 us (41%)
  starting transfers between devices  45.6 us (28%)
  Pallas kernels  24.5 us (15%)
  waiting for transfers between devices  21.7 us (14%)
    all_to_all x4, blocking collectives, trade(): return lax.all_to_all(value, axes, split_axis=0, concat_axis=0, tiled=True)  66 us
    all_to_all x3, starting transfers between devices, trade(): return lax.all_to_all(value, axes, split_axis=0, concat_axis=0, tiled=True)  22.2 us
    ppermute x6, starting transfers between devices, around(): lax.ppermute(blocks[r], 'x', [(i, (i + r) % n) for i in range(n)])  17.8 us
    ppermute x6, waiting for transfers between devices, around(): lax.ppermute(blocks[r], 'x', [(i, (i + r) % n) for i in range(n)])  11.2 us
    all_to_all x3, waiting for transfers between devices, trade(): return lax.all_to_all(value, axes, split_axis=0, concat_axis=0, tiled=True)  6.8 us
    pallas_call x1, Pallas kernels, shards(): call(functools.partial(finish_kernel, nx), (shape(2, 16, points), shape(4...  6.51 us
    pallas_call x1, Pallas kernels, shards(): call(functools.partial(near_kernel, dims), (shape(32, PTS),) + (shape(PTS...  6.25 us
    pallas_call x1, Pallas kernels, shards(): call(functools.partial(far_kernel, dims), shape(targets, SKEL, 32 * nx),...  6.13 us
  transfers between devices with their start and end apart: 11, of which 8 were waited for; matrix products, arithmetic and copies ran while one was open for 0% of the time, Pallas kernels for 6%

profile of v7, /device:TPU:1, one launch (start us, length us, event | category | flops | bytes accessed | tf_op | source)
XLA Modules:
  0.0 159.4 jit_solution(6446293416747330999)
XLA Ops:
  0.6 1.7 %shard_map.94 = (f32[16,8,128]{2,1,0:T(8,128)}, f32[8,128]{1,0:T(8,128)}) custom-call(s32[4,27]{1,0:T(4,128)} %near.3, s32[4]{0:T(128)} %count.3, f32[3,512]{1,0:T(4,128)} %offsets.3, s32[4,32]{1,0:T(4,128)} %skel.1), custom_call_target="tpu_custom_call" | custom-call | bytes 524288 | tf_op jit(solution)/shard_map/pallas_call | solution.py:451
  2.3 10.1 %all-to-all-start = ((f32[16,8,128]{2,1,0:T(8,128)}), f32[16,8,128]{2,1,0:T(8,128)S(1)}, u32[]{:S(2)}, u32[]{:S(2)}) async-start(f32[16,8,128]{2,1,0:T(8,128)} %get-tuple-element.16), calls=%async_computation | async-start | bytes 131072 | tf_op jit(solution)/shard_map/all_to_all | solution.py:439
  12.5 2.2 %shard_map.95 = (f32[40,512]{1,0:T(8,128)}, f32[32,40,128]{2,1,0:T(8,128)}) custom-call(f32[4,2,16,512]{3,2,1,0:T(8,128)} %cur.3, f32[1,512]{1,0:T(1,128)} %bitcast.7, f32[3,512]{1,0:T(4,128)} %offsets.3, f32[4,32,128]{2,1,0:T(8,128)} %interp.3, f32[8,128]{1,0:T(8,128)} %get-tuple-element.17.skelpos), custom_call_target="tpu_custom_call" | custom-call | bytes 524288 | tf_op jit(solution)/shard_map/pallas_call | solution.py:458
  14.6 5.6 %all-to-all-done = f32[16,8,128]{2,1,0:T(8,128)S(1)} async-done(((f32[16,8,128]{2,1,0:T(8,128)}), f32[16,8,128]{2,1,0:T(8,128)S(1)}, u32[]{:S(2)}, u32[]{:S(2)}) %all-to-all-start) | async-done | bytes 65568 | tf_op jit(solution)/shard_map/all_to_all | solution.py:439
  20.3 30.3 %all_to_all.35.gathered = f32[32,40,128]{2,1,0:T(8,128)S(1)} all-to-all(f32[32,40,128]{2,1,0:T(8,128)} %get-tuple-element.18), channel_id=1, replica_groups=mesh['z'=8,'y'=8,'k'=2,'x'=4] {'z','x'}, dimensions={0} | all-to-all | bytes 1310720 | tf_op jit(solution)/shard_map/all_to_all | solution.py:439
  50.6 6.1 %shard_map.96 = f32[16,32,128]{2,1,0:T(8,128)} custom-call(f32[128,128]{1,0:T(8,128)S(1)} %bitcast.6, f32[32,40,128]{2,1,0:T(8,128)S(1)} %all_to_all.35.gathered), custom_call_target="tpu_custom_call" | custom-call | flops 805306368 | bytes 524288 | tf_op jit(solution)/shard_map/pallas_call | solution.py:487
  56.7 0.0 copy-start.4
  56.7 0.0 copy-start
  56.7 0.0 copy-start.2
  56.7 5.8 %all-to-all-start.2 = ((f32[16,32,128]{2,1,0:T(8,128)}), f32[16,32,128]{2,1,0:T(8,128)S(1)}, u32[]{:S(2)}, u32[]{:S(2)}) async-start(f32[16,32,128]{2,1,0:T(8,128)} %shard_map.96), calls=%async_computation.2 | async-start | bytes 524288 | tf_op jit(solution)/shard_map/all_to_all | solution.py:439
  62.5 0.0 copy-start.3
  62.5 0.0 copy-done.4
  62.6 2.1 %collective-permute-start.1 = (f32[40,512]{1,0:T(8,128)S(1)}, f32[40,512]{1,0:T(8,128)S(1)}, u32[]{:S(2)}, u32[]{:S(2)}) collective-permute-start(f32[40,512]{1,0:T(8,128)S(1)} %copy-done.4), channel_id=1, source_target_pairs={{4,0},{8,4},{12,8},{16,12},{20,16},{24,20},{28,24},{32,28},{36,32}... | collective-permute-start | bytes 245768 | tf_op jit(solution)/shard_map/ppermute | solution.py:465
  64.7 3.4 %collective-permute-start = (f32[40,512]{1,0:T(8,128)S(1)}, f32[40,512]{1,0:T(8,128)S(1)}, u32[]{:S(2)}, u32[]{:S(2)}) collective-permute-start(f32[40,512]{1,0:T(8,128)S(1)} %copy-done.4), channel_id=1, source_target_pairs={{0,4},{4,8},{8,12},{12,16},{16,20},{20,24},{24,28},{28,32},{32,36}... | collective-permute-start | bytes 245768 | tf_op jit(solution)/shard_map/ppermute | solution.py:464
  68.1 3.7 %collective-permute-done.1.nxt = f32[40,512]{1,0:T(8,128)S(1)} collective-permute-done((f32[40,512]{1,0:T(8,128)S(1)}, f32[40,512]{1,0:T(8,128)S(1)}, u32[]{:S(2)}, u32[]{:S(2)}) %collective-permute-start.1) | collective-permute-done | bytes 81952 | tf_op jit(solution)/shard_map/ppermute | solution.py:465
  71.8 0.0 collective-permute-done.prev
  71.8 0.0 copy-done
  71.9 0.0 copy-done.2
  71.9 0.0 copy-done.3
  71.9 6.2 %shard_map.97 = (f32[32,128]{1,0:T(8,128)S(1)}, f32[136,512]{1,0:T(8,128)S(1)}, f32[136,512]{1,0:T(8,128)S(1)}, f32[136,512]{1,0:T(8,128)S(1)}) custom-call(s32[4,27]{1,0:T(4,128)S(1)} %copy-done.2, s32[4]{0:T(128)S(1)} %copy-done.3, f32[40,512]{1,0:T(8,128)S(1)} %collective-permute-done.prev, f32[40,512]{1,0:T(8,128)S(1)} %copy-done.4, ...), custom_call_target="tpu_custom_call" | custom-call | flops 301989888 | bytes 524288 | tf_op jit(solution)/shard_map/pallas_call | solution.py:468
  78.1 2.7 %collective-permute-start.2 = (f32[136,512]{1,0:T(8,128)S(1)}, f32[136,512]{1,0:T(8,128)S(1)}, u32[]{:S(2)}, u32[]{:S(2)}) collective-permute-start(f32[136,512]{1,0:T(8,128)S(1)} %get-tuple-element.21), channel_id=1, source_target_pairs={{0,1},{1,2},{2,3},{3,0},{4,5},{5,6},{6,7},{7,4},{8,9},{9,10},{10,1... | collective-permute-start | bytes 835592 | tf_op jit(solution)/shard_map/ppermute | solution.py:434
  80.8 4.3 %collective-permute-start.3 = (f32[136,512]{1,0:T(8,128)S(1)}, f32[136,512]{1,0:T(8,128)S(1)}, u32[]{:S(2)}, u32[]{:S(2)}) collective-permute-start(f32[136,512]{1,0:T(8,128)S(1)} %get-tuple-element.22), channel_id=1, source_target_pairs={{0,2},{1,3},{2,0},{3,1},{4,6},{5,7},{6,4},{7,5},{8,10},{9,11},{10,... | collective-permute-start | bytes 835592 | tf_op jit(solution)/shard_map/ppermute | solution.py:434
  85.1 3.1 %collective-permute-start.4 = (f32[136,512]{1,0:T(8,128)S(1)}, f32[136,512]{1,0:T(8,128)S(1)}, u32[]{:S(2)}, u32[]{:S(2)}) collective-permute-start(f32[136,512]{1,0:T(8,128)S(1)} %get-tuple-element.23), channel_id=1, source_target_pairs={{0,3},{1,0},{2,1},{3,2},{4,7},{5,4},{6,5},{7,6},{8,11},{9,8},{10,9... | collective-permute-start | bytes 835592 | tf_op jit(solution)/shard_map/ppermute | solution.py:434
  88.2 1.4 collective-permute-done.2.refs_0_
  89.6 3.1 %collective-permute-done.3.refs_1_ = f32[136,512]{1,0:T(8,128)S(1)} collective-permute-done((f32[136,512]{1,0:T(8,128)S(1)}, f32[136,512]{1,0:T(8,128)S(1)}, u32[]{:S(2)}, u32[]{:S(2)}) %collective-permute-start.3) | collective-permute-done | bytes 278560 | tf_op jit(solution)/shard_map/ppermute | solution.py:434
  92.7 2.4 %collective-permute-done.4.refs_2_ = f32[136,512]{1,0:T(8,128)S(1)} collective-permute-done((f32[136,512]{1,0:T(8,128)S(1)}, f32[136,512]{1,0:T(8,128)S(1)}, u32[]{:S(2)}, u32[]{:S(2)}) %collective-permute-start.4) | collective-permute-done | bytes 278560 | tf_op jit(solution)/shard_map/ppermute | solution.py:434
  95.1 0.0 copy-start.1
  95.1 0.9 shard_map.98
  96.0 0.0 all-to-all-done.2.phi
  96.0 0.0 copy-done.1
  96.1 0.8 shard_map.99
  96.9 17.9 %all_to_all.36 = f32[16,16,128]{2,1,0:T(8,128)S(1)} all-to-all(f32[16,16,128]{2,1,0:T(8,128)S(1)} %get-tuple-element.27), channel_id=1, replica_groups=mesh['z'=8,'y'=8,'k'=2,'x'=4] {'y','k'}, dimensions={0} | all-to-all | bytes 262144 | tf_op jit(solution)/shard_map/all_to_all | solution.py:439
  114.8 10.0 %all_to_all.37 = f32[8,16,128]{2,1,0:T(8,128)S(1)} all-to-all(f32[8,16,128]{2,1,0:T(8,128)S(1)} %broadcast_in_dim.9), channel_id=1, replica_groups=mesh['z'=8,'y'=8,'k'=2,'x'=4] {'z'}, dimensions={0} | all-to-all | bytes 131072 | tf_op jit(solution)/shard_map/all_to_all | solution.py:439
  124.9 7.8 %all_to_all.38 = f32[4,16,128]{2,1,0:T(8,128)S(1)} all-to-all(f32[4,16,128]{2,1,0:T(8,128)S(1)} %broadcast_in_dim.10), channel_id=1, replica_groups=mesh['z'=8,'y'=8,'k'=2,'x'=4] {'x'}, dimensions={0} | all-to-all | bytes 65536 | tf_op jit(solution)/shard_map/all_to_all | solution.py:439
  132.6 0.7 broadcast_in_dim.11
  133.4 6.2 %all-to-all-start.6 = ((f32[16,40,128]{2,1,0:T(8,128)}), f32[16,40,128]{2,1,0:T(8,128)S(1)}, u32[]{:S(2)}, u32[]{:S(2)}) async-start(f32[16,40,128]{2,1,0:T(8,128)} %broadcast_in_dim.11), calls=%async_computation.6 | async-start | bytes 655360 | tf_op jit(solution)/shard_map/all_to_all | solution.py:439
  139.6 2.8 %collective-permute-start.7 = (f32[64,256]{1,0:T(8,128)S(1)}, f32[64,256]{1,0:T(8,128)S(1)}, u32[]{:S(2)}, u32[]{:S(2)}) collective-permute-start(f32[64,256]{1,0:T(8,128)S(1)} %get-tuple-element.28.refs_0_), channel_id=1, source_target_pairs={{0,3},{1,0},{2,1},{3,2},{4,7},{5,4},{6,5},{7,6},{8,11},{9,8},{10,9... | collective-permute-start | bytes 196616 | tf_op jit(solution)/shard_map/ppermute | solution.py:434
  142.4 3.1 %collective-permute-start.6 = (f32[64,256]{1,0:T(8,128)S(1)}, f32[64,256]{1,0:T(8,128)S(1)}, u32[]{:S(2)}, u32[]{:S(2)}) collective-permute-start(f32[64,256]{1,0:T(8,128)S(1)} %get-tuple-element.28.refs_0_), channel_id=1, source_target_pairs={{0,2},{1,3},{2,0},{3,1},{4,6},{5,7},{6,4},{7,5},{8,10},{9,11},{10,... | collective-permute-start | bytes 196616 | tf_op jit(solution)/shard_map/ppermute | solution.py:434
  145.5 1.9 %collective-permute-start.5 = (f32[64,256]{1,0:T(8,128)S(1)}, f32[64,256]{1,0:T(8,128)S(1)}, u32[]{:S(2)}, u32[]{:S(2)}) collective-permute-start(f32[64,256]{1,0:T(8,128)S(1)} %get-tuple-element.28.refs_0_), channel_id=1, source_target_pairs={{0,1},{1,2},{2,3},{3,0},{4,5},{5,6},{6,7},{7,4},{8,9},{9,10},{10,1... | collective-permute-start | bytes 196616 | tf_op jit(solution)/shard_map/ppermute | solution.py:434
  147.4 0.0 collective-permute-done.7.refs_3_
  147.4 1.8 %collective-permute-done.6.refs_2_ = f32[64,256]{1,0:T(8,128)S(1)} collective-permute-done((f32[64,256]{1,0:T(8,128)S(1)}, f32[64,256]{1,0:T(8,128)S(1)}, u32[]{:S(2)}, u32[]{:S(2)}) %collective-permute-start.6) | collective-permute-done | bytes 65568 | tf_op jit(solution)/shard_map/ppermute | solution.py:434
  149.2 2.5 %collective-permute-done.5.refs_1_ = f32[64,256]{1,0:T(8,128)S(1)} collective-permute-done((f32[64,256]{1,0:T(8,128)S(1)}, f32[64,256]{1,0:T(8,128)S(1)}, u32[]{:S(2)}, u32[]{:S(2)}) %collective-permute-start.5) | collective-permute-done | bytes 65568 | tf_op jit(solution)/shard_map/ppermute | solution.py:434
  151.7 1.2 all-to-all-done.6.summed
  152.9 6.5 %shard_map.100 = (f32[2,16,512]{2,1,0:T(8,128)}, f32[4,64,64]{2,1,0:T(8,128)}, f32[64,64]{1,0:T(8,128)}) custom-call(f32[16,40,128]{2,1,0:T(8,128)S(1)} %all-to-all-done.6.summed, f32[2,256,512]{2,1,0:T(8,128)S(1)} %get-tuple-element.24.ordered, f32[64,256]{1,0:T(8,128)S(1)} %get-tuple-element.28.refs_0_, f32[64,256]{1,0:T(8,128)S(1)} %collective-permute-done.5.refs_1_, ...), custom_call_target="tpu_custom_call" | custom-call | bytes 524288 | tf_op jit(solution)/shard_map/pallas_call | solution.py:519
  (6 shorter events, 0.1 us)
Async XLA Ops:
  2.3 18.0 %all-to-all-start = ((f32[16,8,128]{2,1,0:T(8,128)}), f32[16,8,128]{2,1,0:T(8,128)S(1)}, u32[]{:S(2)}, u32[]{:S(2)}) async-start(f32[16,8,128]{2,1,0:T(8,128)} %get-tuple-element.16), calls=%async_computation | async-start | bytes 131072 | tf_op jit(solution)/shard_map/all_to_all | solution.py:439
  56.7 5.8 %copy-start.4 = (f32[40,512]{1,0:T(8,128)S(1)}, f32[40,512]{1,0:T(8,128)}, u32[]{:S(2)}) copy-start(f32[40,512]{1,0:T(8,128)} %get-tuple-element.19.own) | copy-start | bytes 245764
  56.7 15.1 %copy-start = (f32[4,2,16,512]{3,2,1,0:T(8,128)S(1)}, f32[4,2,16,512]{3,2,1,0:T(8,128)}, u32[]{:S(2)}) copy-start(f32[4,2,16,512]{3,2,1,0:T(8,128)} %cur.3) | copy-start | bytes 786436
  56.7 15.1 %copy-start.2 = (s32[4,27]{1,0:T(4,128)S(1)}, s32[4,27]{1,0:T(4,128)}, u32[]{:S(2)}) copy-start(s32[4,27]{1,0:T(4,128)} %near.3) | copy-start | bytes 1300
  56.7 39.3 %all-to-all-start.2 = ((f32[16,32,128]{2,1,0:T(8,128)}), f32[16,32,128]{2,1,0:T(8,128)S(1)}, u32[]{:S(2)}, u32[]{:S(2)}) async-start(f32[16,32,128]{2,1,0:T(8,128)} %shard_map.96), calls=%async_computation.2 | async-start | bytes 524288 | tf_op jit(solution)/shard_map/all_to_all | solution.py:439
  62.5 9.3 %copy-start.3 = (s32[4]{0:T(128)S(1)}, s32[4]{0:T(128)}, u32[]{:S(2)}) copy-start(s32[4]{0:T(128)} %count.3) | copy-start | bytes 52
  62.6 9.3 %collective-permute-start.1 = (f32[40,512]{1,0:T(8,128)S(1)}, f32[40,512]{1,0:T(8,128)S(1)}, u32[]{:S(2)}, u32[]{:S(2)}) collective-permute-start(f32[40,512]{1,0:T(8,128)S(1)} %copy-done.4), channel_id=1, source_target_pairs={{4,0},{8,4},{12,8},{16,12},{20,16},{24,20},{28,24},{32,28},{36,32}... | collective-permute-start | bytes 245768 | tf_op jit(solution)/shard_map/ppermute | solution.py:465
  64.7 7.2 %collective-permute-start = (f32[40,512]{1,0:T(8,128)S(1)}, f32[40,512]{1,0:T(8,128)S(1)}, u32[]{:S(2)}, u32[]{:S(2)}) collective-permute-start(f32[40,512]{1,0:T(8,128)S(1)} %copy-done.4), channel_id=1, source_target_pairs={{0,4},{4,8},{8,12},{12,16},{16,20},{20,24},{24,28},{28,32},{32,36}... | collective-permute-start | bytes 245768 | tf_op jit(solution)/shard_map/ppermute | solution.py:464
  78.1 11.5 %collective-permute-start.2 = (f32[136,512]{1,0:T(8,128)S(1)}, f32[136,512]{1,0:T(8,128)S(1)}, u32[]{:S(2)}, u32[]{:S(2)}) collective-permute-start(f32[136,512]{1,0:T(8,128)S(1)} %get-tuple-element.21), channel_id=1, source_target_pairs={{0,1},{1,2},{2,3},{3,0},{4,5},{5,6},{6,7},{7,4},{8,9},{9,10},{10,1... | collective-permute-start | bytes 835592 | tf_op jit(solution)/shard_map/ppermute | solution.py:434
  80.8 11.9 %collective-permute-start.3 = (f32[136,512]{1,0:T(8,128)S(1)}, f32[136,512]{1,0:T(8,128)S(1)}, u32[]{:S(2)}, u32[]{:S(2)}) collective-permute-start(f32[136,512]{1,0:T(8,128)S(1)} %get-tuple-element.22), channel_id=1, source_target_pairs={{0,2},{1,3},{2,0},{3,1},{4,6},{5,7},{6,4},{7,5},{8,10},{9,11},{10,... | collective-permute-start | bytes 835592 | tf_op jit(solution)/shard_map/ppermute | solution.py:434
  85.1 10.0 %collective-permute-start.4 = (f32[136,512]{1,0:T(8,128)S(1)}, f32[136,512]{1,0:T(8,128)S(1)}, u32[]{:S(2)}, u32[]{:S(2)}) collective-permute-start(f32[136,512]{1,0:T(8,128)S(1)} %get-tuple-element.23), channel_id=1, source_target_pairs={{0,3},{1,0},{2,1},{3,2},{4,7},{5,4},{6,5},{7,6},{8,11},{9,8},{10,9... | collective-permute-start | bytes 835592 | tf_op jit(solution)/shard_map/ppermute | solution.py:434
  95.1 1.0 copy-start.1
  133.4 19.5 %all-to-all-start.6 = ((f32[16,40,128]{2,1,0:T(8,128)}), f32[16,40,128]{2,1,0:T(8,128)S(1)}, u32[]{:S(2)}, u32[]{:S(2)}) async-start(f32[16,40,128]{2,1,0:T(8,128)} %broadcast_in_dim.11), calls=%async_computation.6 | async-start | bytes 655360 | tf_op jit(solution)/shard_map/all_to_all | solution.py:439
  139.6 7.8 %collective-permute-start.7 = (f32[64,256]{1,0:T(8,128)S(1)}, f32[64,256]{1,0:T(8,128)S(1)}, u32[]{:S(2)}, u32[]{:S(2)}) collective-permute-start(f32[64,256]{1,0:T(8,128)S(1)} %get-tuple-element.28.refs_0_), channel_id=1, source_target_pairs={{0,3},{1,0},{2,1},{3,2},{4,7},{5,4},{6,5},{7,6},{8,11},{9,8},{10,9... | collective-permute-start | bytes 196616 | tf_op jit(solution)/shard_map/ppermute | solution.py:434
  142.4 6.8 %collective-permute-start.6 = (f32[64,256]{1,0:T(8,128)S(1)}, f32[64,256]{1,0:T(8,128)S(1)}, u32[]{:S(2)}, u32[]{:S(2)}) collective-permute-start(f32[64,256]{1,0:T(8,128)S(1)} %get-tuple-element.28.refs_0_), channel_id=1, source_target_pairs={{0,2},{1,3},{2,0},{3,1},{4,6},{5,7},{6,4},{7,5},{8,10},{9,11},{10,... | collective-permute-start | bytes 196616 | tf_op jit(solution)/shard_map/ppermute | solution.py:434
  145.5 6.2 %collective-permute-start.5 = (f32[64,256]{1,0:T(8,128)S(1)}, f32[64,256]{1,0:T(8,128)S(1)}, u32[]{:S(2)}, u32[]{:S(2)}) collective-permute-start(f32[64,256]{1,0:T(8,128)S(1)} %get-tuple-element.28.refs_0_), channel_id=1, source_target_pairs={{0,1},{1,2},{2,3},{3,0},{4,5},{5,6},{6,7},{7,4},{8,9},{9,10},{10,1... | collective-permute-start | bytes 196616 | tf_op jit(solution)/shard_map/ppermute | solution.py:434

commit v8 on v7

--- a/solution.py
+++ b/solution.py
@@ -22,6 +22,7 @@
 F32 = jnp.float32
 BF16 = jnp.bfloat16
 INTERPRET = False
+PIVOTS = 4
 
 GRID = (8, 8, 2)
 BOX = ("z", "y", "k")
@@ -226,7 +227,7 @@
         )
 
 
-def far_kernel(dims, info, gathered, out, tpos, rhi, rlo, weight, acc):
+def far_kernel(dims, info, gathered, out, tpos, rcat, weight, acc):
     nz, ny, nk, nx = dims
     targets = ny * nk
     mine = lax.axis_index("y") * nk + lax.axis_index("k")
@@ -243,8 +244,7 @@
     for g in range(nz):
         rows = jnp.concatenate([gathered[nx * g + c, 0:32, :] for c in range(nx)], axis=0)
         hi, lo = split(jnp.concatenate([rows, rotate(rows)], axis=1))
-        rhi[g] = hi
-        rlo[g] = lo
+        rcat[g] = jnp.concatenate([hi, lo], axis=0)
     acc[...] = jnp.zeros_like(acc)
     per = min(4, targets)
 
@@ -273,8 +273,10 @@
                 weight[span, :],
             )
             khi, klo = split(jnp.concatenate([re, im], axis=1))
-            acc[span, :] += dot(khi, rhi[g], 1, 1) + (
-                dot(khi, rlo[g], 1, 1) + dot(klo, rhi[g], 1, 1)
+            width = acc.shape[1]
+            both = dot(khi, rcat[g], 1, 1)
+            acc[span, :] += both[:, 0:width] + (
+                both[:, width:] + dot(klo, rcat[g, 0:width, :], 1, 1)
             )
         return carry
 
@@ -392,25 +394,35 @@
     m = jnp.concatenate([g, eye.astype(F32)], axis=1)
     tiles = [m[8 * i : 8 * i + 8] for i in range(8)]
     sub = lax.broadcasted_iota(jnp.int32, (8, 1), 0)
-    for j in range(0, 64, 2):
+    for j in range(0, 64, PIVOTS):
         at, top = divmod(j, 8)
-        ones = [jnp.broadcast_to(tile[:, j : j + 1], (8, PTS)) for tile in tiles[at:]]
-        twos = [jnp.broadcast_to(tile[:, j + 1 : j + 2], (8, PTS)) for tile in tiles[at:]]
-        one = tiles[at][top : top + 1]
-        two = tiles[at][top + 1 : top + 2]
-        p1, a = ones[0][top : top + 1], ones[0][top + 1 : top + 2]
-        p2 = twos[0][top + 1 : top + 2]
-        det = p1 * p2 - a * a
-        r1 = 1.0 / p1
-        q = p1 / det
-        two = two - (a * r1) * one
-        for i, (c1, c2) in enumerate(zip(ones, twos)):
-            f1 = c1 * r1
-            f2 = (c2 - f1 * a) * q
-            if i == 0:
-                f1 = jnp.where(sub > top, f1, 0.0)
-                f2 = jnp.where(sub > top + 1, f2, 0.0)
-            tiles[at + i] = tiles[at + i] - f1 * one - f2 * two
+        live = tiles[at:]
+        cols = [
+            [jnp.broadcast_to(tile[:, j + n : j + n + 1], (8, PTS)) for tile in live]
+            for n in range(PIVOTS)
+        ]
+        lines = [tiles[at][top + n : top + n + 1] for n in range(PIVOTS)]
+        sm = [[cols[n][0][top + r : top + r + 1] for n in range(PIVOTS)] for r in range(PIVOTS)]
+        factors = []
+        for n in range(PIVOTS):
+            inverse = 1.0 / sm[n][n]
+            ratio = [sm[r][n] * inverse for r in range(PIVOTS)]
+            factors.append(inverse)
+            for r in range(n + 1, PIVOTS):
+                lines[r] = lines[r] - ratio[r] * lines[n]
+                for e in range(n + 1, PIVOTS):
+                    sm[r][e] = sm[r][e] - ratio[r] * sm[n][e]
+        for i in range(len(live)):
+            bar = [cols[n][i] for n in range(PIVOTS)]
+            new = live[i]
+            for n in range(PIVOTS):
+                f = bar[n] * factors[n]
+                for r in range(n + 1, PIVOTS):
+                    bar[r] = bar[r] - f * sm[n][r]
+                if i == 0:
+                    f = jnp.where(sub > top + n, f, 0.0)
+                new = new - f * lines[n]
+            tiles[at + i] = new
     m = jnp.concatenate(tiles, axis=0)
     pivots = jnp.sum(jnp.where(eye, m[:, 0:64], 0.0), axis=1, keepdims=True)
     m = m * (1.0 / jnp.sqrt(pivots))
@@ -490,8 +502,7 @@
         [VMEM] * 2,
         [
             pltpu.VMEM((3, SKEL * targets, PTS), F32),
-            pltpu.VMEM((nz, 32 * nx, 2 * PTS), BF16),
-            pltpu.VMEM((nz, 32 * nx, 2 * PTS), BF16),
+            pltpu.VMEM((nz, 64 * nx, 2 * PTS), BF16),
             pltpu.VMEM((SKEL * targets, PTS), F32),
             pltpu.VMEM((SKEL * targets, 32 * nx), F32),
         ],

time: 160 us -> 158 us (0.988)
  Pallas kernels: 24.5 us -> 22.4 us
    pallas_call x1, Pallas kernels: 6.51 us -> 4.69 us  [shards(): call(functools.partial(finish_kernel, nx), (shape(2, 16, points), shape(4...]
where the time goes in v8:
time: 158 us; the launch traced here: 157 us
  blocking collectives  66 us (42%)
  starting transfers between devices  45.6 us (29%)
  Pallas kernels  22.4 us (14%)
  waiting for transfers between devices  21.7 us (14%)
    all_to_all x4, blocking collectives, trade(): return lax.all_to_all(value, axes, split_axis=0, concat_axis=0, tiled=True)  66 us
    all_to_all x3, starting transfers between devices, trade(): return lax.all_to_all(value, axes, split_axis=0, concat_axis=0, tiled=True)  22.2 us
    ppermute x6, starting transfers between devices, around(): lax.ppermute(blocks[r], 'x', [(i, (i + r) % n) for i in range(n)])  17.8 us
    ppermute x6, waiting for transfers between devices, around(): lax.ppermute(blocks[r], 'x', [(i, (i + r) % n) for i in range(n)])  11.2 us
    all_to_all x3, waiting for transfers between devices, trade(): return lax.all_to_all(value, axes, split_axis=0, concat_axis=0, tiled=True)  6.8 us
    pallas_call x1, Pallas kernels, shards(): call(functools.partial(near_kernel, dims), (shape(32, PTS),) + (shape(PTS...  6.25 us
    pallas_call x1, Pallas kernels, shards(): call(functools.partial(far_kernel, dims), shape(targets, SKEL, 32 * nx),...  5.78 us
    pallas_call x1, Pallas kernels, shards(): call(functools.partial(finish_kernel, nx), (shape(2, 16, points), shape(4...  4.69 us
  transfers between devices with their start and end apart: 11, of which 8 were waited for; matrix products, arithmetic and copies ran while one was open for 0% of the time, Pallas kernels for 6%

profile of v8, /device:TPU:1, one launch (start us, length us, event | category | flops | bytes accessed | tf_op | source)
XLA Modules:
  0.0 157.2 jit_solution(7880869574790457132)
XLA Ops:
  0.6 1.7 %shard_map.94 = (f32[16,8,128]{2,1,0:T(8,128)}, f32[8,128]{1,0:T(8,128)}) custom-call(s32[4,27]{1,0:T(4,128)} %near.3, s32[4]{0:T(128)} %count.3, f32[3,512]{1,0:T(4,128)} %offsets.3, s32[4,32]{1,0:T(4,128)} %skel.1), custom_call_target="tpu_custom_call" | custom-call | bytes 524288 | tf_op jit(solution)/shard_map/pallas_call | solution.py:463
  2.3 10.1 %all-to-all-start = ((f32[16,8,128]{2,1,0:T(8,128)}), f32[16,8,128]{2,1,0:T(8,128)S(1)}, u32[]{:S(2)}, u32[]{:S(2)}) async-start(f32[16,8,128]{2,1,0:T(8,128)} %get-tuple-element.16), calls=%async_computation | async-start | bytes 131072 | tf_op jit(solution)/shard_map/all_to_all | solution.py:451
  12.5 2.2 %shard_map.95 = (f32[40,512]{1,0:T(8,128)}, f32[32,40,128]{2,1,0:T(8,128)}) custom-call(f32[4,2,16,512]{3,2,1,0:T(8,128)} %cur.3, f32[1,512]{1,0:T(1,128)} %bitcast.7, f32[3,512]{1,0:T(4,128)} %offsets.3, f32[4,32,128]{2,1,0:T(8,128)} %interp.3, f32[8,128]{1,0:T(8,128)} %get-tuple-element.17.skelpos), custom_call_target="tpu_custom_call" | custom-call | bytes 524288 | tf_op jit(solution)/shard_map/pallas_call | solution.py:470
  14.6 5.6 %all-to-all-done = f32[16,8,128]{2,1,0:T(8,128)S(1)} async-done(((f32[16,8,128]{2,1,0:T(8,128)}), f32[16,8,128]{2,1,0:T(8,128)S(1)}, u32[]{:S(2)}, u32[]{:S(2)}) %all-to-all-start) | async-done | bytes 65568 | tf_op jit(solution)/shard_map/all_to_all | solution.py:451
  20.3 30.3 %all_to_all.35.gathered = f32[32,40,128]{2,1,0:T(8,128)S(1)} all-to-all(f32[32,40,128]{2,1,0:T(8,128)} %get-tuple-element.18), channel_id=1, replica_groups=mesh['z'=8,'y'=8,'k'=2,'x'=4] {'z','x'}, dimensions={0} | all-to-all | bytes 1310720 | tf_op jit(solution)/shard_map/all_to_all | solution.py:451
  50.6 5.8 %shard_map.96 = f32[16,32,128]{2,1,0:T(8,128)} custom-call(f32[128,128]{1,0:T(8,128)S(1)} %bitcast.6, f32[32,40,128]{2,1,0:T(8,128)S(1)} %all_to_all.35.gathered), custom_call_target="tpu_custom_call" | custom-call | flops 805306368 | bytes 524288 | tf_op jit(solution)/shard_map/pallas_call | solution.py:499
  56.4 0.0 copy-start.4
  56.4 0.0 copy-start
  56.4 0.0 copy-start.2
  56.4 5.8 %all-to-all-start.2 = ((f32[16,32,128]{2,1,0:T(8,128)}), f32[16,32,128]{2,1,0:T(8,128)S(1)}, u32[]{:S(2)}, u32[]{:S(2)}) async-start(f32[16,32,128]{2,1,0:T(8,128)} %shard_map.96), calls=%async_computation.2 | async-start | bytes 524288 | tf_op jit(solution)/shard_map/all_to_all | solution.py:451
  62.2 0.0 copy-start.3
  62.2 0.0 copy-done.4
  62.2 2.1 %collective-permute-start.1 = (f32[40,512]{1,0:T(8,128)S(1)}, f32[40,512]{1,0:T(8,128)S(1)}, u32[]{:S(2)}, u32[]{:S(2)}) collective-permute-start(f32[40,512]{1,0:T(8,128)S(1)} %copy-done.4), channel_id=1, source_target_pairs={{4,0},{8,4},{12,8},{16,12},{20,16},{24,20},{28,24},{32,28},{36,32}... | collective-permute-start | bytes 245768 | tf_op jit(solution)/shard_map/ppermute | solution.py:477
  64.4 3.4 %collective-permute-start = (f32[40,512]{1,0:T(8,128)S(1)}, f32[40,512]{1,0:T(8,128)S(1)}, u32[]{:S(2)}, u32[]{:S(2)}) collective-permute-start(f32[40,512]{1,0:T(8,128)S(1)} %copy-done.4), channel_id=1, source_target_pairs={{0,4},{4,8},{8,12},{12,16},{16,20},{20,24},{24,28},{28,32},{32,36}... | collective-permute-start | bytes 245768 | tf_op jit(solution)/shard_map/ppermute | solution.py:476
  67.8 3.7 %collective-permute-done.1.nxt = f32[40,512]{1,0:T(8,128)S(1)} collective-permute-done((f32[40,512]{1,0:T(8,128)S(1)}, f32[40,512]{1,0:T(8,128)S(1)}, u32[]{:S(2)}, u32[]{:S(2)}) %collective-permute-start.1) | collective-permute-done | bytes 81952 | tf_op jit(solution)/shard_map/ppermute | solution.py:477
  71.5 0.0 collective-permute-done.prev
  71.5 0.0 copy-done
  71.5 0.0 copy-done.2
  71.5 0.0 copy-done.3
  71.5 6.2 %shard_map.97 = (f32[32,128]{1,0:T(8,128)S(1)}, f32[136,512]{1,0:T(8,128)S(1)}, f32[136,512]{1,0:T(8,128)S(1)}, f32[136,512]{1,0:T(8,128)S(1)}) custom-call(s32[4,27]{1,0:T(4,128)S(1)} %copy-done.2, s32[4]{0:T(128)S(1)} %copy-done.3, f32[40,512]{1,0:T(8,128)S(1)} %collective-permute-done.prev, f32[40,512]{1,0:T(8,128)S(1)} %copy-done.4, ...), custom_call_target="tpu_custom_call" | custom-call | flops 301989888 | bytes 524288 | tf_op jit(solution)/shard_map/pallas_call | solution.py:480
  77.8 2.7 %collective-permute-start.2 = (f32[136,512]{1,0:T(8,128)S(1)}, f32[136,512]{1,0:T(8,128)S(1)}, u32[]{:S(2)}, u32[]{:S(2)}) collective-permute-start(f32[136,512]{1,0:T(8,128)S(1)} %get-tuple-element.21), channel_id=1, source_target_pairs={{0,1},{1,2},{2,3},{3,0},{4,5},{5,6},{6,7},{7,4},{8,9},{9,10},{10,1... | collective-permute-start | bytes 835592 | tf_op jit(solution)/shard_map/ppermute | solution.py:446
  80.4 4.3 %collective-permute-start.3 = (f32[136,512]{1,0:T(8,128)S(1)}, f32[136,512]{1,0:T(8,128)S(1)}, u32[]{:S(2)}, u32[]{:S(2)}) collective-permute-start(f32[136,512]{1,0:T(8,128)S(1)} %get-tuple-element.22), channel_id=1, source_target_pairs={{0,2},{1,3},{2,0},{3,1},{4,6},{5,7},{6,4},{7,5},{8,10},{9,11},{10,... | collective-permute-start | bytes 835592 | tf_op jit(solution)/shard_map/ppermute | solution.py:446
  84.8 3.1 %collective-permute-start.4 = (f32[136,512]{1,0:T(8,128)S(1)}, f32[136,512]{1,0:T(8,128)S(1)}, u32[]{:S(2)}, u32[]{:S(2)}) collective-permute-start(f32[136,512]{1,0:T(8,128)S(1)} %get-tuple-element.23), channel_id=1, source_target_pairs={{0,3},{1,0},{2,1},{3,2},{4,7},{5,4},{6,5},{7,6},{8,11},{9,8},{10,9... | collective-permute-start | bytes 835592 | tf_op jit(solution)/shard_map/ppermute | solution.py:446
  87.9 1.4 collective-permute-done.2.refs_0_
  89.3 3.1 %collective-permute-done.3.refs_1_ = f32[136,512]{1,0:T(8,128)S(1)} collective-permute-done((f32[136,512]{1,0:T(8,128)S(1)}, f32[136,512]{1,0:T(8,128)S(1)}, u32[]{:S(2)}, u32[]{:S(2)}) %collective-permute-start.3) | collective-permute-done | bytes 278560 | tf_op jit(solution)/shard_map/ppermute | solution.py:446
  92.3 2.4 %collective-permute-done.4.refs_2_ = f32[136,512]{1,0:T(8,128)S(1)} collective-permute-done((f32[136,512]{1,0:T(8,128)S(1)}, f32[136,512]{1,0:T(8,128)S(1)}, u32[]{:S(2)}, u32[]{:S(2)}) %collective-permute-start.4) | collective-permute-done | bytes 278560 | tf_op jit(solution)/shard_map/ppermute | solution.py:446
  94.7 0.0 copy-start.1
  94.8 0.9 shard_map.98
  95.7 0.0 all-to-all-done.2.phi
  95.7 0.0 copy-done.1
  95.7 0.8 shard_map.99
  96.6 17.9 %all_to_all.36 = f32[16,16,128]{2,1,0:T(8,128)S(1)} all-to-all(f32[16,16,128]{2,1,0:T(8,128)S(1)} %get-tuple-element.27), channel_id=1, replica_groups=mesh['z'=8,'y'=8,'k'=2,'x'=4] {'y','k'}, dimensions={0} | all-to-all | bytes 262144 | tf_op jit(solution)/shard_map/all_to_all | solution.py:451
  114.5 10.0 %all_to_all.37 = f32[8,16,128]{2,1,0:T(8,128)S(1)} all-to-all(f32[8,16,128]{2,1,0:T(8,128)S(1)} %broadcast_in_dim.9), channel_id=1, replica_groups=mesh['z'=8,'y'=8,'k'=2,'x'=4] {'z'}, dimensions={0} | all-to-all | bytes 131072 | tf_op jit(solution)/shard_map/all_to_all | solution.py:451
  124.5 7.8 %all_to_all.38 = f32[4,16,128]{2,1,0:T(8,128)S(1)} all-to-all(f32[4,16,128]{2,1,0:T(8,128)S(1)} %broadcast_in_dim.10), channel_id=1, replica_groups=mesh['z'=8,'y'=8,'k'=2,'x'=4] {'x'}, dimensions={0} | all-to-all | bytes 65536 | tf_op jit(solution)/shard_map/all_to_all | solution.py:451
  132.3 0.7 broadcast_in_dim.11
  133.0 6.2 %all-to-all-start.6 = ((f32[16,40,128]{2,1,0:T(8,128)}), f32[16,40,128]{2,1,0:T(8,128)S(1)}, u32[]{:S(2)}, u32[]{:S(2)}) async-start(f32[16,40,128]{2,1,0:T(8,128)} %broadcast_in_dim.11), calls=%async_computation.6 | async-start | bytes 655360 | tf_op jit(solution)/shard_map/all_to_all | solution.py:451
  139.3 2.8 %collective-permute-start.7 = (f32[64,256]{1,0:T(8,128)S(1)}, f32[64,256]{1,0:T(8,128)S(1)}, u32[]{:S(2)}, u32[]{:S(2)}) collective-permute-start(f32[64,256]{1,0:T(8,128)S(1)} %get-tuple-element.28.refs_0_), channel_id=1, source_target_pairs={{0,3},{1,0},{2,1},{3,2},{4,7},{5,4},{6,5},{7,6},{8,11},{9,8},{10,9... | collective-permute-start | bytes 196616 | tf_op jit(solution)/shard_map/ppermute | solution.py:446
  142.1 3.1 %collective-permute-start.6 = (f32[64,256]{1,0:T(8,128)S(1)}, f32[64,256]{1,0:T(8,128)S(1)}, u32[]{:S(2)}, u32[]{:S(2)}) collective-permute-start(f32[64,256]{1,0:T(8,128)S(1)} %get-tuple-element.28.refs_0_), channel_id=1, source_target_pairs={{0,2},{1,3},{2,0},{3,1},{4,6},{5,7},{6,4},{7,5},{8,10},{9,11},{10,... | collective-permute-start | bytes 196616 | tf_op jit(solution)/shard_map/ppermute | solution.py:446
  145.2 1.9 %collective-permute-start.5 = (f32[64,256]{1,0:T(8,128)S(1)}, f32[64,256]{1,0:T(8,128)S(1)}, u32[]{:S(2)}, u32[]{:S(2)}) collective-permute-start(f32[64,256]{1,0:T(8,128)S(1)} %get-tuple-element.28.refs_0_), channel_id=1, source_target_pairs={{0,1},{1,2},{2,3},{3,0},{4,5},{5,6},{6,7},{7,4},{8,9},{9,10},{10,1... | collective-permute-start | bytes 196616 | tf_op jit(solution)/shard_map/ppermute | solution.py:446
  147.1 0.0 collective-permute-done.7.refs_3_
  147.1 1.8 %collective-permute-done.6.refs_2_ = f32[64,256]{1,0:T(8,128)S(1)} collective-permute-done((f32[64,256]{1,0:T(8,128)S(1)}, f32[64,256]{1,0:T(8,128)S(1)}, u32[]{:S(2)}, u32[]{:S(2)}) %collective-permute-start.6) | collective-permute-done | bytes 65568 | tf_op jit(solution)/shard_map/ppermute | solution.py:446
  148.9 2.5 %collective-permute-done.5.refs_1_ = f32[64,256]{1,0:T(8,128)S(1)} collective-permute-done((f32[64,256]{1,0:T(8,128)S(1)}, f32[64,256]{1,0:T(8,128)S(1)}, u32[]{:S(2)}, u32[]{:S(2)}) %collective-permute-start.5) | collective-permute-done | bytes 65568 | tf_op jit(solution)/shard_map/ppermute | solution.py:446
  151.4 1.2 all-to-all-done.6.summed
  152.5 4.7 %shard_map.100 = (f32[2,16,512]{2,1,0:T(8,128)}, f32[4,64,64]{2,1,0:T(8,128)}, f32[64,64]{1,0:T(8,128)}) custom-call(f32[16,40,128]{2,1,0:T(8,128)S(1)} %all-to-all-done.6.summed, f32[2,256,512]{2,1,0:T(8,128)S(1)} %get-tuple-element.24.ordered, f32[64,256]{1,0:T(8,128)S(1)} %get-tuple-element.28.refs_0_, f32[64,256]{1,0:T(8,128)S(1)} %collective-permute-done.5.refs_1_, ...), custom_call_target="tpu_custom_call" | custom-call | bytes 524288 | tf_op jit(solution)/shard_map/pallas_call | solution.py:530
  (6 shorter events, 0.1 us)
Async XLA Ops:
  2.3 18.0 %all-to-all-start = ((f32[16,8,128]{2,1,0:T(8,128)}), f32[16,8,128]{2,1,0:T(8,128)S(1)}, u32[]{:S(2)}, u32[]{:S(2)}) async-start(f32[16,8,128]{2,1,0:T(8,128)} %get-tuple-element.16), calls=%async_computation | async-start | bytes 131072 | tf_op jit(solution)/shard_map/all_to_all | solution.py:451
  56.4 5.8 %copy-start.4 = (f32[40,512]{1,0:T(8,128)S(1)}, f32[40,512]{1,0:T(8,128)}, u32[]{:S(2)}) copy-start(f32[40,512]{1,0:T(8,128)} %get-tuple-element.19.own) | copy-start | bytes 245764
  56.4 15.1 %copy-start = (f32[4,2,16,512]{3,2,1,0:T(8,128)S(1)}, f32[4,2,16,512]{3,2,1,0:T(8,128)}, u32[]{:S(2)}) copy-start(f32[4,2,16,512]{3,2,1,0:T(8,128)} %cur.3) | copy-start | bytes 786436
  56.4 15.1 %copy-start.2 = (s32[4,27]{1,0:T(4,128)S(1)}, s32[4,27]{1,0:T(4,128)}, u32[]{:S(2)}) copy-start(s32[4,27]{1,0:T(4,128)} %near.3) | copy-start | bytes 1300
  56.4 39.3 %all-to-all-start.2 = ((f32[16,32,128]{2,1,0:T(8,128)}), f32[16,32,128]{2,1,0:T(8,128)S(1)}, u32[]{:S(2)}, u32[]{:S(2)}) async-start(f32[16,32,128]{2,1,0:T(8,128)} %shard_map.96), calls=%async_computation.2 | async-start | bytes 524288 | tf_op jit(solution)/shard_map/all_to_all | solution.py:451
  62.2 9.3 %copy-start.3 = (s32[4]{0:T(128)S(1)}, s32[4]{0:T(128)}, u32[]{:S(2)}) copy-start(s32[4]{0:T(128)} %count.3) | copy-start | bytes 52
  62.2 9.3 %collective-permute-start.1 = (f32[40,512]{1,0:T(8,128)S(1)}, f32[40,512]{1,0:T(8,128)S(1)}, u32[]{:S(2)}, u32[]{:S(2)}) collective-permute-start(f32[40,512]{1,0:T(8,128)S(1)} %copy-done.4), channel_id=1, source_target_pairs={{4,0},{8,4},{12,8},{16,12},{20,16},{24,20},{28,24},{32,28},{36,32}... | collective-permute-start | bytes 245768 | tf_op jit(solution)/shard_map/ppermute | solution.py:477
  64.4 7.2 %collective-permute-start = (f32[40,512]{1,0:T(8,128)S(1)}, f32[40,512]{1,0:T(8,128)S(1)}, u32[]{:S(2)}, u32[]{:S(2)}) collective-permute-start(f32[40,512]{1,0:T(8,128)S(1)} %copy-done.4), channel_id=1, source_target_pairs={{0,4},{4,8},{8,12},{12,16},{16,20},{20,24},{24,28},{28,32},{32,36}... | collective-permute-start | bytes 245768 | tf_op jit(solution)/shard_map/ppermute | solution.py:476
  77.8 11.5 %collective-permute-start.2 = (f32[136,512]{1,0:T(8,128)S(1)}, f32[136,512]{1,0:T(8,128)S(1)}, u32[]{:S(2)}, u32[]{:S(2)}) collective-permute-start(f32[136,512]{1,0:T(8,128)S(1)} %get-tuple-element.21), channel_id=1, source_target_pairs={{0,1},{1,2},{2,3},{3,0},{4,5},{5,6},{6,7},{7,4},{8,9},{9,10},{10,1... | collective-permute-start | bytes 835592 | tf_op jit(solution)/shard_map/ppermute | solution.py:446
  80.4 11.9 %collective-permute-start.3 = (f32[136,512]{1,0:T(8,128)S(1)}, f32[136,512]{1,0:T(8,128)S(1)}, u32[]{:S(2)}, u32[]{:S(2)}) collective-permute-start(f32[136,512]{1,0:T(8,128)S(1)} %get-tuple-element.22), channel_id=1, source_target_pairs={{0,2},{1,3},{2,0},{3,1},{4,6},{5,7},{6,4},{7,5},{8,10},{9,11},{10,... | collective-permute-start | bytes 835592 | tf_op jit(solution)/shard_map/ppermute | solution.py:446
  84.8 10.0 %collective-permute-start.4 = (f32[136,512]{1,0:T(8,128)S(1)}, f32[136,512]{1,0:T(8,128)S(1)}, u32[]{:S(2)}, u32[]{:S(2)}) collective-permute-start(f32[136,512]{1,0:T(8,128)S(1)} %get-tuple-element.23), channel_id=1, source_target_pairs={{0,3},{1,0},{2,1},{3,2},{4,7},{5,4},{6,5},{7,6},{8,11},{9,8},{10,9... | collective-permute-start | bytes 835592 | tf_op jit(solution)/shard_map/ppermute | solution.py:446
  94.7 1.0 copy-start.1
  133.0 19.5 %all-to-all-start.6 = ((f32[16,40,128]{2,1,0:T(8,128)}), f32[16,40,128]{2,1,0:T(8,128)S(1)}, u32[]{:S(2)}, u32[]{:S(2)}) async-start(f32[16,40,128]{2,1,0:T(8,128)} %broadcast_in_dim.11), calls=%async_computation.6 | async-start | bytes 655360 | tf_op jit(solution)/shard_map/all_to_all | solution.py:451
  139.3 7.8 %collective-permute-start.7 = (f32[64,256]{1,0:T(8,128)S(1)}, f32[64,256]{1,0:T(8,128)S(1)}, u32[]{:S(2)}, u32[]{:S(2)}) collective-permute-start(f32[64,256]{1,0:T(8,128)S(1)} %get-tuple-element.28.refs_0_), channel_id=1, source_target_pairs={{0,3},{1,0},{2,1},{3,2},{4,7},{5,4},{6,5},{7,6},{8,11},{9,8},{10,9... | collective-permute-start | bytes 196616 | tf_op jit(solution)/shard_map/ppermute | solution.py:446
  142.1 6.8 %collective-permute-start.6 = (f32[64,256]{1,0:T(8,128)S(1)}, f32[64,256]{1,0:T(8,128)S(1)}, u32[]{:S(2)}, u32[]{:S(2)}) collective-permute-start(f32[64,256]{1,0:T(8,128)S(1)} %get-tuple-element.28.refs_0_), channel_id=1, source_target_pairs={{0,2},{1,3},{2,0},{3,1},{4,6},{5,7},{6,4},{7,5},{8,10},{9,11},{10,... | collective-permute-start | bytes 196616 | tf_op jit(solution)/shard_map/ppermute | solution.py:446
  145.2 6.2 %collective-permute-start.5 = (f32[64,256]{1,0:T(8,128)S(1)}, f32[64,256]{1,0:T(8,128)S(1)}, u32[]{:S(2)}, u32[]{:S(2)}) collective-permute-start(f32[64,256]{1,0:T(8,128)S(1)} %get-tuple-element.28.refs_0_), channel_id=1, source_target_pairs={{0,1},{1,2},{2,3},{3,0},{4,5},{5,6},{6,7},{7,4},{8,9},{9,10},{10,1... | collective-permute-start | bytes 196616 | tf_op jit(solution)/shard_map/ppermute | solution.py:446

commit v9 on v8

--- a/solution.py
+++ b/solution.py
@@ -358,20 +358,19 @@
     applied, (out, coupling, factor, inv) = refs[:-4], refs[-4:]
     n = summed.shape[0]
     lead = 128 // n
-    tail = 128 // n
     packed = jnp.concatenate([summed[d, 0:lead, :] for d in range(n)], axis=0)
     c = jnp.concatenate([packed[:, 0:64], packed[:, 64:128]], axis=0)
     for k in range(4):
         coupling[k] = c[64 * k : 64 * k + 64]
-    own = None
+    base = lead + 32 // n
+    own = jnp.concatenate([summed[:, e, :] for e in range(lead, base)], axis=0)
     de, h = [], []
     for x in range(nx):
-        rest = [summed[:, lead + tail * x + e, :] for e in range(112 // n)]
+        rest = [summed[:, base + 80 // n * x + e, :] for e in range(80 // n)]
         rest = jnp.concatenate(rest, axis=0)
-        own = rest[0:32] if own is None else own + rest[0:32]
-        de.append(rest[32:96])
+        de.append(rest[0:64])
         h.append(
-            jnp.concatenate([rest[96:112, 32 * g : 32 * g + 32] for g in range(4)], axis=0)
+            jnp.concatenate([rest[64:80, 32 * g : 32 * g + 32] for g in range(4)], axis=0)
         )
     g = jnp.concatenate([own[:, 0:64], own[:, 64:128]], axis=0)
     blocks = [c[64 * k : 64 * k + 64] for k in range(4)]
@@ -512,6 +511,8 @@
 
     lead = 128 // targets
     tall = 2 * lead
+    added = lead + 32 // targets
+    used = added + 80 // targets
     applied, part = call(
         functools.partial(couple_kernel, scale),
         (shape(64, 2 * PTS), shape(targets, tall, PTS)),
@@ -522,7 +523,7 @@
     part = jnp.sum(trade(jnp.broadcast_to(part[None], (nz, tall, PTS)), "z"), axis=0)
     part = trade(jnp.broadcast_to(part[None], (nx, tall, PTS)), "x")
     part = jnp.concatenate(
-        [jnp.sum(part[:, :lead], axis=0), part[:, lead:].reshape(nx * (tall - lead), PTS)],
+        [jnp.sum(part[:, :added], axis=0), part[:, added:used].reshape(nx * (used - added), PTS)],
         axis=0,
     )
     summed = trade(jnp.broadcast_to(part[None], (targets,) + part.shape), YK)

time: 158 us -> 158 us (level)
  transfers between devices with their start and end apart: 11 -> 11, of which waited for: 8 -> 7; matrix products, arithmetic and copies ran while one was open for 0% -> 0% of each run, Pallas kernels for 6% -> 6%
where the time goes in v9:
time: 158 us; the launch traced here: 156 us
  blocking collectives  66 us (42%)
  starting transfers between devices  45.6 us (29%)
  Pallas kernels  22.4 us (14%)
  waiting for transfers between devices  20.5 us (13%)
    all_to_all x4, blocking collectives, trade(): return lax.all_to_all(value, axes, split_axis=0, concat_axis=0, tiled=True)  66 us
    all_to_all x3, starting transfers between devices, trade(): return lax.all_to_all(value, axes, split_axis=0, concat_axis=0, tiled=True)  22.2 us
    ppermute x6, starting transfers between devices, around(): lax.ppermute(blocks[r], 'x', [(i, (i + r) % n) for i in range(n)])  17.8 us
    ppermute x6, waiting for transfers between devices, around(): lax.ppermute(blocks[r], 'x', [(i, (i + r) % n) for i in range(n)])  11.2 us
    pallas_call x1, Pallas kernels, shards(): call(functools.partial(near_kernel, dims), (shape(32, PTS),) + (shape(PTS...  6.25 us
    pallas_call x1, Pallas kernels, shards(): call(functools.partial(far_kernel, dims), shape(targets, SKEL, 32 * nx),...  5.79 us
    all_to_all x3, waiting for transfers between devices, trade(): return lax.all_to_all(value, axes, split_axis=0, concat_axis=0, tiled=True)  5.65 us
    pallas_call x1, Pallas kernels, shards(): call(functools.partial(finish_kernel, nx), (shape(2, 16, points), shape(4...  4.7 us
  transfers between devices with their start and end apart: 11, of which 7 were waited for; matrix products, arithmetic and copies ran while one was open for 0% of the time, Pallas kernels for 6%

profile of v9, /device:TPU:1, one launch (start us, length us, event | category | flops | bytes accessed | tf_op | source)
XLA Modules:
  0.0 156.1 jit_solution(10488524007058156248)
XLA Ops:
  0.6 1.7 %shard_map.94 = (f32[16,8,128]{2,1,0:T(8,128)}, f32[8,128]{1,0:T(8,128)}) custom-call(s32[4,27]{1,0:T(4,128)} %near.3, s32[4]{0:T(128)} %count.3, f32[3,512]{1,0:T(4,128)} %offsets.3, s32[4,32]{1,0:T(4,128)} %skel.1), custom_call_target="tpu_custom_call" | custom-call | bytes 524288 | tf_op jit(solution)/shard_map/pallas_call | solution.py:462
  2.3 10.1 %all-to-all-start = ((f32[16,8,128]{2,1,0:T(8,128)}), f32[16,8,128]{2,1,0:T(8,128)S(1)}, u32[]{:S(2)}, u32[]{:S(2)}) async-start(f32[16,8,128]{2,1,0:T(8,128)} %get-tuple-element.16), calls=%async_computation | async-start | bytes 131072 | tf_op jit(solution)/shard_map/all_to_all | solution.py:450
  12.5 2.2 %shard_map.95 = (f32[40,512]{1,0:T(8,128)}, f32[32,40,128]{2,1,0:T(8,128)}) custom-call(f32[4,2,16,512]{3,2,1,0:T(8,128)} %cur.3, f32[1,512]{1,0:T(1,128)} %bitcast.5, f32[3,512]{1,0:T(4,128)} %offsets.3, f32[4,32,128]{2,1,0:T(8,128)} %interp.3, f32[8,128]{1,0:T(8,128)} %get-tuple-element.17.skelpos), custom_call_target="tpu_custom_call" | custom-call | bytes 524288 | tf_op jit(solution)/shard_map/pallas_call | solution.py:469
  14.6 5.6 %all-to-all-done = f32[16,8,128]{2,1,0:T(8,128)S(1)} async-done(((f32[16,8,128]{2,1,0:T(8,128)}), f32[16,8,128]{2,1,0:T(8,128)S(1)}, u32[]{:S(2)}, u32[]{:S(2)}) %all-to-all-start) | async-done | bytes 65568 | tf_op jit(solution)/shard_map/all_to_all | solution.py:450
  20.3 30.3 %all_to_all.35.gathered = f32[32,40,128]{2,1,0:T(8,128)S(1)} all-to-all(f32[32,40,128]{2,1,0:T(8,128)} %get-tuple-element.18), channel_id=1, replica_groups=mesh['z'=8,'y'=8,'k'=2,'x'=4] {'z','x'}, dimensions={0} | all-to-all | bytes 1310720 | tf_op jit(solution)/shard_map/all_to_all | solution.py:450
  50.6 5.8 %shard_map.96 = f32[16,32,128]{2,1,0:T(8,128)} custom-call(f32[128,128]{1,0:T(8,128)S(1)} %bitcast.4, f32[32,40,128]{2,1,0:T(8,128)S(1)} %all_to_all.35.gathered), custom_call_target="tpu_custom_call" | custom-call | flops 805306368 | bytes 524288 | tf_op jit(solution)/shard_map/pallas_call | solution.py:498
  56.4 0.0 copy-start.4
  56.4 0.0 copy-start
  56.4 0.0 copy-start.2
  56.4 5.8 %all-to-all-start.2 = ((f32[16,32,128]{2,1,0:T(8,128)}), f32[16,32,128]{2,1,0:T(8,128)S(1)}, u32[]{:S(2)}, u32[]{:S(2)}) async-start(f32[16,32,128]{2,1,0:T(8,128)} %shard_map.96), calls=%async_computation.2 | async-start | bytes 524288 | tf_op jit(solution)/shard_map/all_to_all | solution.py:450
  62.2 0.0 copy-start.3
  62.2 0.0 copy-done.4
  62.2 2.1 %collective-permute-start.1 = (f32[40,512]{1,0:T(8,128)S(1)}, f32[40,512]{1,0:T(8,128)S(1)}, u32[]{:S(2)}, u32[]{:S(2)}) collective-permute-start(f32[40,512]{1,0:T(8,128)S(1)} %copy-done.4), channel_id=1, source_target_pairs={{4,0},{8,4},{12,8},{16,12},{20,16},{24,20},{28,24},{32,28},{36,32}... | collective-permute-start | bytes 245768 | tf_op jit(solution)/shard_map/ppermute | solution.py:476
  64.4 3.4 %collective-permute-start = (f32[40,512]{1,0:T(8,128)S(1)}, f32[40,512]{1,0:T(8,128)S(1)}, u32[]{:S(2)}, u32[]{:S(2)}) collective-permute-start(f32[40,512]{1,0:T(8,128)S(1)} %copy-done.4), channel_id=1, source_target_pairs={{0,4},{4,8},{8,12},{12,16},{16,20},{20,24},{24,28},{28,32},{32,36}... | collective-permute-start | bytes 245768 | tf_op jit(solution)/shard_map/ppermute | solution.py:475
  67.8 3.7 %collective-permute-done.1.nxt = f32[40,512]{1,0:T(8,128)S(1)} collective-permute-done((f32[40,512]{1,0:T(8,128)S(1)}, f32[40,512]{1,0:T(8,128)S(1)}, u32[]{:S(2)}, u32[]{:S(2)}) %collective-permute-start.1) | collective-permute-done | bytes 81952 | tf_op jit(solution)/shard_map/ppermute | solution.py:476
  71.5 0.0 collective-permute-done.prev
  71.5 0.0 copy-done
  71.5 0.0 copy-done.2
  71.5 0.0 copy-done.3
  71.5 6.2 %shard_map.97 = (f32[32,128]{1,0:T(8,128)S(1)}, f32[136,512]{1,0:T(8,128)S(1)}, f32[136,512]{1,0:T(8,128)S(1)}, f32[136,512]{1,0:T(8,128)S(1)}) custom-call(s32[4,27]{1,0:T(4,128)S(1)} %copy-done.2, s32[4]{0:T(128)S(1)} %copy-done.3, f32[40,512]{1,0:T(8,128)S(1)} %collective-permute-done.prev, f32[40,512]{1,0:T(8,128)S(1)} %copy-done.4, ...), custom_call_target="tpu_custom_call" | custom-call | flops 301989888 | bytes 524288 | tf_op jit(solution)/shard_map/pallas_call | solution.py:479
  77.8 2.7 %collective-permute-start.2 = (f32[136,512]{1,0:T(8,128)S(1)}, f32[136,512]{1,0:T(8,128)S(1)}, u32[]{:S(2)}, u32[]{:S(2)}) collective-permute-start(f32[136,512]{1,0:T(8,128)S(1)} %get-tuple-element.21), channel_id=1, source_target_pairs={{0,1},{1,2},{2,3},{3,0},{4,5},{5,6},{6,7},{7,4},{8,9},{9,10},{10,1... | collective-permute-start | bytes 835592 | tf_op jit(solution)/shard_map/ppermute | solution.py:445
  80.4 4.3 %collective-permute-start.3 = (f32[136,512]{1,0:T(8,128)S(1)}, f32[136,512]{1,0:T(8,128)S(1)}, u32[]{:S(2)}, u32[]{:S(2)}) collective-permute-start(f32[136,512]{1,0:T(8,128)S(1)} %get-tuple-element.22), channel_id=1, source_target_pairs={{0,2},{1,3},{2,0},{3,1},{4,6},{5,7},{6,4},{7,5},{8,10},{9,11},{10,... | collective-permute-start | bytes 835592 | tf_op jit(solution)/shard_map/ppermute | solution.py:445
  84.8 3.1 %collective-permute-start.4 = (f32[136,512]{1,0:T(8,128)S(1)}, f32[136,512]{1,0:T(8,128)S(1)}, u32[]{:S(2)}, u32[]{:S(2)}) collective-permute-start(f32[136,512]{1,0:T(8,128)S(1)} %get-tuple-element.23), channel_id=1, source_target_pairs={{0,3},{1,0},{2,1},{3,2},{4,7},{5,4},{6,5},{7,6},{8,11},{9,8},{10,9... | collective-permute-start | bytes 835592 | tf_op jit(solution)/shard_map/ppermute | solution.py:445
  87.9 1.4 collective-permute-done.2.refs_0_
  89.3 3.1 %collective-permute-done.3.refs_1_ = f32[136,512]{1,0:T(8,128)S(1)} collective-permute-done((f32[136,512]{1,0:T(8,128)S(1)}, f32[136,512]{1,0:T(8,128)S(1)}, u32[]{:S(2)}, u32[]{:S(2)}) %collective-permute-start.3) | collective-permute-done | bytes 278560 | tf_op jit(solution)/shard_map/ppermute | solution.py:445
  92.3 2.4 %collective-permute-done.4.refs_2_ = f32[136,512]{1,0:T(8,128)S(1)} collective-permute-done((f32[136,512]{1,0:T(8,128)S(1)}, f32[136,512]{1,0:T(8,128)S(1)}, u32[]{:S(2)}, u32[]{:S(2)}) %collective-permute-start.4) | collective-permute-done | bytes 278560 | tf_op jit(solution)/shard_map/ppermute | solution.py:445
  94.8 0.0 copy-start.1
  94.8 0.9 shard_map.98
  95.7 0.0 all-to-all-done.2.phi
  95.7 0.0 copy-done.1
  95.7 0.8 shard_map.99
  96.6 17.9 %all_to_all.36 = f32[16,16,128]{2,1,0:T(8,128)S(1)} all-to-all(f32[16,16,128]{2,1,0:T(8,128)S(1)} %get-tuple-element.27), channel_id=1, replica_groups=mesh['z'=8,'y'=8,'k'=2,'x'=4] {'y','k'}, dimensions={0} | all-to-all | bytes 262144 | tf_op jit(solution)/shard_map/all_to_all | solution.py:450
  114.5 10.0 %all_to_all.37 = f32[8,16,128]{2,1,0:T(8,128)S(1)} all-to-all(f32[8,16,128]{2,1,0:T(8,128)S(1)} %broadcast_in_dim.9), channel_id=1, replica_groups=mesh['z'=8,'y'=8,'k'=2,'x'=4] {'z'}, dimensions={0} | all-to-all | bytes 131072 | tf_op jit(solution)/shard_map/all_to_all | solution.py:450
  124.5 7.8 %all_to_all.38 = f32[4,16,128]{2,1,0:T(8,128)S(1)} all-to-all(f32[4,16,128]{2,1,0:T(8,128)S(1)} %broadcast_in_dim.10), channel_id=1, replica_groups=mesh['z'=8,'y'=8,'k'=2,'x'=4] {'x'}, dimensions={0} | all-to-all | bytes 65536 | tf_op jit(solution)/shard_map/all_to_all | solution.py:450
  132.3 0.7 broadcast_in_dim.11
  133.0 6.2 %all-to-all-start.6 = ((f32[16,30,128]{2,1,0:T(8,128)}), f32[16,30,128]{2,1,0:T(8,128)S(1)}, u32[]{:S(2)}, u32[]{:S(2)}) async-start(f32[16,30,128]{2,1,0:T(8,128)} %broadcast_in_dim.11), calls=%async_computation.6 | async-start | bytes 524288 | tf_op jit(solution)/shard_map/all_to_all | solution.py:450
  139.3 2.8 %collective-permute-start.7 = (f32[64,256]{1,0:T(8,128)S(1)}, f32[64,256]{1,0:T(8,128)S(1)}, u32[]{:S(2)}, u32[]{:S(2)}) collective-permute-start(f32[64,256]{1,0:T(8,128)S(1)} %get-tuple-element.28.refs_0_), channel_id=1, source_target_pairs={{0,3},{1,0},{2,1},{3,2},{4,7},{5,4},{6,5},{7,6},{8,11},{9,8},{10,9... | collective-permute-start | bytes 196616 | tf_op jit(solution)/shard_map/ppermute | solution.py:445
  142.1 3.1 %collective-permute-start.6 = (f32[64,256]{1,0:T(8,128)S(1)}, f32[64,256]{1,0:T(8,128)S(1)}, u32[]{:S(2)}, u32[]{:S(2)}) collective-permute-start(f32[64,256]{1,0:T(8,128)S(1)} %get-tuple-element.28.refs_0_), channel_id=1, source_target_pairs={{0,2},{1,3},{2,0},{3,1},{4,6},{5,7},{6,4},{7,5},{8,10},{9,11},{10,... | collective-permute-start | bytes 196616 | tf_op jit(solution)/shard_map/ppermute | solution.py:445
  145.2 1.9 %collective-permute-start.5 = (f32[64,256]{1,0:T(8,128)S(1)}, f32[64,256]{1,0:T(8,128)S(1)}, u32[]{:S(2)}, u32[]{:S(2)}) collective-permute-start(f32[64,256]{1,0:T(8,128)S(1)} %get-tuple-element.28.refs_0_), channel_id=1, source_target_pairs={{0,1},{1,2},{2,3},{3,0},{4,5},{5,6},{6,7},{7,4},{8,9},{9,10},{10,1... | collective-permute-start | bytes 196616 | tf_op jit(solution)/shard_map/ppermute | solution.py:445
  147.1 0.0 collective-permute-done.7.refs_3_
  147.1 1.5 collective-permute-done.6.refs_2_
  148.6 2.8 %collective-permute-done.5.refs_1_ = f32[64,256]{1,0:T(8,128)S(1)} collective-permute-done((f32[64,256]{1,0:T(8,128)S(1)}, f32[64,256]{1,0:T(8,128)S(1)}, u32[]{:S(2)}, u32[]{:S(2)}) %collective-permute-start.5) | collective-permute-done | bytes 65568 | tf_op jit(solution)/shard_map/ppermute | solution.py:445
  151.4 0.0 all-to-all-done.6.summed
  151.4 4.7 %shard_map.100 = (f32[2,16,512]{2,1,0:T(8,128)}, f32[4,64,64]{2,1,0:T(8,128)}, f32[64,64]{1,0:T(8,128)}) custom-call(f32[16,30,128]{2,1,0:T(8,128)S(1)} %all-to-all-done.6.summed, f32[2,256,512]{2,1,0:T(8,128)S(1)} %get-tuple-element.24.ordered, f32[64,256]{1,0:T(8,128)S(1)} %get-tuple-element.28.refs_0_, f32[64,256]{1,0:T(8,128)S(1)} %collective-permute-done.5.refs_1_, ...), custom_call_target="tpu_custom_call" | custom-call | bytes 524288 | tf_op jit(solution)/shard_map/pallas_call | solution.py:531
  (8 shorter events, 0.1 us)
Async XLA Ops:
  2.3 18.0 %all-to-all-start = ((f32[16,8,128]{2,1,0:T(8,128)}), f32[16,8,128]{2,1,0:T(8,128)S(1)}, u32[]{:S(2)}, u32[]{:S(2)}) async-start(f32[16,8,128]{2,1,0:T(8,128)} %get-tuple-element.16), calls=%async_computation | async-start | bytes 131072 | tf_op jit(solution)/shard_map/all_to_all | solution.py:450
  56.4 5.8 %copy-start.4 = (f32[40,512]{1,0:T(8,128)S(1)}, f32[40,512]{1,0:T(8,128)}, u32[]{:S(2)}) copy-start(f32[40,512]{1,0:T(8,128)} %get-tuple-element.19.own) | copy-start | bytes 245764
  56.4 15.1 %copy-start = (f32[4,2,16,512]{3,2,1,0:T(8,128)S(1)}, f32[4,2,16,512]{3,2,1,0:T(8,128)}, u32[]{:S(2)}) copy-start(f32[4,2,16,512]{3,2,1,0:T(8,128)} %cur.3) | copy-start | bytes 786436
  56.4 15.1 %copy-start.2 = (s32[4,27]{1,0:T(4,128)S(1)}, s32[4,27]{1,0:T(4,128)}, u32[]{:S(2)}) copy-start(s32[4,27]{1,0:T(4,128)} %near.3) | copy-start | bytes 1300
  56.4 39.3 %all-to-all-start.2 = ((f32[16,32,128]{2,1,0:T(8,128)}), f32[16,32,128]{2,1,0:T(8,128)S(1)}, u32[]{:S(2)}, u32[]{:S(2)}) async-start(f32[16,32,128]{2,1,0:T(8,128)} %shard_map.96), calls=%async_computation.2 | async-start | bytes 524288 | tf_op jit(solution)/shard_map/all_to_all | solution.py:450
  62.2 9.3 %copy-start.3 = (s32[4]{0:T(128)S(1)}, s32[4]{0:T(128)}, u32[]{:S(2)}) copy-start(s32[4]{0:T(128)} %count.3) | copy-start | bytes 52
  62.2 9.3 %collective-permute-start.1 = (f32[40,512]{1,0:T(8,128)S(1)}, f32[40,512]{1,0:T(8,128)S(1)}, u32[]{:S(2)}, u32[]{:S(2)}) collective-permute-start(f32[40,512]{1,0:T(8,128)S(1)} %copy-done.4), channel_id=1, source_target_pairs={{4,0},{8,4},{12,8},{16,12},{20,16},{24,20},{28,24},{32,28},{36,32}... | collective-permute-start | bytes 245768 | tf_op jit(solution)/shard_map/ppermute | solution.py:476
  64.4 7.2 %collective-permute-start = (f32[40,512]{1,0:T(8,128)S(1)}, f32[40,512]{1,0:T(8,128)S(1)}, u32[]{:S(2)}, u32[]{:S(2)}) collective-permute-start(f32[40,512]{1,0:T(8,128)S(1)} %copy-done.4), channel_id=1, source_target_pairs={{0,4},{4,8},{8,12},{12,16},{16,20},{20,24},{24,28},{28,32},{32,36}... | collective-permute-start | bytes 245768 | tf_op jit(solution)/shard_map/ppermute | solution.py:475
  77.8 11.5 %collective-permute-start.2 = (f32[136,512]{1,0:T(8,128)S(1)}, f32[136,512]{1,0:T(8,128)S(1)}, u32[]{:S(2)}, u32[]{:S(2)}) collective-permute-start(f32[136,512]{1,0:T(8,128)S(1)} %get-tuple-element.21), channel_id=1, source_target_pairs={{0,1},{1,2},{2,3},{3,0},{4,5},{5,6},{6,7},{7,4},{8,9},{9,10},{10,1... | collective-permute-start | bytes 835592 | tf_op jit(solution)/shard_map/ppermute | solution.py:445
  80.4 11.9 %collective-permute-start.3 = (f32[136,512]{1,0:T(8,128)S(1)}, f32[136,512]{1,0:T(8,128)S(1)}, u32[]{:S(2)}, u32[]{:S(2)}) collective-permute-start(f32[136,512]{1,0:T(8,128)S(1)} %get-tuple-element.22), channel_id=1, source_target_pairs={{0,2},{1,3},{2,0},{3,1},{4,6},{5,7},{6,4},{7,5},{8,10},{9,11},{10,... | collective-permute-start | bytes 835592 | tf_op jit(solution)/shard_map/ppermute | solution.py:445
  84.8 10.0 %collective-permute-start.4 = (f32[136,512]{1,0:T(8,128)S(1)}, f32[136,512]{1,0:T(8,128)S(1)}, u32[]{:S(2)}, u32[]{:S(2)}) collective-permute-start(f32[136,512]{1,0:T(8,128)S(1)} %get-tuple-element.23), channel_id=1, source_target_pairs={{0,3},{1,0},{2,1},{3,2},{4,7},{5,4},{6,5},{7,6},{8,11},{9,8},{10,9... | collective-permute-start | bytes 835592 | tf_op jit(solution)/shard_map/ppermute | solution.py:445
  94.8 1.0 copy-start.1
  133.0 18.3 %all-to-all-start.6 = ((f32[16,30,128]{2,1,0:T(8,128)}), f32[16,30,128]{2,1,0:T(8,128)S(1)}, u32[]{:S(2)}, u32[]{:S(2)}) async-start(f32[16,30,128]{2,1,0:T(8,128)} %broadcast_in_dim.11), calls=%async_computation.6 | async-start | bytes 524288 | tf_op jit(solution)/shard_map/all_to_all | solution.py:450
  139.3 7.8 %collective-permute-start.7 = (f32[64,256]{1,0:T(8,128)S(1)}, f32[64,256]{1,0:T(8,128)S(1)}, u32[]{:S(2)}, u32[]{:S(2)}) collective-permute-start(f32[64,256]{1,0:T(8,128)S(1)} %get-tuple-element.28.refs_0_), channel_id=1, source_target_pairs={{0,3},{1,0},{2,1},{3,2},{4,7},{5,4},{6,5},{7,6},{8,11},{9,8},{10,9... | collective-permute-start | bytes 196616 | tf_op jit(solution)/shard_map/ppermute | solution.py:445
  142.1 6.5 %collective-permute-start.6 = (f32[64,256]{1,0:T(8,128)S(1)}, f32[64,256]{1,0:T(8,128)S(1)}, u32[]{:S(2)}, u32[]{:S(2)}) collective-permute-start(f32[64,256]{1,0:T(8,128)S(1)} %get-tuple-element.28.refs_0_), channel_id=1, source_target_pairs={{0,2},{1,3},{2,0},{3,1},{4,6},{5,7},{6,4},{7,5},{8,10},{9,11},{10,... | collective-permute-start | bytes 196616 | tf_op jit(solution)/shard_map/ppermute | solution.py:445
  145.2 6.2 %collective-permute-start.5 = (f32[64,256]{1,0:T(8,128)S(1)}, f32[64,256]{1,0:T(8,128)S(1)}, u32[]{:S(2)}, u32[]{:S(2)}) collective-permute-start(f32[64,256]{1,0:T(8,128)S(1)} %get-tuple-element.28.refs_0_), channel_id=1, source_target_pairs={{0,1},{1,2},{2,3},{3,0},{4,5},{5,6},{6,7},{7,4},{8,9},{9,10},{10,1... | collective-permute-start | bytes 196616 | tf_op jit(solution)/shard_map/ppermute | solution.py:445

commit v10 on v9

--- a/solution.py
+++ b/solution.py
@@ -26,8 +26,8 @@
 
 GRID = (8, 8, 2)
 BOX = ("z", "y", "k")
-YK = ("y", "k")
-ZX = ("z", "x")
+YK = ("k", "y")
+ZX = ("x", "z")
 
 TURNS = WAVENUMBER / (2.0 * math.pi)
 SCALE = TURNS / (4.0 * math.pi)
@@ -242,19 +242,19 @@
                 turned[0:SKEL, 8 * d + c : 8 * d + c + 1], (SKEL, PTS)
             )
     for g in range(nz):
-        rows = jnp.concatenate([gathered[nx * g + c, 0:32, :] for c in range(nx)], axis=0)
+        rows = jnp.concatenate([gathered[nz * c + g, 0:32, :] for c in range(nx)], axis=0)
         hi, lo = split(jnp.concatenate([rows, rotate(rows)], axis=1))
         rcat[g] = jnp.concatenate([hi, lo], axis=0)
     acc[...] = jnp.zeros_like(acc)
     per = min(4, targets)
 
     def step(g, carry):
-        sx = TURNS * gathered[nx * g, 32:33, :]
-        sy = TURNS * gathered[nx * g, 33:34, :]
-        sz = TURNS * gathered[nx * g, 34:35, :]
+        sx = TURNS * gathered[g, 32:33, :]
+        sy = TURNS * gathered[g, 33:34, :]
+        sz = TURNS * gathered[g, 34:35, :]
         source_group = g * targets + mine
         for d in range(targets):
-            delta = source_group - (first + d)
+            delta = source_group - (first + d % ny * nk + d // ny)
             w = jnp.where(delta == -1, info[8 * d + 3 : 8 * d + 4, :], 1.0)
             w = jnp.where(delta == 0, info[8 * d + 4 : 8 * d + 5, :], w)
             w = jnp.where(delta == 1, info[8 * d + 5 : 8 * d + 6, :], w)

time: 158 us -> 157 us (level)
  blocking collectives: 66 us -> 62.4 us
  starting transfers between devices: 45.6 us -> 47.8 us
    all_to_all x3, starting transfers between devices: 22.2 us -> 26 us  [trade(): return lax.all_to_all(value, axes, split_axis=0, concat_axis=0, tiled=True)]
    all_to_all x4, blocking collectives: 66 us -> 62.4 us  [trade(): return lax.all_to_all(value, axes, split_axis=0, concat_axis=0, tiled=True)]
    ppermute x6, starting transfers between devices: 17.8 us -> 16.2 us  [around(): lax.ppermute(blocks[r], 'x', [(i, (i + r) % n) for i in range(n)])]
  transfers between devices with their start and end apart: 11 -> 11, of which waited for: 7 -> 6; matrix products, arithmetic and copies ran while one was open for 0% -> 0% of each run, Pallas kernels for 6% -> 6%
where the time goes in v10:
time: 157 us; the launch traced here: 156 us
  blocking collectives  62.4 us (40%)
  starting transfers between devices  47.8 us (30%)
  Pallas kernels  22.4 us (14%)
  waiting for transfers between devices  21.4 us (14%)
    all_to_all x4, blocking collectives, trade(): return lax.all_to_all(value, axes, split_axis=0, concat_axis=0, tiled=True)  62.4 us
    all_to_all x3, starting transfers between devices, trade(): return lax.all_to_all(value, axes, split_axis=0, concat_axis=0, tiled=True)  26 us
    ppermute x6, starting transfers between devices, around(): lax.ppermute(blocks[r], 'x', [(i, (i + r) % n) for i in range(n)])  16.2 us
    ppermute x6, waiting for transfers between devices, around(): lax.ppermute(blocks[r], 'x', [(i, (i + r) % n) for i in range(n)])  12.7 us
    pallas_call x1, Pallas kernels, shards(): call(functools.partial(near_kernel, dims), (shape(32, PTS),) + (shape(PTS...  6.25 us
    pallas_call x1, Pallas kernels, shards(): call(functools.partial(far_kernel, dims), shape(targets, SKEL, 32 * nx),...  5.79 us
    all_to_all x3, waiting for transfers between devices, trade(): return lax.all_to_all(value, axes, split_axis=0, concat_axis=0, tiled=True)  5 us
    pallas_call x1, Pallas kernels, shards(): call(functools.partial(finish_kernel, nx), (shape(2, 16, points), shape(4...  4.7 us
  transfers between devices with their start and end apart: 11, of which 6 were waited for; matrix products, arithmetic and copies ran while one was open for 0% of the time, Pallas kernels for 6%

profile of v10, /device:TPU:1, one launch (start us, length us, event | category | flops | bytes accessed | tf_op | source)
XLA Modules:
  0.0 155.6 jit_solution(6875026398422876609)
XLA Ops:
  0.6 1.7 %shard_map.94 = (f32[16,8,128]{2,1,0:T(8,128)}, f32[8,128]{1,0:T(8,128)}) custom-call(s32[4,27]{1,0:T(4,128)} %near.3, s32[4]{0:T(128)} %count.3, f32[3,512]{1,0:T(4,128)} %offsets.3, s32[4,32]{1,0:T(4,128)} %skel.1), custom_call_target="tpu_custom_call" | custom-call | bytes 524288 | tf_op jit(solution)/shard_map/pallas_call | solution.py:462
  2.3 10.2 %all-to-all-start = ((f32[16,8,128]{2,1,0:T(8,128)}), f32[16,8,128]{2,1,0:T(8,128)S(1)}, u32[]{:S(2)}, u32[]{:S(2)}) async-start(f32[16,8,128]{2,1,0:T(8,128)} %get-tuple-element.16), calls=%async_computation | async-start | bytes 131072 | tf_op jit(solution)/shard_map/all_to_all | solution.py:450
  12.5 2.2 %shard_map.95 = (f32[40,512]{1,0:T(8,128)}, f32[32,40,128]{2,1,0:T(8,128)}) custom-call(f32[4,2,16,512]{3,2,1,0:T(8,128)} %cur.3, f32[1,512]{1,0:T(1,128)} %bitcast.5, f32[3,512]{1,0:T(4,128)} %offsets.3, f32[4,32,128]{2,1,0:T(8,128)} %interp.3, f32[8,128]{1,0:T(8,128)} %get-tuple-element.17.skelpos), custom_call_target="tpu_custom_call" | custom-call | bytes 524288 | tf_op jit(solution)/shard_map/pallas_call | solution.py:469
  14.7 5.0 %all-to-all-done = f32[16,8,128]{2,1,0:T(8,128)S(1)} async-done(((f32[16,8,128]{2,1,0:T(8,128)}), f32[16,8,128]{2,1,0:T(8,128)S(1)}, u32[]{:S(2)}, u32[]{:S(2)}) %all-to-all-start) | async-done | bytes 65568 | tf_op jit(solution)/shard_map/all_to_all | solution.py:450
  19.7 27.9 %all_to_all.35.gathered = f32[32,40,128]{2,1,0:T(8,128)S(1)} all-to-all(f32[32,40,128]{2,1,0:T(8,128)} %get-tuple-element.18), channel_id=1, replica_groups=mesh['z'=8,'y'=8,'k'=2,'x'=4] {'x','z'}, dimensions={0} | all-to-all | bytes 1310720 | tf_op jit(solution)/shard_map/all_to_all | solution.py:450
  47.6 5.8 %shard_map.96 = f32[16,32,128]{2,1,0:T(8,128)} custom-call(f32[128,128]{1,0:T(8,128)S(1)} %bitcast.4, f32[32,40,128]{2,1,0:T(8,128)S(1)} %all_to_all.35.gathered), custom_call_target="tpu_custom_call" | custom-call | flops 805306368 | bytes 524288 | tf_op jit(solution)/shard_map/pallas_call | solution.py:498
  53.4 0.0 copy-start.4
  53.4 0.0 copy-start
  53.4 0.0 copy-start.2
  53.4 8.3 %all-to-all-start.2 = ((f32[16,32,128]{2,1,0:T(8,128)}), f32[16,32,128]{2,1,0:T(8,128)S(1)}, u32[]{:S(2)}, u32[]{:S(2)}) async-start(f32[16,32,128]{2,1,0:T(8,128)} %shard_map.96), calls=%async_computation.2 | async-start | bytes 524288 | tf_op jit(solution)/shard_map/all_to_all | solution.py:450
  61.7 0.0 copy-start.3
  61.7 0.0 copy-done.4
  61.7 2.1 %collective-permute-start.1 = (f32[40,512]{1,0:T(8,128)S(1)}, f32[40,512]{1,0:T(8,128)S(1)}, u32[]{:S(2)}, u32[]{:S(2)}) collective-permute-start(f32[40,512]{1,0:T(8,128)S(1)} %copy-done.4), channel_id=1, source_target_pairs={{4,0},{8,4},{12,8},{16,12},{20,16},{24,20},{28,24},{32,28},{36,32}... | collective-permute-start | bytes 245768 | tf_op jit(solution)/shard_map/ppermute | solution.py:476
  63.8 3.5 %collective-permute-start = (f32[40,512]{1,0:T(8,128)S(1)}, f32[40,512]{1,0:T(8,128)S(1)}, u32[]{:S(2)}, u32[]{:S(2)}) collective-permute-start(f32[40,512]{1,0:T(8,128)S(1)} %copy-done.4), channel_id=1, source_target_pairs={{0,4},{4,8},{8,12},{12,16},{16,20},{20,24},{24,28},{28,32},{32,36}... | collective-permute-start | bytes 245768 | tf_op jit(solution)/shard_map/ppermute | solution.py:475
  67.3 3.7 %collective-permute-done.1.nxt = f32[40,512]{1,0:T(8,128)S(1)} collective-permute-done((f32[40,512]{1,0:T(8,128)S(1)}, f32[40,512]{1,0:T(8,128)S(1)}, u32[]{:S(2)}, u32[]{:S(2)}) %collective-permute-start.1) | collective-permute-done | bytes 81952 | tf_op jit(solution)/shard_map/ppermute | solution.py:476
  71.0 0.0 collective-permute-done.prev
  71.0 0.0 copy-done
  71.0 0.0 copy-done.2
  71.0 0.0 copy-done.3
  71.0 6.2 %shard_map.97 = (f32[32,128]{1,0:T(8,128)S(1)}, f32[136,512]{1,0:T(8,128)S(1)}, f32[136,512]{1,0:T(8,128)S(1)}, f32[136,512]{1,0:T(8,128)S(1)}) custom-call(s32[4,27]{1,0:T(4,128)S(1)} %copy-done.2, s32[4]{0:T(128)S(1)} %copy-done.3, f32[40,512]{1,0:T(8,128)S(1)} %collective-permute-done.prev, f32[40,512]{1,0:T(8,128)S(1)} %copy-done.4, ...), custom_call_target="tpu_custom_call" | custom-call | flops 301989888 | bytes 524288 | tf_op jit(solution)/shard_map/pallas_call | solution.py:479
  77.3 1.9 %collective-permute-start.2 = (f32[136,512]{1,0:T(8,128)S(1)}, f32[136,512]{1,0:T(8,128)S(1)}, u32[]{:S(2)}, u32[]{:S(2)}) collective-permute-start(f32[136,512]{1,0:T(8,128)S(1)} %get-tuple-element.21), channel_id=1, source_target_pairs={{0,1},{1,2},{2,3},{3,0},{4,5},{5,6},{6,7},{7,4},{8,9},{9,10},{10,1... | collective-permute-start | bytes 835592 | tf_op jit(solution)/shard_map/ppermute | solution.py:445
  79.2 3.6 %collective-permute-start.3 = (f32[136,512]{1,0:T(8,128)S(1)}, f32[136,512]{1,0:T(8,128)S(1)}, u32[]{:S(2)}, u32[]{:S(2)}) collective-permute-start(f32[136,512]{1,0:T(8,128)S(1)} %get-tuple-element.22), channel_id=1, source_target_pairs={{0,2},{1,3},{2,0},{3,1},{4,6},{5,7},{6,4},{7,5},{8,10},{9,11},{10,... | collective-permute-start | bytes 835592 | tf_op jit(solution)/shard_map/ppermute | solution.py:445
  82.8 2.9 %collective-permute-start.4 = (f32[136,512]{1,0:T(8,128)S(1)}, f32[136,512]{1,0:T(8,128)S(1)}, u32[]{:S(2)}, u32[]{:S(2)}) collective-permute-start(f32[136,512]{1,0:T(8,128)S(1)} %get-tuple-element.23), channel_id=1, source_target_pairs={{0,3},{1,0},{2,1},{3,2},{4,7},{5,4},{6,5},{7,6},{8,11},{9,8},{10,9... | collective-permute-start | bytes 835592 | tf_op jit(solution)/shard_map/ppermute | solution.py:445
  85.7 5.6 %collective-permute-done.2.refs_0_ = f32[136,512]{1,0:T(8,128)S(1)} collective-permute-done((f32[136,512]{1,0:T(8,128)S(1)}, f32[136,512]{1,0:T(8,128)S(1)}, u32[]{:S(2)}, u32[]{:S(2)}) %collective-permute-start.2) | collective-permute-done | bytes 278560 | tf_op jit(solution)/shard_map/ppermute | solution.py:445
  91.3 0.0 collective-permute-done.3.refs_1_
  91.3 2.8 %collective-permute-done.4.refs_2_ = f32[136,512]{1,0:T(8,128)S(1)} collective-permute-done((f32[136,512]{1,0:T(8,128)S(1)}, f32[136,512]{1,0:T(8,128)S(1)}, u32[]{:S(2)}, u32[]{:S(2)}) %collective-permute-start.4) | collective-permute-done | bytes 278560 | tf_op jit(solution)/shard_map/ppermute | solution.py:445
  94.1 0.0 copy-start.1
  94.1 0.9 shard_map.98
  95.1 0.0 all-to-all-done.2.phi
  95.1 0.0 copy-done.1
  95.1 0.8 shard_map.99
  95.9 16.5 %all_to_all.36 = f32[16,16,128]{2,1,0:T(8,128)S(1)} all-to-all(f32[16,16,128]{2,1,0:T(8,128)S(1)} %get-tuple-element.27), channel_id=1, replica_groups=mesh['z'=8,'y'=8,'k'=2,'x'=4] {'k','y'}, dimensions={0} | all-to-all | bytes 262144 | tf_op jit(solution)/shard_map/all_to_all | solution.py:450
  112.5 10.2 %all_to_all.37 = f32[8,16,128]{2,1,0:T(8,128)S(1)} all-to-all(f32[8,16,128]{2,1,0:T(8,128)S(1)} %broadcast_in_dim.9), channel_id=1, replica_groups=mesh['z'=8,'y'=8,'k'=2,'x'=4] {'z'}, dimensions={0} | all-to-all | bytes 131072 | tf_op jit(solution)/shard_map/all_to_all | solution.py:450
  122.7 7.8 %all_to_all.38 = f32[4,16,128]{2,1,0:T(8,128)S(1)} all-to-all(f32[4,16,128]{2,1,0:T(8,128)S(1)} %broadcast_in_dim.10), channel_id=1, replica_groups=mesh['z'=8,'y'=8,'k'=2,'x'=4] {'x'}, dimensions={0} | all-to-all | bytes 65536 | tf_op jit(solution)/shard_map/all_to_all | solution.py:450
  130.5 0.7 broadcast_in_dim.11
  131.3 7.5 %all-to-all-start.6 = ((f32[16,30,128]{2,1,0:T(8,128)}), f32[16,30,128]{2,1,0:T(8,128)S(1)}, u32[]{:S(2)}, u32[]{:S(2)}) async-start(f32[16,30,128]{2,1,0:T(8,128)} %broadcast_in_dim.11), calls=%async_computation.6 | async-start | bytes 524288 | tf_op jit(solution)/shard_map/all_to_all | solution.py:450
  138.7 2.8 %collective-permute-start.7 = (f32[64,256]{1,0:T(8,128)S(1)}, f32[64,256]{1,0:T(8,128)S(1)}, u32[]{:S(2)}, u32[]{:S(2)}) collective-permute-start(f32[64,256]{1,0:T(8,128)S(1)} %get-tuple-element.28.refs_0_), channel_id=1, source_target_pairs={{0,3},{1,0},{2,1},{3,2},{4,7},{5,4},{6,5},{7,6},{8,11},{9,8},{10,9... | collective-permute-start | bytes 196616 | tf_op jit(solution)/shard_map/ppermute | solution.py:445
  141.5 3.1 %collective-permute-start.6 = (f32[64,256]{1,0:T(8,128)S(1)}, f32[64,256]{1,0:T(8,128)S(1)}, u32[]{:S(2)}, u32[]{:S(2)}) collective-permute-start(f32[64,256]{1,0:T(8,128)S(1)} %get-tuple-element.28.refs_0_), channel_id=1, source_target_pairs={{0,2},{1,3},{2,0},{3,1},{4,6},{5,7},{6,4},{7,5},{8,10},{9,11},{10,... | collective-permute-start | bytes 196616 | tf_op jit(solution)/shard_map/ppermute | solution.py:445
  144.6 1.9 %collective-permute-start.5 = (f32[64,256]{1,0:T(8,128)S(1)}, f32[64,256]{1,0:T(8,128)S(1)}, u32[]{:S(2)}, u32[]{:S(2)}) collective-permute-start(f32[64,256]{1,0:T(8,128)S(1)} %get-tuple-element.28.refs_0_), channel_id=1, source_target_pairs={{0,1},{1,2},{2,3},{3,0},{4,5},{5,6},{6,7},{7,4},{8,9},{9,10},{10,1... | collective-permute-start | bytes 196616 | tf_op jit(solution)/shard_map/ppermute | solution.py:445
  146.6 0.0 collective-permute-done.7.refs_3_
  146.6 1.5 collective-permute-done.6.refs_2_
  148.1 2.8 %collective-permute-done.5.refs_1_ = f32[64,256]{1,0:T(8,128)S(1)} collective-permute-done((f32[64,256]{1,0:T(8,128)S(1)}, f32[64,256]{1,0:T(8,128)S(1)}, u32[]{:S(2)}, u32[]{:S(2)}) %collective-permute-start.5) | collective-permute-done | bytes 65568 | tf_op jit(solution)/shard_map/ppermute | solution.py:445
  150.9 0.0 all-to-all-done.6.summed
  150.9 4.7 %shard_map.100 = (f32[2,16,512]{2,1,0:T(8,128)}, f32[4,64,64]{2,1,0:T(8,128)}, f32[64,64]{1,0:T(8,128)}) custom-call(f32[16,30,128]{2,1,0:T(8,128)S(1)} %all-to-all-done.6.summed, f32[2,256,512]{2,1,0:T(8,128)S(1)} %get-tuple-element.24.ordered, f32[64,256]{1,0:T(8,128)S(1)} %get-tuple-element.28.refs_0_, f32[64,256]{1,0:T(8,128)S(1)} %collective-permute-done.5.refs_1_, ...), custom_call_target="tpu_custom_call" | custom-call | bytes 524288 | tf_op jit(solution)/shard_map/pallas_call | solution.py:531
  (8 shorter events, 0.1 us)
Async XLA Ops:
  2.3 17.3 %all-to-all-start = ((f32[16,8,128]{2,1,0:T(8,128)}), f32[16,8,128]{2,1,0:T(8,128)S(1)}, u32[]{:S(2)}, u32[]{:S(2)}) async-start(f32[16,8,128]{2,1,0:T(8,128)} %get-tuple-element.16), calls=%async_computation | async-start | bytes 131072 | tf_op jit(solution)/shard_map/all_to_all | solution.py:450
  53.4 8.3 %copy-start.4 = (f32[40,512]{1,0:T(8,128)S(1)}, f32[40,512]{1,0:T(8,128)}, u32[]{:S(2)}) copy-start(f32[40,512]{1,0:T(8,128)} %get-tuple-element.19.own) | copy-start | bytes 245764
  53.4 17.6 %copy-start = (f32[4,2,16,512]{3,2,1,0:T(8,128)S(1)}, f32[4,2,16,512]{3,2,1,0:T(8,128)}, u32[]{:S(2)}) copy-start(f32[4,2,16,512]{3,2,1,0:T(8,128)} %cur.3) | copy-start | bytes 786436
  53.4 17.6 %copy-start.2 = (s32[4,27]{1,0:T(4,128)S(1)}, s32[4,27]{1,0:T(4,128)}, u32[]{:S(2)}) copy-start(s32[4,27]{1,0:T(4,128)} %near.3) | copy-start | bytes 1300
  53.4 41.7 %all-to-all-start.2 = ((f32[16,32,128]{2,1,0:T(8,128)}), f32[16,32,128]{2,1,0:T(8,128)S(1)}, u32[]{:S(2)}, u32[]{:S(2)}) async-start(f32[16,32,128]{2,1,0:T(8,128)} %shard_map.96), calls=%async_computation.2 | async-start | bytes 524288 | tf_op jit(solution)/shard_map/all_to_all | solution.py:450
  61.7 9.3 %copy-start.3 = (s32[4]{0:T(128)S(1)}, s32[4]{0:T(128)}, u32[]{:S(2)}) copy-start(s32[4]{0:T(128)} %count.3) | copy-start | bytes 52
  61.7 9.3 %collective-permute-start.1 = (f32[40,512]{1,0:T(8,128)S(1)}, f32[40,512]{1,0:T(8,128)S(1)}, u32[]{:S(2)}, u32[]{:S(2)}) collective-permute-start(f32[40,512]{1,0:T(8,128)S(1)} %copy-done.4), channel_id=1, source_target_pairs={{4,0},{8,4},{12,8},{16,12},{20,16},{24,20},{28,24},{32,28},{36,32}... | collective-permute-start | bytes 245768 | tf_op jit(solution)/shard_map/ppermute | solution.py:476
  63.8 7.2 %collective-permute-start = (f32[40,512]{1,0:T(8,128)S(1)}, f32[40,512]{1,0:T(8,128)S(1)}, u32[]{:S(2)}, u32[]{:S(2)}) collective-permute-start(f32[40,512]{1,0:T(8,128)S(1)} %copy-done.4), channel_id=1, source_target_pairs={{0,4},{4,8},{8,12},{12,16},{16,20},{20,24},{24,28},{28,32},{32,36}... | collective-permute-start | bytes 245768 | tf_op jit(solution)/shard_map/ppermute | solution.py:475
  77.3 14.0 %collective-permute-start.2 = (f32[136,512]{1,0:T(8,128)S(1)}, f32[136,512]{1,0:T(8,128)S(1)}, u32[]{:S(2)}, u32[]{:S(2)}) collective-permute-start(f32[136,512]{1,0:T(8,128)S(1)} %get-tuple-element.21), channel_id=1, source_target_pairs={{0,1},{1,2},{2,3},{3,0},{4,5},{5,6},{6,7},{7,4},{8,9},{9,10},{10,1... | collective-permute-start | bytes 835592 | tf_op jit(solution)/shard_map/ppermute | solution.py:445
  79.2 12.1 %collective-permute-start.3 = (f32[136,512]{1,0:T(8,128)S(1)}, f32[136,512]{1,0:T(8,128)S(1)}, u32[]{:S(2)}, u32[]{:S(2)}) collective-permute-start(f32[136,512]{1,0:T(8,128)S(1)} %get-tuple-element.22), channel_id=1, source_target_pairs={{0,2},{1,3},{2,0},{3,1},{4,6},{5,7},{6,4},{7,5},{8,10},{9,11},{10,... | collective-permute-start | bytes 835592 | tf_op jit(solution)/shard_map/ppermute | solution.py:445
  82.8 11.3 %collective-permute-start.4 = (f32[136,512]{1,0:T(8,128)S(1)}, f32[136,512]{1,0:T(8,128)S(1)}, u32[]{:S(2)}, u32[]{:S(2)}) collective-permute-start(f32[136,512]{1,0:T(8,128)S(1)} %get-tuple-element.23), channel_id=1, source_target_pairs={{0,3},{1,0},{2,1},{3,2},{4,7},{5,4},{6,5},{7,6},{8,11},{9,8},{10,9... | collective-permute-start | bytes 835592 | tf_op jit(solution)/shard_map/ppermute | solution.py:445
  94.1 1.0 copy-start.1
  131.3 19.6 %all-to-all-start.6 = ((f32[16,30,128]{2,1,0:T(8,128)}), f32[16,30,128]{2,1,0:T(8,128)S(1)}, u32[]{:S(2)}, u32[]{:S(2)}) async-start(f32[16,30,128]{2,1,0:T(8,128)} %broadcast_in_dim.11), calls=%async_computation.6 | async-start | bytes 524288 | tf_op jit(solution)/shard_map/all_to_all | solution.py:450
  138.7 7.8 %collective-permute-start.7 = (f32[64,256]{1,0:T(8,128)S(1)}, f32[64,256]{1,0:T(8,128)S(1)}, u32[]{:S(2)}, u32[]{:S(2)}) collective-permute-start(f32[64,256]{1,0:T(8,128)S(1)} %get-tuple-element.28.refs_0_), channel_id=1, source_target_pairs={{0,3},{1,0},{2,1},{3,2},{4,7},{5,4},{6,5},{7,6},{8,11},{9,8},{10,9... | collective-permute-start | bytes 196616 | tf_op jit(solution)/shard_map/ppermute | solution.py:445
  141.5 6.5 %collective-permute-start.6 = (f32[64,256]{1,0:T(8,128)S(1)}, f32[64,256]{1,0:T(8,128)S(1)}, u32[]{:S(2)}, u32[]{:S(2)}) collective-permute-start(f32[64,256]{1,0:T(8,128)S(1)} %get-tuple-element.28.refs_0_), channel_id=1, source_target_pairs={{0,2},{1,3},{2,0},{3,1},{4,6},{5,7},{6,4},{7,5},{8,10},{9,11},{10,... | collective-permute-start | bytes 196616 | tf_op jit(solution)/shard_map/ppermute | solution.py:445
  144.6 6.2 %collective-permute-start.5 = (f32[64,256]{1,0:T(8,128)S(1)}, f32[64,256]{1,0:T(8,128)S(1)}, u32[]{:S(2)}, u32[]{:S(2)}) collective-permute-start(f32[64,256]{1,0:T(8,128)S(1)} %get-tuple-element.28.refs_0_), channel_id=1, source_target_pairs={{0,1},{1,2},{2,3},{3,0},{4,5},{5,6},{6,7},{7,4},{8,9},{9,10},{10,1... | collective-permute-start | bytes 196616 | tf_op jit(solution)/shard_map/ppermute | solution.py:445
